TPU v7x, 256 devices: a whole 4x4x8 slice. The times are simulated.
256 devices in a mesh: user: 16 (over x, y), item: 16 (over z, core).
Axes of the slice: x: 4, y: 4, z: 8, core: 2. Of those that a mesh axis runs over, the one named last changes fastest.
Arguments:
- item_factors: bfloat16 [32768, 256], P('item'), may hold values from -0.125 to 0.125
- item_gram: float32 [256, 256], replicated, as said below
- tile_users: int32 [16, 16, 48], P('user', 'item'), may hold values from 0 to 3
- tile_items: int32 [16, 16, 48], P('user', 'item'), may hold values from 0 to 15, as said below
- tile_counts: int32 [16, 16], P('user', 'item'), may hold values from 12 to 48, as said below
- tile_values: bfloat16 [16, 16, 48, 128, 128], P('user', 'item'), may hold values from 0 to 8
Outputs:
- user_factors: float32 [8192, 256], P(('user', 'item'))
- item_rhs: float32 [16, 2048, 256], P('item', 'user')
Inputs may be any that keep to these rules, and one draw needn't show every extreme that they name: `item_gram`: symmetric positive definite. The pairs (tile_users, tile_items) of one device's slots are all different. `tile_counts`: some device uses all 48 slots in every draw.
All inputs are finite; a program needn't handle non-finite values.
Results may differ from a plain program's by a relative error of at most 0.0032.
Values may be sent and summed in bfloat16 or wider, within the bound.
No kernel may reach another device: no remote copies, remote signals or barrier semaphores. Data moves between devices by JAX's collectives and lax.ppermute only.
A program may use at most 64 MiB of HBM per device.

v0:
```python
import jax
import jax.numpy as jnp
from jax import lax
from jax.experimental import pallas as pl
from jax.experimental.pallas import tpu as pltpu
from jax.sharding import Mesh, PartitionSpec as P

USER_BLK = 4
TILE = 128
RANK = 256
EPS = 1e-06
N_Z = 8
N_CORE = 2
N_ITEM = 16
N_USER = 16
OWN = 32
ROWS = 512
ITEMS = 2048
CHUNK = 256

HIGHEST = lax.Precision.HIGHEST
F32 = jnp.float32
BF16 = jnp.bfloat16
SEND = jnp.float32
RHS_SEND = jnp.bfloat16

VMEM = pl.BlockSpec(memory_space=pltpu.VMEM)
SMEM = pl.BlockSpec(memory_space=pltpu.SMEM)


def call(body, outs, specs, scratch=()):
    return pl.pallas_call(
        body,
        out_shape=outs,
        in_specs=specs,
        out_specs=[VMEM] * len(outs),
        scratch_shapes=list(scratch),
        compiler_params=pltpu.CompilerParams(vmem_limit_bytes=40 << 20),
    )


def shape(dims, dtype):
    return jax.ShapeDtypeStruct(dims, dtype)


def split_by_core(total, core, mine, other):
    for z in range(N_Z):
        mine[z] = total[pl.ds(pl.multiple_of((2 * z + core) * OWN, OWN), OWN), :]
        other[z] = total[pl.ds(pl.multiple_of((2 * z + 1 - core) * OWN, OWN), OWN), :]


def confidence_of(w):
    w = w.astype(F32)
    return jnp.where(w > 0, 1.0 + w, 0.0).astype(BF16)


def rhs_body(users, items, count, place, vals, factors, dense, conf, mine, other, total):
    dense[...] = jnp.zeros_like(dense)

    def put(s, carry):
        row = pl.multiple_of(users[s] * TILE, TILE)
        col = pl.multiple_of(items[s] * TILE, TILE)
        dense[pl.ds(row, TILE), pl.ds(col, TILE)] = vals[s]
        return carry

    lax.fori_loop(0, count[0], put, 0)
    for j in range(0, ITEMS, CHUNK):
        conf[:, j : j + CHUNK] = confidence_of(dense[:, j : j + CHUNK])
    total[...] = jnp.dot(conf[...], factors[...], preferred_element_type=F32)
    split_by_core(total, place[1], mine, other)


def scores_of(rows, factors, j):
    return lax.dot_general(
        rows, factors[j : j + CHUNK, :], (((1,), (1,)), ((), ())), preferred_element_type=F32
    )


def apply_body(place, dirs, dense, factors, mine, other, weighted, total):
    rows = dirs[...].reshape(ROWS, RANK)
    for j in range(0, ITEMS, CHUNK):
        scores = scores_of(rows, factors, j)
        weighted[:, j : j + CHUNK] = (scores * dense[:, j : j + CHUNK].astype(F32)).astype(BF16)
    total[...] = jnp.dot(weighted[...], factors[...], preferred_element_type=F32)
    split_by_core(total, place[1], mine, other)


def row_sum(value):
    return jnp.sum(value, axis=1, keepdims=True)


def arrived_sum(arrived):
    total = arrived[0].astype(F32)
    for k in range(1, N_Z):
        total = total + arrived[k].astype(F32)
    return total


def first_body(arrived, direction, sent):
    rhs = arrived_sum(arrived)
    direction[...] = rhs
    low = rhs.astype(BF16)
    for k in range(N_ITEM):
        sent[k] = low


def step_of(arrived, gram, direction, residual):
    norm = row_sum(residual * residual)
    image = jnp.dot(direction, gram, precision=HIGHEST, preferred_element_type=F32) + arrived_sum(arrived)
    step = norm / (row_sum(direction * image) + EPS)
    residual = residual - step * image
    norm_next = row_sum(residual * residual)
    direction = residual + norm_next / (norm + EPS) * direction
    return step, residual, direction, norm_next


def second_body(arrived, gram, rhs, direction, residual, step, sent):
    alpha, res, new, _ = step_of(arrived, gram[...], rhs[...], rhs[...])
    step[...] = alpha
    residual[...] = res
    direction[...] = new
    low = new.astype(BF16)
    for k in range(N_ITEM):
        sent[k] = low


def third_body(arrived, gram, rhs, dir_one, res_one, step_one, direction, partial, scalars, sent):
    first = rhs[...]
    second = dir_one[...]
    alpha, _, new, norm = step_of(arrived, gram[...], second, res_one[...])
    so_far = step_one[...] * first + alpha * second
    direction[...] = new
    partial[...] = so_far
    low = new.astype(BF16)
    rest = so_far - step_one[...] * first.astype(BF16).astype(F32) - alpha * second.astype(BF16).astype(F32)
    rest = rest.astype(BF16)
    gram_term = row_sum(
        new * jnp.dot(new, gram[...], precision=HIGHEST, preferred_element_type=F32)
    )
    scalars[0] = jnp.broadcast_to(gram_term, (OWN, TILE))
    scalars[1] = jnp.broadcast_to(norm, (OWN, TILE))
    scalars[2] = jnp.broadcast_to(step_one[...], (OWN, TILE))
    scalars[3] = jnp.broadcast_to(alpha, (OWN, TILE))
    for k in range(N_ITEM):
        sent[k, :OWN] = low
        sent[k, OWN:] = rest


def quad_body(place, dirs, dense, factors, scalars, sent, rows, column):
    for o in range(N_ITEM):
        rows[o * OWN : (o + 1) * OWN, :] = dirs[o, :OWN]
    lanes = jnp.zeros((ROWS, TILE), F32)
    for j in range(0, ITEMS, CHUNK):
        scores = scores_of(rows[...], factors, j)
        weighted = (scores * dense[:, j : j + CHUNK].astype(F32)).astype(BF16).astype(F32)
        both = weighted * scores
        lanes = lanes + both[:, :TILE] + both[:, TILE:]
    column[:ROWS, :] = jnp.broadcast_to(row_sum(lanes), (ROWS, TILE))
    mine = pl.ds(pl.multiple_of(place[0] * OWN, OWN), OWN)
    column[mine, :] = column[mine, :] + scalars[0]
    column[ROWS:, :] = jnp.zeros((3 * TILE, TILE), F32)
    spot = (place[0] % 4) * OWN
    for k in range(3):
        at = pl.ds(pl.multiple_of(ROWS + k * TILE + spot, OWN), OWN)
        column[at, :] = scalars[k + 1]
    for k in range(7):
        turned = column[k * TILE : (k + 1) * TILE, :].T
        for copy in range(N_ITEM):
            sent[copy, k : k + 1, :] = turned[:1, :]
    for copy in range(N_ITEM):
        sent[copy, 7:8, :] = jnp.zeros((1, TILE), F32)


def close_body(
    place, arrived, dirs_zero, dirs_one, dirs_two, conf, partial, direction, user_out, sent, rows, alphas
):
    summed = arrived[0]
    for o in range(1, N_ITEM):
        summed = summed + arrived[o]
    for u in range(USER_BLK):
        block = arrived[4 * u] + arrived[4 * u + 1] + arrived[4 * u + 2] + arrived[4 * u + 3]
        last = block[4:5, :] / (summed[u : u + 1, :] + EPS)
        one = jnp.broadcast_to(block[5:6, :], (TILE, TILE)).T
        two = jnp.broadcast_to(block[6:7, :], (TILE, TILE)).T
        three = jnp.broadcast_to(last, (TILE, TILE)).T
        alphas[u * TILE : (u + 1) * TILE, :] = three
        for k in range(4):
            o = 4 * u + k
            part = slice(k * OWN, (k + 1) * OWN)
            for h in range(0, RANK, TILE):
                lanes = slice(h, h + TILE)
                value = (
                    one[part] * dirs_zero[o, :, lanes].astype(F32)
                    + two[part] * dirs_one[o, :, lanes].astype(F32)
                    + dirs_two[o, OWN:, lanes].astype(F32)
                    + three[part] * dirs_two[o, :OWN, lanes].astype(F32)
                )
                rows[o * OWN : (o + 1) * OWN, lanes] = value
    mine = alphas[pl.ds(pl.multiple_of(place[0] * OWN, OWN), OWN), :]
    for h in range(0, RANK, TILE):
        user_out[:, h : h + TILE] = partial[:, h : h + TILE] + mine * direction[:, h : h + TILE]
    turned = rows[...].T.astype(BF16)
    for j in range(0, ITEMS, CHUNK):
        block = jnp.dot(turned, conf[:, j : j + CHUNK], preferred_element_type=F32)
        for h in range(0, CHUNK, TILE):
            sent[(j + h) // TILE] = block[:, h : h + TILE].astype(RHS_SEND)


def item_body(arrived, out):
    total = arrived[0].astype(F32)
    for g in range(1, N_USER):
        total = total + arrived[g].astype(F32)
    out[0] = (total * (N_USER * ROWS) ** (-0.5)).T


def exchange(value, axes):
    return lax.all_to_all(value, axes, split_axis=0, concat_axis=0, tiled=True)


def reduce_rows(mine, other):
    swapped = lax.ppermute(other, "core", [(0, 1), (1, 0)])
    return exchange((mine + swapped).astype(SEND), "z")


ITEM_AXES = ("z", "core")


def local(item_factors, item_gram, tile_users, tile_items, tile_counts, tile_values):
    core = lax.axis_index("core")
    place = jnp.stack([lax.axis_index("z") * N_CORE + core, core]).astype(jnp.int32)
    halves = [shape((N_Z, OWN, RANK), F32)] * 2
    dense, conf, mine, other = call(
        rhs_body,
        [shape((ROWS, ITEMS), BF16)] * 2 + halves,
        [SMEM] * 4 + [VMEM] * 2,
        [pltpu.VMEM((ROWS, RANK), F32)],
    )(tile_users[0, 0], tile_items[0, 0], tile_counts[0], place, tile_values[0, 0], item_factors)

    own = shape((OWN, RANK), F32)
    column = shape((OWN, 1), F32)
    spread = shape((N_ITEM, OWN, RANK), BF16)
    rhs, sent = call(first_body, [own, spread], [VMEM])(reduce_rows(mine, other))
    dirs_zero = exchange(sent, ITEM_AXES)

    def apply_tiles(dirs):
        return call(
            apply_body,
            halves,
            [SMEM] + [VMEM] * 3,
            [pltpu.VMEM((ROWS, ITEMS), BF16), pltpu.VMEM((ROWS, RANK), F32)],
        )(place, dirs, dense, item_factors)

    dir_one, res_one, step_one, sent = call(second_body, [own, own, column, spread], [VMEM] * 3)(
        reduce_rows(*apply_tiles(dirs_zero)), item_gram, rhs
    )
    dirs_one = exchange(sent, ITEM_AXES)
    dir_two, partial, scalars, sent = call(
        third_body,
        [own, own, shape((4, OWN, TILE), F32), shape((N_ITEM, 2 * OWN, RANK), BF16)],
        [VMEM] * 6,
    )(reduce_rows(*apply_tiles(dirs_one)), item_gram, rhs, dir_one, res_one, step_one)
    dirs_two = exchange(sent, ITEM_AXES)
    (sent,) = call(
        quad_body,
        [shape((N_ITEM, 8, TILE), F32)],
        [SMEM] + [VMEM] * 4,
        [pltpu.VMEM((ROWS, RANK), BF16), pltpu.VMEM((ROWS + 3 * TILE, TILE), F32)],
    )(place, dirs_two, dense, item_factors, scalars)
    user_out, sent = call(
        close_body,
        [own, shape((N_ITEM, RANK, TILE), RHS_SEND)],
        [SMEM] + [VMEM] * 7,
        [pltpu.VMEM((ROWS, RANK), F32), pltpu.VMEM((ROWS, TILE), F32)],
    )(place, exchange(sent, ITEM_AXES), dirs_zero, dirs_one, dirs_two, conf, partial, dir_two)
    (item_out,) = call(item_body, [shape((1, TILE, RANK), F32)], [VMEM])(exchange(sent, ("x", "y")))
    return user_out, item_out


def solution(mesh):
    fine = Mesh(mesh.devices.reshape(4, 4, N_Z, N_CORE), ("x", "y", "z", "core"))
    user = ("x", "y")
    return jax.shard_map(
        local,
        mesh=fine,
        in_specs=(
            P(ITEM_AXES, None),
            P(),
            P(user, ITEM_AXES, None),
            P(user, ITEM_AXES, None),
            P(user, ITEM_AXES),
            P(user, ITEM_AXES, None, None, None),
        ),
        out_specs=(P(("x", "y", "z", "core"), None), P(ITEM_AXES, user, None)),
        check_vma=False,
    )
```

profile of v0, /device:TPU:1, one launch (start us, length us, event | category | flops | bytes accessed | tf_op | source)
XLA Modules:
  0.0 155.4 jit_solution(5588756801040354863)
XLA Ops:
  1.3 0.1 pad_add_fusion.place
  1.4 0.0 copy-start
  1.4 1.2 copy-done
  2.6 0.0 copy-start.1
  2.6 1.4 copy-done.1
  4.0 0.0 copy-start.3
  4.0 0.7 copy-done.3
  4.6 0.0 copy-start.4
  4.6 0.7 copy-done.4
  5.3 1.7 %shard_map.77 = (bf16[512,2048]{1,0:T(8,128)(2,1)S(1)}, bf16[512,2048]{1,0:T(8,128)(2,1)S(1)}, f32[8,32,256]{2,1,0:T(8,128)S(1)}, f32[8,32,256]{2,1,0:T(8,128)S(1)}) custom-call(s32[48]{0:T(128)S(1)} %bitcast.8, s32[48]{0:T(128)S(1)} %bitcast.9, s32[1]{0:T(128)} %bitcast.6.count, s32[2]{0:T(128)S(1)} %pad_add_fusion.place, ...), custom_call_target="tpu_custom_call" | custom-call | tf_op jit(solution)/shard_map/pallas_call | solution.py:232
  7.0 3.5 %collective-permute-start = (f32[8,32,256]{2,1,0:T(8,128)S(1)}, f32[8,32,256]{2,1,0:T(8,128)S(1)}, u32[]{:S(2)}, u32[]{:S(2)}) collective-permute-start(f32[8,32,256]{2,1,0:T(8,128)S(1)} %get-tuple-element.23), channel_id=1, source_target_pairs={{0,1},{1,0},{2,3},{3,2},{4,5},{5,4},{6,7},{7,6},{8,9},{9,8},{10,11... | collective-permute-start | bytes 786440 | tf_op jit(solution)/shard_map/ppermute | solution.py:221
  10.4 1.2 collective-permute-done
  11.7 17.6 %all_to_all.40.arrived = f32[8,32,256]{2,1,0:T(8,128)S(1)} all-to-all(f32[8,32,256]{2,1,0:T(8,128)S(1)} %add.13), channel_id=1, replica_groups=mesh['x'=4,'y'=4,'z'=8,'core'=2] {'z'}, dimensions={0} | all-to-all | bytes 524288 | tf_op jit(solution)/shard_map/all_to_all | solution.py:217
  29.3 16.0 %all_to_all.41.dirs.dirs_zero = bf16[16,32,256]{2,1,0:T(8,128)(2,1)S(1)} all-to-all(bf16[16,32,256]{2,1,0:T(8,128)(2,1)S(1)} %get-tuple-element.24), channel_id=1, replica_groups=mesh['x'=4,'y'=4,'z'=8,'core'=2] {'z','core'}, dimensions={0} | all-to-all | bytes 524288 | tf_op jit(solution)/shard_map/all_to_all | solution.py:217
  45.3 2.0 %shard_map.79 = (f32[8,32,256]{2,1,0:T(8,128)S(1)}, f32[8,32,256]{2,1,0:T(8,128)S(1)}) custom-call(s32[2]{0:T(128)S(1)} %pad_add_fusion.place, bf16[16,32,256]{2,1,0:T(8,128)(2,1)S(1)} %all_to_all.41.dirs.dirs_zero, bf16[512,2048]{1,0:T(8,128)(2,1)S(1)} %get-tuple-element.25.dense, bf16[2048,256]{1,0:T(8,128)(2,1)S(1)} %copy-done), custom_call_target="tpu_custom_call" | custom-call | tf_op jit(solution)/shard_map/pallas_call | solution.py:246
  47.3 0.1 collective-permute-start.1
  47.4 1.5 collective-permute-done.1
  49.0 14.8 %all_to_all.42.arrived = f32[8,32,256]{2,1,0:T(8,128)S(1)} all-to-all(f32[8,32,256]{2,1,0:T(8,128)S(1)} %add.14), channel_id=1, replica_groups=mesh['x'=4,'y'=4,'z'=8,'core'=2] {'z'}, dimensions={0} | all-to-all | bytes 524288 | tf_op jit(solution)/shard_map/all_to_all | solution.py:217
  63.7 0.0 copy-done.2
  63.7 0.4 shard_map.80
  64.2 14.7 %all_to_all.43.dirs.dirs_one = bf16[16,32,256]{2,1,0:T(8,128)(2,1)S(1)} all-to-all(bf16[16,32,256]{2,1,0:T(8,128)(2,1)S(1)} %get-tuple-element.29), channel_id=1, replica_groups=mesh['x'=4,'y'=4,'z'=8,'core'=2] {'z','core'}, dimensions={0} | all-to-all | bytes 524288 | tf_op jit(solution)/shard_map/all_to_all | solution.py:217
  78.9 2.0 %shard_map.81 = (f32[8,32,256]{2,1,0:T(8,128)S(1)}, f32[8,32,256]{2,1,0:T(8,128)S(1)}) custom-call(s32[2]{0:T(128)S(1)} %pad_add_fusion.place, bf16[16,32,256]{2,1,0:T(8,128)(2,1)S(1)} %all_to_all.43.dirs.dirs_one, bf16[512,2048]{1,0:T(8,128)(2,1)S(1)} %get-tuple-element.25.dense, bf16[2048,256]{1,0:T(8,128)(2,1)S(1)} %copy-done), custom_call_target="tpu_custom_call" | custom-call | tf_op jit(solution)/shard_map/pallas_call | solution.py:246
  80.9 0.1 collective-permute-start.2
  81.0 1.5 collective-permute-done.2
  82.6 14.8 %all_to_all.44.arrived = f32[8,32,256]{2,1,0:T(8,128)S(1)} all-to-all(f32[8,32,256]{2,1,0:T(8,128)S(1)} %add.15), channel_id=1, replica_groups=mesh['x'=4,'y'=4,'z'=8,'core'=2] {'z'}, dimensions={0} | all-to-all | bytes 524288 | tf_op jit(solution)/shard_map/all_to_all | solution.py:217
  97.3 0.9 shard_map.82
  98.2 20.2 %all_to_all.45.dirs.dirs_two = bf16[16,64,256]{2,1,0:T(8,128)(2,1)S(1)} all-to-all(bf16[16,64,256]{2,1,0:T(8,128)(2,1)S(1)} %get-tuple-element.35), channel_id=1, replica_groups=mesh['x'=4,'y'=4,'z'=8,'core'=2] {'z','core'}, dimensions={0} | all-to-all | bytes 1048576 | tf_op jit(solution)/shard_map/all_to_all | solution.py:217
  118.5 1.8 %shard_map.83 = f32[16,8,128]{2,1,0:T(8,128)S(1)} custom-call(s32[2]{0:T(128)S(1)} %pad_add_fusion.place, bf16[16,64,256]{2,1,0:T(8,128)(2,1)S(1)} %all_to_all.45.dirs.dirs_two, bf16[512,2048]{1,0:T(8,128)(2,1)S(1)} %get-tuple-element.25.dense, bf16[2048,256]{1,0:T(8,128)(2,1)S(1)} %copy-done, f32[4,32,128]{2,1,0:T(8,128)S(1)} %get-tuple-element.36.scalars), custom_call_target="tpu_custom_call" | custom-call | tf_op jit(solution)/shard_map/pallas_call | solution.py:263
  120.3 10.5 %all_to_all.46.arrived = f32[16,8,128]{2,1,0:T(8,128)S(1)} all-to-all(f32[16,8,128]{2,1,0:T(8,128)S(1)} %shard_map.83), channel_id=1, replica_groups=mesh['x'=4,'y'=4,'z'=8,'core'=2] {'z','core'}, dimensions={0} | all-to-all | bytes 131072 | tf_op jit(solution)/shard_map/all_to_all | solution.py:217
  130.8 1.6 %shard_map.84 = (f32[32,256]{1,0:T(8,128)}, bf16[16,256,128]{2,1,0:T(8,128)(2,1)S(1)}) custom-call(s32[2]{0:T(128)S(1)} %pad_add_fusion.place, f32[16,8,128]{2,1,0:T(8,128)S(1)} %all_to_all.46.arrived, bf16[16,32,256]{2,1,0:T(8,128)(2,1)S(1)} %all_to_all.41.dirs.dirs_zero, bf16[16,32,256]{2,1,0:T(8,128)(2,1)S(1)} %all_to_all.43.dirs.dirs_one, ...), custom_call_target="tpu_custom_call" | custom-call | tf_op jit(solution)/shard_map/pallas_call | solution.py:269
  132.5 22.1 %all_to_all.47.arrived = bf16[16,256,128]{2,1,0:T(8,128)(2,1)S(1)} all-to-all(bf16[16,256,128]{2,1,0:T(8,128)(2,1)S(1)} %get-tuple-element.41), channel_id=1, replica_groups=mesh['x'=4,'y'=4,'z'=8,'core'=2] {'x','y'}, dimensions={0} | all-to-all | bytes 2097152 | tf_op jit(solution)/shard_map/all_to_all | solution.py:217
  154.6 0.9 shard_map.85
  (5 shorter events, 0.1 us)
Async XLA Ops:
  1.4 1.2 copy-start
  2.6 1.4 copy-start.1
  4.0 0.7 copy-start.3
  4.6 0.7 copy-start.4
  7.0 4.6 %collective-permute-start = (f32[8,32,256]{2,1,0:T(8,128)S(1)}, f32[8,32,256]{2,1,0:T(8,128)S(1)}, u32[]{:S(2)}, u32[]{:S(2)}) collective-permute-start(f32[8,32,256]{2,1,0:T(8,128)S(1)} %get-tuple-element.23), channel_id=1, source_target_pairs={{0,1},{1,0},{2,3},{3,2},{4,5},{5,4},{6,7},{7,6},{8,9},{9,8},{10,11... | collective-permute-start | bytes 786440 | tf_op jit(solution)/shard_map/ppermute | solution.py:221
  45.3 18.5 %copy-start.2 = (f32[256,256]{1,0:T(8,128)S(1)}, f32[256,256]{1,0:T(8,128)}, u32[]{:S(2)}) copy-start(f32[256,256]{1,0:T(8,128)} %gram.3) | copy-start | bytes 786436
  47.3 1.6 %collective-permute-start.1 = (f32[8,32,256]{2,1,0:T(8,128)S(1)}, f32[8,32,256]{2,1,0:T(8,128)S(1)}, u32[]{:S(2)}, u32[]{:S(2)}) collective-permute-start(f32[8,32,256]{2,1,0:T(8,128)S(1)} %get-tuple-element.27), channel_id=1, source_target_pairs={{0,1},{1,0},{2,3},{3,2},{4,5},{5,4},{6,7},{7,6},{8,9},{9,8},{10,11... | collective-permute-start | bytes 786440 | tf_op jit(solution)/shard_map/ppermute | solution.py:221
  80.9 1.6 %collective-permute-start.2 = (f32[8,32,256]{2,1,0:T(8,128)S(1)}, f32[8,32,256]{2,1,0:T(8,128)S(1)}, u32[]{:S(2)}, u32[]{:S(2)}) collective-permute-start(f32[8,32,256]{2,1,0:T(8,128)S(1)} %get-tuple-element.31), channel_id=1, source_target_pairs={{0,1},{1,0},{2,3},{3,2},{4,5},{5,4},{6,7},{7,6},{8,9},{9,8},{10,11... | collective-permute-start | bytes 786440 | tf_op jit(solution)/shard_map/ppermute | solution.py:221
where the time goes:
time: 156 us; the launch traced here: 155 us
  blocking collectives  131 us (84%)
  Pallas kernels  11.3 us (7%)
  waiting for transfers between devices  4.21 us (3%)
  local copies, waits for them, and re-layouts  3.95 us (3%)
  starting transfers between devices  3.64 us (2%)
    all_to_all x8, blocking collectives, exchange(): return lax.all_to_all(value, axes, split_axis=0, concat_axis=0, tiled=True)  131 us
    ppermute x3, waiting for transfers between devices, reduce_rows(): swapped = lax.ppermute(other, 'core', [(0, 1), (1, 0)])  4.21 us
    pallas_call x2, Pallas kernels, apply_tiles(): call(apply_body, halves, [SMEM] + [VMEM] * 3, [pltpu.VMEM((ROWS, ITEMS),...  3.99 us
    unnamed x10, local copies, waits for them, and re-layouts  3.95 us
    ppermute x3, starting transfers between devices, reduce_rows(): swapped = lax.ppermute(other, 'core', [(0, 1), (1, 0)])  3.64 us
  transfers between devices with their start and end apart: 3, of which 3 were waited for; matrix products, arithmetic and copies ran while one was open for 0% of the time, Pallas kernels for 0%

commit v1 on v0

v1 whole, which is shorter than its diff:
```python
import jax
import jax.numpy as jnp
from jax import lax
from jax.experimental import pallas as pl
from jax.experimental.pallas import tpu as pltpu
from jax.sharding import Mesh, PartitionSpec as P

USER_BLK = 4
TILE = 128
RANK = 256
EPS = 1e-06
N_Z = 8
N_CORE = 2
N_ITEM = 16
N_USER = 16
OWN = 32
ROWS = 512
HALF = 256
ITEMS = 2048
CHUNK = 256

HIGHEST = lax.Precision.HIGHEST
F32 = jnp.float32
BF16 = jnp.bfloat16
IMAGE_SEND = jnp.bfloat16
RHS_SEND = jnp.bfloat16

VMEM = pl.BlockSpec(memory_space=pltpu.VMEM)
SMEM = pl.BlockSpec(memory_space=pltpu.SMEM)
HBM = pl.BlockSpec(memory_space=pltpu.HBM)


def call(body, outs, specs, scratch=(), limit=40):
    return pl.pallas_call(
        body,
        out_shape=outs,
        in_specs=specs,
        out_specs=[VMEM] * len(outs),
        scratch_shapes=list(scratch),
        compiler_params=pltpu.CompilerParams(vmem_limit_bytes=limit << 20),
    )


def shape(dims, dtype):
    return jax.ShapeDtypeStruct(dims, dtype)


def halves_of(total, out):
    out[...] = total.reshape(N_Z, OWN, RANK)


def confidence_of(w):
    w = w.astype(F32)
    return jnp.where(w > 0, 1.0 + w, 0.0).astype(BF16)


def confidence_into(conf, dense, half):
    for j in range(0, ITEMS, CHUNK):
        conf[:, j : j + CHUNK] = confidence_of(dense[half, :, j : j + CHUNK])


def load_body(
    place, users_in, items_in, count_in, vals_in, factors_in,
    dense, factors, conf, other, users, items, count, vals, sems,
):
    copies = [
        pltpu.make_async_copy(source, target, sems.at[k])
        for k, (source, target) in enumerate(
            [(users_in, users), (items_in, items), (count_in, count), (vals_in, vals), (factors_in, factors)]
        )
    ]
    for copy in copies:
        copy.start()
    dense[...] = jnp.zeros_like(dense)
    for copy in copies[:4]:
        copy.wait()
    core = place[1]

    def put(s, carry):
        user = users[s]
        col = pl.multiple_of(items[s] * TILE, TILE)
        for q in range(4):
            half = (q + core) % 2
            row = pl.multiple_of((2 * user + q // 2) * OWN, OWN)
            dense[half, pl.ds(row, OWN), pl.ds(col, TILE)] = vals[s, q * OWN : (q + 1) * OWN, :]
        return carry

    lax.fori_loop(0, count[0], put, 0)
    confidence_into(conf, dense, 1)
    copies[4].wait()
    halves_of(jnp.dot(conf[...], factors[...], preferred_element_type=F32), other)


def own_rhs_body(dense, factors, conf, mine):
    confidence_into(conf, dense, 0)
    halves_of(jnp.dot(conf[...], factors[...], preferred_element_type=F32), mine)


def scores_of(rows, factors, j):
    return lax.dot_general(
        rows, factors[j : j + CHUNK, :], (((1,), (1,)), ((), ())), preferred_element_type=F32
    )


def weigh(dirs, dense, half, factors, weighted):
    rows = dirs[...].reshape(HALF, RANK)
    for j in range(0, ITEMS, CHUNK):
        scores = scores_of(rows, factors, j)
        weighted[:, j : j + CHUNK] = (scores * dense[half, :, j : j + CHUNK].astype(F32)).astype(BF16)


def own_scores_body(dirs, dense, factors, weighted):
    weigh(dirs, dense, 0, factors, weighted)


def other_apply_body(dirs, dense, factors, other, weighted):
    weigh(dirs, dense, 1, factors, weighted)
    halves_of(jnp.dot(weighted[...], factors[...], preferred_element_type=F32), other)


def own_sums_body(weighted, factors, mine):
    halves_of(jnp.dot(weighted[...], factors[...], preferred_element_type=F32), mine)


def row_sum(value):
    return jnp.sum(value, axis=1, keepdims=True)


def arrived_sum(arrived):
    total = arrived[0].astype(F32)
    for k in range(1, N_Z):
        total = total + arrived[k].astype(F32)
    return total


def first_body(arrived, direction, sent):
    rhs = arrived_sum(arrived)
    direction[...] = rhs
    low = rhs.astype(BF16)
    for k in range(N_Z):
        sent[k] = low


def step_of(arrived, gram, direction, residual):
    norm = row_sum(residual * residual)
    image = jnp.dot(direction, gram, precision=HIGHEST, preferred_element_type=F32) + arrived_sum(arrived)
    step = norm / (row_sum(direction * image) + EPS)
    residual = residual - step * image
    norm_next = row_sum(residual * residual)
    direction = residual + norm_next / (norm + EPS) * direction
    return step, residual, direction, norm_next


def second_body(arrived, gram, rhs, direction, residual, step, sent):
    alpha, res, new, _ = step_of(arrived, gram[...], rhs[...], rhs[...])
    step[...] = alpha
    residual[...] = res
    direction[...] = new
    low = new.astype(BF16)
    for k in range(N_Z):
        sent[k] = low


def third_body(arrived, gram, rhs, dir_one, res_one, step_one, direction, partial, scalars, sent):
    first = rhs[...]
    second = dir_one[...]
    alpha, _, new, norm = step_of(arrived, gram[...], second, res_one[...])
    so_far = step_one[...] * first + alpha * second
    direction[...] = new
    partial[...] = so_far
    low = new.astype(BF16)
    rest = so_far - step_one[...] * first.astype(BF16).astype(F32) - alpha * second.astype(BF16).astype(F32)
    rest = rest.astype(BF16)
    gram_term = row_sum(
        new * jnp.dot(new, gram[...], precision=HIGHEST, preferred_element_type=F32)
    )
    scalars[0] = jnp.broadcast_to(gram_term, (OWN, TILE))
    scalars[1] = jnp.broadcast_to(norm, (OWN, TILE))
    scalars[2] = jnp.broadcast_to(step_one[...], (OWN, TILE))
    scalars[3] = jnp.broadcast_to(alpha, (OWN, TILE))
    for k in range(N_Z):
        sent[k, :OWN] = low
        sent[k, OWN:] = rest


def quadratic(dirs, dense, half, factors, rows):
    for z in range(N_Z):
        rows[z * OWN : (z + 1) * OWN, :] = dirs[z, :OWN]
    lanes = jnp.zeros((HALF, TILE), F32)
    for j in range(0, ITEMS, CHUNK):
        scores = scores_of(rows[...], factors, j)
        weighted = (scores * dense[half, :, j : j + CHUNK].astype(F32)).astype(BF16).astype(F32)
        both = weighted * scores
        lanes = lanes + both[:, :TILE] + both[:, TILE:]
    return jnp.broadcast_to(row_sum(lanes), (HALF, TILE))


def own_quad_body(place, dirs, dense, factors, scalars, out, rows):
    out[...] = quadratic(dirs, dense, 0, factors, rows)
    mine = pl.ds(pl.multiple_of(place[0] * OWN, OWN), OWN)
    out[mine, :] = out[mine, :] + scalars[0]


def other_quad_body(place, dirs, dense, factors, scalars, own, sent, rows, column):
    core = place[1]
    column[pl.ds(pl.multiple_of(core * HALF, HALF), HALF), :] = own[...]
    column[pl.ds(pl.multiple_of((1 - core) * HALF, HALF), HALF), :] = quadratic(dirs, dense, 1, factors, rows)
    column[ROWS:, :] = jnp.zeros((3 * TILE, TILE), F32)
    spot = (place[0] % 4) * OWN
    for k in range(3):
        at = pl.ds(pl.multiple_of(ROWS + k * TILE + spot, OWN), OWN)
        column[at, :] = scalars[k + 1]
    for k in range(7):
        turned = column[k * TILE : (k + 1) * TILE, :].T
        for copy in range(N_ITEM):
            sent[copy, k : k + 1, :] = turned[:1, :]
    for copy in range(N_ITEM):
        sent[copy, 7:8, :] = jnp.zeros((1, TILE), F32)


def close_body(
    place, arrived, zero_own, zero_other, one_own, one_other, two_own, two_other,
    conf_own, conf_other, partial, direction, user_out, sent, rows, alphas,
):
    core = place[1]
    summed = arrived[0]
    for o in range(1, N_ITEM):
        summed = summed + arrived[o]
    for c in range(N_CORE):
        for part in range(2):
            block = arrived[8 * part + c]
            for z in range(4 * part + 1, 4 * part + 4):
                block = block + arrived[2 * z + c]
            row = 2 * c + part
            last = block[4:5, :] / (summed[row : row + 1, :] + EPS)
            at = slice(row * TILE, (row + 1) * TILE)
            alphas[0, at, :] = jnp.broadcast_to(block[5:6, :], (TILE, TILE)).T
            alphas[1, at, :] = jnp.broadcast_to(block[6:7, :], (TILE, TILE)).T
            alphas[2, at, :] = jnp.broadcast_to(last, (TILE, TILE)).T
    for half, (zero, one, two) in enumerate(
        [(zero_own, one_own, two_own), (zero_other, one_other, two_other)]
    ):
        base = (core + half) % 2 * HALF
        for z in range(N_Z):
            at = pl.ds(pl.multiple_of(base + z * OWN, OWN), OWN)
            for h in range(0, RANK, TILE):
                lanes = slice(h, h + TILE)
                rows[half * HALF + z * OWN : half * HALF + (z + 1) * OWN, lanes] = (
                    alphas[0, at, :] * zero[z, :, lanes].astype(F32)
                    + alphas[1, at, :] * one[z, :, lanes].astype(F32)
                    + two[z, OWN:, lanes].astype(F32)
                    + alphas[2, at, :] * two[z, :OWN, lanes].astype(F32)
                )
    mine = alphas[2, pl.ds(pl.multiple_of(core * HALF + place[0] * OWN, OWN), OWN), :]
    for h in range(0, RANK, TILE):
        user_out[:, h : h + TILE] = partial[:, h : h + TILE] + mine * direction[:, h : h + TILE]
    turned = rows[...].T.astype(BF16)
    for j in range(0, ITEMS, CHUNK):
        block = jnp.dot(
            turned[:, :HALF], conf_own[:, j : j + CHUNK], preferred_element_type=F32
        ) + jnp.dot(turned[:, HALF:], conf_other[:, j : j + CHUNK], preferred_element_type=F32)
        for h in range(0, CHUNK, TILE):
            sent[(j + h) // TILE] = block[:, h : h + TILE].astype(RHS_SEND)


def item_body(arrived, out):
    total = arrived[0].astype(F32)
    for g in range(1, N_USER):
        total = total + arrived[g].astype(F32)
    out[0] = (total * (N_USER * ROWS) ** (-0.5)).T


def exchange(value, axes):
    return lax.all_to_all(value, axes, split_axis=0, concat_axis=0, tiled=True)


def swap(value):
    return lax.ppermute(value, "core", [(0, 1), (1, 0)])


ITEM_AXES = ("z", "core")


def local(item_factors, item_gram, tile_users, tile_items, tile_counts, tile_values):
    core = lax.axis_index("core")
    place = jnp.stack([lax.axis_index("z"), core]).astype(jnp.int32)
    half = shape((N_Z, OWN, RANK), F32)
    half_conf = shape((HALF, ITEMS), BF16)
    slots = tile_users.shape[2]
    dense, factors, conf_other, other = call(
        load_body,
        [pltpu.VMEM((N_CORE, HALF, ITEMS), BF16), pltpu.VMEM((ITEMS, RANK), BF16), pltpu.VMEM((HALF, ITEMS), BF16), pltpu.VMEM((N_Z, OWN, RANK), F32)],
        [SMEM] + [HBM] * 5,
        [
            pltpu.SMEM((slots,), jnp.int32),
            pltpu.SMEM((slots,), jnp.int32),
            pltpu.SMEM((1,), jnp.int32),
            pltpu.VMEM((slots, TILE, TILE), BF16),
            pltpu.SemaphoreType.DMA((5,)),
        ],
        54,
    )(
        place,
        tile_users[0, 0],
        tile_items[0, 0],
        tile_counts[0],
        tile_values[0, 0],
        item_factors,
    )
    swapped = swap(other)
    conf_own, mine = call(own_rhs_body, [half_conf, half], [VMEM] * 2)(dense, factors)
    arrived = exchange(mine + swapped, "z")

    own = shape((OWN, RANK), F32)
    column = shape((OWN, 1), F32)
    spread = shape((N_Z, OWN, RANK), BF16)

    def apply_tiles(dirs_own, dirs_other):
        (weighted,) = call(own_scores_body, [half_conf], [VMEM] * 3)(dirs_own, dense, factors)
        weighted, dirs_other = lax.optimization_barrier((weighted, dirs_other))
        (other,) = call(
            other_apply_body, [half], [VMEM] * 3, [pltpu.VMEM((HALF, ITEMS), BF16)]
        )(dirs_other, dense, factors)
        swapped = swap(other)
        (mine,) = call(own_sums_body, [half], [VMEM] * 2)(weighted, factors)
        return exchange((mine + swapped).astype(IMAGE_SEND), "z")

    rhs, sent = call(first_body, [own, spread], [VMEM])(arrived)
    zero_own = exchange(sent, "z")
    zero_other = swap(zero_own)
    dir_one, res_one, step_one, sent = call(second_body, [own, own, column, spread], [VMEM] * 3)(
        apply_tiles(zero_own, zero_other), item_gram, rhs
    )
    one_own = exchange(sent, "z")
    one_other = swap(one_own)
    dir_two, partial, scalars, sent = call(
        third_body,
        [own, own, shape((4, OWN, TILE), F32), shape((N_Z, 2 * OWN, RANK), BF16)],
        [VMEM] * 6,
    )(apply_tiles(one_own, one_other), item_gram, rhs, dir_one, res_one, step_one)
    two_own = exchange(sent, "z")
    two_other = swap(two_own)
    rows = pltpu.VMEM((HALF, RANK), BF16)
    (quad_own,) = call(own_quad_body, [shape((HALF, TILE), F32)], [SMEM] + [VMEM] * 4, [rows])(
        place, two_own, dense, factors, scalars
    )
    (sent,) = call(
        other_quad_body,
        [shape((N_ITEM, 8, TILE), F32)],
        [SMEM] + [VMEM] * 5,
        [rows, pltpu.VMEM((ROWS + 3 * TILE, TILE), F32)],
    )(place, two_other, dense, factors, scalars, quad_own)
    user_out, sent = call(
        close_body,
        [own, shape((N_ITEM, RANK, TILE), RHS_SEND)],
        [SMEM] + [VMEM] * 11,
        [pltpu.VMEM((ROWS, RANK), F32), pltpu.VMEM((3, ROWS, TILE), F32)],
    )(
        place, exchange(sent, ITEM_AXES), zero_own, zero_other, one_own, one_other, two_own, two_other,
        conf_own, conf_other, partial, dir_two,
    )
    (item_out,) = call(item_body, [shape((1, TILE, RANK), F32)], [VMEM])(exchange(sent, ("x", "y")))
    return user_out, item_out


def solution(mesh):
    fine = Mesh(mesh.devices.reshape(4, 4, N_Z, N_CORE), ("x", "y", "z", "core"))
    user = ("x", "y")
    return jax.shard_map(
        local,
        mesh=fine,
        in_specs=(
            P(ITEM_AXES, None),
            P(),
            P(user, ITEM_AXES, None),
            P(user, ITEM_AXES, None),
            P(user, ITEM_AXES),
            P(user, ITEM_AXES, None, None, None),
        ),
        out_specs=(P(("x", "y", "z", "core"), None), P(ITEM_AXES, user, None)),
        check_vma=False,
    )
```

time: 156 us -> 137 us (0.88)
  blocking collectives: 131 us -> 105 us
  starting transfers between devices: 3.64 us -> 13.2 us
  local copies, waits for them, and re-layouts: 3.95 us -> 0.01 us
  Pallas kernels: 11.3 us -> 13.5 us
    all_to_all x8, blocking collectives: 131 us -> 105 us  [exchange(): return lax.all_to_all(value, axes, split_axis=0, concat_axis=0, tiled=True)]
    ppermute x3 -> x6, starting transfers between devices: 3.64 us -> 13.2 us  [swap(): return lax.ppermute(value, 'core', [(0, 1), (1, 0)])]
    unnamed x10 -> x4, local copies, waits for them, and re-layouts: 3.95 us -> 0.01 us
    pallas_call x6 -> x12, Pallas kernels: 8.42 us -> 10.6 us  [the longest x1 3.11 us: local(): call(load_body, [pltpu.VMEM((N_CORE, HALF, ITEMS), BF16), pltpu.VMEM((ITE...]
    ppermute x3 -> x6, waiting for transfers between devices: 4.21 us -> 3.14 us  [swap(): return lax.ppermute(value, 'core', [(0, 1), (1, 0)])]
  transfers between devices with their start and end apart: 3 -> 6, of which waited for: 3 -> 5; matrix products, arithmetic and copies ran while one was open for 0% -> 0% of each run, Pallas kernels for 0% -> 3%
where the time goes in v1:
time: 137 us
  blocking collectives  105 us (77%)
  Pallas kernels  13.5 us (10%)
  starting transfers between devices  13.2 us (10%)
  waiting for transfers between devices  3.14 us (2%)
  between operations  1.39 us (1%)
    all_to_all x8, blocking collectives, exchange(): return lax.all_to_all(value, axes, split_axis=0, concat_axis=0, tiled=True)  105 us
    ppermute x6, starting transfers between devices, swap(): return lax.ppermute(value, 'core', [(0, 1), (1, 0)])  13.2 us
    ppermute x6, waiting for transfers between devices, swap(): return lax.ppermute(value, 'core', [(0, 1), (1, 0)])  3.14 us
    pallas_call x1, Pallas kernels, local(): call(load_body, [pltpu.VMEM((N_CORE, HALF, ITEMS), BF16), pltpu.VMEM((ITE...  3.11 us
  transfers between devices with their start and end apart: 6, of which 5 were waited for; matrix products, arithmetic and copies ran while one was open for 0% of the time, Pallas kernels for 3%

profile of v1, /device:TPU:1, one launch (start us, length us, event | category | flops | bytes accessed | tf_op | source)
XLA Modules:
  0.0 137.2 jit_solution(10307436733043118069)
XLA Ops:
  1.3 0.6 pad_add_fusion.place
  1.9 3.1 %shard_map.77 = (bf16[2,256,2048]{2,1,0:T(8,128)(2,1)S(1)}, bf16[2048,256]{1,0:T(8,128)(2,1)S(1)}, bf16[256,2048]{1,0:T(8,128)(2,1)S(1)}, f32[8,32,256]{2,1,0:T(8,128)S(1)}) custom-call(s32[2]{0:T(128)} %pad_add_fusion.place, s32[48]{0:T(128)} %bitcast.8, s32[48]{0:T(128)} %bitcast.9, s32[1]{0:T(128)} %bitcast.6.count_in, bf16[48,128,128]{2,1,0:T(8,128)(2,1)} %bitcast.7, ...), custom_call_target="tpu_custom_call" | custom-call | tf_op jit(solution)/shard_map/pallas_call | solution.py:290
  5.0 3.6 %collective-permute-start = (f32[8,32,256]{2,1,0:T(8,128)S(1)}, f32[8,32,256]{2,1,0:T(8,128)S(1)}, u32[]{:S(2)}, u32[]{:S(2)}) collective-permute-start(f32[8,32,256]{2,1,0:T(8,128)S(1)} %get-tuple-element.27), channel_id=1, source_target_pairs={{0,1},{1,0},{2,3},{3,2},{4,5},{5,4},{6,7},{7,6},{8,9},{9,8},{10,11... | collective-permute-start | bytes 786440 | tf_op jit(solution)/shard_map/ppermute | solution.py:278
  8.6 0.5 shard_map.78
  9.1 0.7 collective-permute-done
  9.8 17.9 %all_to_all.40.arrived = f32[8,32,256]{2,1,0:T(8,128)S(1)} all-to-all(f32[8,32,256]{2,1,0:T(8,128)S(1)} %add.9), channel_id=1, replica_groups=mesh['x'=4,'y'=4,'z'=8,'core'=2] {'z'}, dimensions={0} | all-to-all | bytes 524288 | tf_op jit(solution)/shard_map/all_to_all | solution.py:274
  27.7 10.3 %all_to_all.41.dirs.zero_own = bf16[8,32,256]{2,1,0:T(8,128)(2,1)S(1)} all-to-all(bf16[8,32,256]{2,1,0:T(8,128)(2,1)S(1)} %get-tuple-element.28), channel_id=1, replica_groups=mesh['x'=4,'y'=4,'z'=8,'core'=2] {'z'}, dimensions={0} | all-to-all | bytes 262144 | tf_op jit(solution)/shard_map/all_to_all | solution.py:274
  38.0 2.9 %collective-permute-start.1 = (bf16[8,32,256]{2,1,0:T(8,128)(2,1)S(1)}, bf16[8,32,256]{2,1,0:T(8,128)(2,1)S(1)}, u32[]{:S(2)}, u32[]{:S(2)}) collective-permute-start(bf16[8,32,256]{2,1,0:T(8,128)(2,1)S(1)} %all_to_all.41.dirs.zero_own), channel_id=1, source_target_pairs={{0,1},{1,0},{2,3},{3,2},{4,5},{5,4},{6,7},{7,6},{8,9},{9,8},{10,11... | collective-permute-start | bytes 393224 | tf_op jit(solution)/shard_map/ppermute | solution.py:278
  40.9 0.5 shard_map.80.weighted
  41.4 0.5 collective-permute-done.1.dirs.zero_other
  41.9 0.9 shard_map.82
  42.7 0.4 collective-permute-start.2
  43.6 0.7 collective-permute-done.2
  44.4 10.8 %all_to_all.42.arrived = bf16[8,32,256]{2,1,0:T(8,128)(2,1)S(1)} all-to-all(bf16[8,32,256]{2,1,0:T(8,128)(2,1)S(1)} %add_convert_fusion.1), channel_id=1, replica_groups=mesh['x'=4,'y'=4,'z'=8,'core'=2] {'z'}, dimensions={0} | all-to-all | bytes 262144 | tf_op jit(solution)/shard_map/all_to_all | solution.py:274
  55.6 10.3 %all_to_all.43.dirs.one_own = bf16[8,32,256]{2,1,0:T(8,128)(2,1)S(1)} all-to-all(bf16[8,32,256]{2,1,0:T(8,128)(2,1)S(1)} %get-tuple-element.32), channel_id=1, replica_groups=mesh['x'=4,'y'=4,'z'=8,'core'=2] {'z'}, dimensions={0} | all-to-all | bytes 262144 | tf_op jit(solution)/shard_map/all_to_all | solution.py:274
  65.9 2.7 %collective-permute-start.3 = (bf16[8,32,256]{2,1,0:T(8,128)(2,1)S(1)}, bf16[8,32,256]{2,1,0:T(8,128)(2,1)S(1)}, u32[]{:S(2)}, u32[]{:S(2)}) collective-permute-start(bf16[8,32,256]{2,1,0:T(8,128)(2,1)S(1)} %all_to_all.43.dirs.one_own), channel_id=1, source_target_pairs={{0,1},{1,0},{2,3},{3,2},{4,5},{5,4},{6,7},{7,6},{8,9},{9,8},{10,11... | collective-permute-start | bytes 393224 | tf_op jit(solution)/shard_map/ppermute | solution.py:278
  68.7 0.5 shard_map.84.weighted
  69.2 0.5 collective-permute-done.3.dirs.one_other
  69.7 0.9 shard_map.86
  70.5 0.4 collective-permute-start.4
  71.0 0.4 shard_map.85
  71.4 0.7 collective-permute-done.4
  72.2 10.8 %all_to_all.44.arrived = bf16[8,32,256]{2,1,0:T(8,128)(2,1)S(1)} all-to-all(bf16[8,32,256]{2,1,0:T(8,128)(2,1)S(1)} %add_convert_fusion), channel_id=1, replica_groups=mesh['x'=4,'y'=4,'z'=8,'core'=2] {'z'}, dimensions={0} | all-to-all | bytes 262144 | tf_op jit(solution)/shard_map/all_to_all | solution.py:274
  83.0 0.8 shard_map.87
  83.8 12.2 %all_to_all.45.dirs.two_own = bf16[8,64,256]{2,1,0:T(8,128)(2,1)S(1)} all-to-all(bf16[8,64,256]{2,1,0:T(8,128)(2,1)S(1)} %get-tuple-element.38), channel_id=1, replica_groups=mesh['x'=4,'y'=4,'z'=8,'core'=2] {'z'}, dimensions={0} | all-to-all | bytes 524288 | tf_op jit(solution)/shard_map/all_to_all | solution.py:274
  96.0 3.0 %collective-permute-start.5 = (bf16[8,64,256]{2,1,0:T(8,128)(2,1)S(1)}, bf16[8,64,256]{2,1,0:T(8,128)(2,1)S(1)}, u32[]{:S(2)}, u32[]{:S(2)}) collective-permute-start(bf16[8,64,256]{2,1,0:T(8,128)(2,1)S(1)} %all_to_all.45.dirs.two_own), channel_id=1, source_target_pairs={{0,1},{1,0},{2,3},{3,2},{4,5},{5,4},{6,7},{7,6},{8,9},{9,8},{10,11... | collective-permute-start | bytes 786440 | tf_op jit(solution)/shard_map/ppermute | solution.py:278
  99.1 1.2 shard_map.88.own
  100.3 1.4 %shard_map.89 = f32[16,8,128]{2,1,0:T(8,128)S(1)} custom-call(s32[2]{0:T(128)S(1)} %copy-done.1, bf16[8,64,256]{2,1,0:T(8,128)(2,1)S(1)} %collective-permute-done.5.dirs.two_other, bf16[2,256,2048]{2,1,0:T(8,128)(2,1)S(1)} %get-tuple-element.24.dense, bf16[2048,256]{1,0:T(8,128)(2,1)S(1)} %get-tuple-element.25.factors, ...), custom_call_target="tpu_custom_call" | custom-call | tf_op jit(solution)/shard_map/pallas_call | solution.py:347
  101.7 10.5 %all_to_all.46.arrived = f32[16,8,128]{2,1,0:T(8,128)S(1)} all-to-all(f32[16,8,128]{2,1,0:T(8,128)S(1)} %shard_map.89), channel_id=1, replica_groups=mesh['x'=4,'y'=4,'z'=8,'core'=2] {'z','core'}, dimensions={0} | all-to-all | bytes 131072 | tf_op jit(solution)/shard_map/all_to_all | solution.py:274
  112.2 1.7 %shard_map.90 = (f32[32,256]{1,0:T(8,128)}, bf16[16,256,128]{2,1,0:T(8,128)(2,1)S(1)}) custom-call(s32[2]{0:T(128)S(1)} %copy-done.1, f32[16,8,128]{2,1,0:T(8,128)S(1)} %all_to_all.46.arrived, bf16[8,32,256]{2,1,0:T(8,128)(2,1)S(1)} %all_to_all.41.dirs.zero_own, bf16[8,32,256]{2,1,0:T(8,128)(2,1)S(1)} %collective-permute-done.1.dirs.zero_other, ...), custom_call_target="tpu_custom_call" | custom-call | tf_op jit(solution)/shard_map/pallas_call | solution.py:353
  113.9 22.3 %all_to_all.47.arrived = bf16[16,256,128]{2,1,0:T(8,128)(2,1)S(1)} all-to-all(bf16[16,256,128]{2,1,0:T(8,128)(2,1)S(1)} %get-tuple-element.45), channel_id=1, replica_groups=mesh['x'=4,'y'=4,'z'=8,'core'=2] {'x','y'}, dimensions={0} | all-to-all | bytes 2097152 | tf_op jit(solution)/shard_map/all_to_all | solution.py:274
  136.3 0.9 shard_map.91
  (11 shorter events, 1.0 us)
Async XLA Ops:
  5.0 4.8 %collective-permute-start = (f32[8,32,256]{2,1,0:T(8,128)S(1)}, f32[8,32,256]{2,1,0:T(8,128)S(1)}, u32[]{:S(2)}, u32[]{:S(2)}) collective-permute-start(f32[8,32,256]{2,1,0:T(8,128)S(1)} %get-tuple-element.27), channel_id=1, source_target_pairs={{0,1},{1,0},{2,3},{3,2},{4,5},{5,4},{6,7},{7,6},{8,9},{9,8},{10,11... | collective-permute-start | bytes 786440 | tf_op jit(solution)/shard_map/ppermute | solution.py:278
  38.0 3.9 %collective-permute-start.1 = (bf16[8,32,256]{2,1,0:T(8,128)(2,1)S(1)}, bf16[8,32,256]{2,1,0:T(8,128)(2,1)S(1)}, u32[]{:S(2)}, u32[]{:S(2)}) collective-permute-start(bf16[8,32,256]{2,1,0:T(8,128)(2,1)S(1)} %all_to_all.41.dirs.zero_own), channel_id=1, source_target_pairs={{0,1},{1,0},{2,3},{3,2},{4,5},{5,4},{6,7},{7,6},{8,9},{9,8},{10,11... | collective-permute-start | bytes 393224 | tf_op jit(solution)/shard_map/ppermute | solution.py:278
  42.7 12.5 %copy-start = (f32[256,256]{1,0:T(8,128)S(1)}, f32[256,256]{1,0:T(8,128)}, u32[]{:S(2)}) copy-start(f32[256,256]{1,0:T(8,128)} %gram.3) | copy-start | bytes 786436
  42.7 1.6 %collective-permute-start.2 = (f32[8,32,256]{2,1,0:T(8,128)S(1)}, f32[8,32,256]{2,1,0:T(8,128)S(1)}, u32[]{:S(2)}, u32[]{:S(2)}) collective-permute-start(f32[8,32,256]{2,1,0:T(8,128)S(1)} %shard_map.82), channel_id=1, source_target_pairs={{0,1},{1,0},{2,3},{3,2},{4,5},{5,4},{6,7},{7,6},{8,9},{9,8},{10,11... | collective-permute-start | bytes 786440 | tf_op jit(solution)/shard_map/ppermute | solution.py:278
  65.9 3.7 %collective-permute-start.3 = (bf16[8,32,256]{2,1,0:T(8,128)(2,1)S(1)}, bf16[8,32,256]{2,1,0:T(8,128)(2,1)S(1)}, u32[]{:S(2)}, u32[]{:S(2)}) collective-permute-start(bf16[8,32,256]{2,1,0:T(8,128)(2,1)S(1)} %all_to_all.43.dirs.one_own), channel_id=1, source_target_pairs={{0,1},{1,0},{2,3},{3,2},{4,5},{5,4},{6,7},{7,6},{8,9},{9,8},{10,11... | collective-permute-start | bytes 393224 | tf_op jit(solution)/shard_map/ppermute | solution.py:278
  70.5 28.6 %copy-start.1 = (s32[2]{0:T(128)S(1)}, s32[2]{0:T(128)}, u32[]{:S(2)}) copy-start(s32[2]{0:T(128)} %pad_add_fusion.place) | copy-start | bytes 28
  70.5 1.6 %collective-permute-start.4 = (f32[8,32,256]{2,1,0:T(8,128)S(1)}, f32[8,32,256]{2,1,0:T(8,128)S(1)}, u32[]{:S(2)}, u32[]{:S(2)}) collective-permute-start(f32[8,32,256]{2,1,0:T(8,128)S(1)} %shard_map.86), channel_id=1, source_target_pairs={{0,1},{1,0},{2,3},{3,2},{4,5},{5,4},{6,7},{7,6},{8,9},{9,8},{10,11... | collective-permute-start | bytes 786440 | tf_op jit(solution)/shard_map/ppermute | solution.py:278
  96.0 4.2 %collective-permute-start.5 = (bf16[8,64,256]{2,1,0:T(8,128)(2,1)S(1)}, bf16[8,64,256]{2,1,0:T(8,128)(2,1)S(1)}, u32[]{:S(2)}, u32[]{:S(2)}) collective-permute-start(bf16[8,64,256]{2,1,0:T(8,128)(2,1)S(1)} %all_to_all.45.dirs.two_own), channel_id=1, source_target_pairs={{0,1},{1,0},{2,3},{3,2},{4,5},{5,4},{6,7},{7,6},{8,9},{9,8},{10,11... | collective-permute-start | bytes 786440 | tf_op jit(solution)/shard_map/ppermute | solution.py:278

commit v2 on v1

--- a/solution.py
+++ b/solution.py
@@ -18,15 +18,16 @@
 HALF = 256
 ITEMS = 2048
 CHUNK = 256
+GROUP = 4
 
 HIGHEST = lax.Precision.HIGHEST
 F32 = jnp.float32
 BF16 = jnp.bfloat16
-IMAGE_SEND = jnp.bfloat16
+SUM_SEND = jnp.bfloat16
+IMAGE_SWAP = jnp.bfloat16
 RHS_SEND = jnp.bfloat16
 
 VMEM = pl.BlockSpec(memory_space=pltpu.VMEM)
-SMEM = pl.BlockSpec(memory_space=pltpu.SMEM)
 HBM = pl.BlockSpec(memory_space=pltpu.HBM)
 
 
@@ -46,7 +47,7 @@
 
 
 def halves_of(total, out):
-    out[...] = total.reshape(N_Z, OWN, RANK)
+    out[...] = total.reshape(N_Z, OWN, RANK).astype(out.dtype)
 
 
 def confidence_of(w):
@@ -60,7 +61,7 @@
 
 
 def load_body(
-    place, users_in, items_in, count_in, vals_in, factors_in,
+    users_in, items_in, count_in, vals_in, factors_in,
     dense, factors, conf, other, users, items, count, vals, sems,
 ):
     copies = [
@@ -74,7 +75,7 @@
     dense[...] = jnp.zeros_like(dense)
     for copy in copies[:4]:
         copy.wait()
-    core = place[1]
+    core = lax.axis_index("core")
 
     def put(s, carry):
         user = users[s]
@@ -85,7 +86,14 @@
             dense[half, pl.ds(row, OWN), pl.ds(col, TILE)] = vals[s, q * OWN : (q + 1) * OWN, :]
         return carry
 
-    lax.fori_loop(0, count[0], put, 0)
+    def put_group(group, carry):
+        for k in range(GROUP):
+            put(group * GROUP + k, carry)
+        return carry
+
+    groups = count[0] // GROUP
+    lax.fori_loop(0, groups, put_group, 0)
+    lax.fori_loop(groups * GROUP, count[0], put, 0)
     confidence_into(conf, dense, 1)
     copies[4].wait()
     halves_of(jnp.dot(conf[...], factors[...], preferred_element_type=F32), other)
@@ -161,68 +169,68 @@
         sent[k] = low
 
 
-def third_body(arrived, gram, rhs, dir_one, res_one, step_one, direction, partial, scalars, sent):
+def third_body(arrived, gram, rhs, dir_one, res_one, step_one, direction, partial, norm_out, step_out, sent):
     first = rhs[...]
     second = dir_one[...]
     alpha, _, new, norm = step_of(arrived, gram[...], second, res_one[...])
     so_far = step_one[...] * first + alpha * second
     direction[...] = new
     partial[...] = so_far
+    norm_out[...] = norm
+    step_out[...] = alpha
     low = new.astype(BF16)
     rest = so_far - step_one[...] * first.astype(BF16).astype(F32) - alpha * second.astype(BF16).astype(F32)
     rest = rest.astype(BF16)
-    gram_term = row_sum(
-        new * jnp.dot(new, gram[...], precision=HIGHEST, preferred_element_type=F32)
-    )
-    scalars[0] = jnp.broadcast_to(gram_term, (OWN, TILE))
-    scalars[1] = jnp.broadcast_to(norm, (OWN, TILE))
-    scalars[2] = jnp.broadcast_to(step_one[...], (OWN, TILE))
-    scalars[3] = jnp.broadcast_to(alpha, (OWN, TILE))
     for k in range(N_Z):
         sent[k, :OWN] = low
         sent[k, OWN:] = rest
 
 
-def quadratic(dirs, dense, half, factors, rows):
+def quadratic(dirs, dense, half, factors, rows, out):
     for z in range(N_Z):
         rows[z * OWN : (z + 1) * OWN, :] = dirs[z, :OWN]
     lanes = jnp.zeros((HALF, TILE), F32)
     for j in range(0, ITEMS, CHUNK):
         scores = scores_of(rows[...], factors, j)
-        weighted = (scores * dense[half, :, j : j + CHUNK].astype(F32)).astype(BF16).astype(F32)
-        both = weighted * scores
+        both = scores * dense[half, :, j : j + CHUNK].astype(F32) * scores
         lanes = lanes + both[:, :TILE] + both[:, TILE:]
-    return jnp.broadcast_to(row_sum(lanes), (HALF, TILE))
-
-
-def own_quad_body(place, dirs, dense, factors, scalars, out, rows):
-    out[...] = quadratic(dirs, dense, 0, factors, rows)
-    mine = pl.ds(pl.multiple_of(place[0] * OWN, OWN), OWN)
-    out[mine, :] = out[mine, :] + scalars[0]
-
-
-def other_quad_body(place, dirs, dense, factors, scalars, own, sent, rows, column):
-    core = place[1]
-    column[pl.ds(pl.multiple_of(core * HALF, HALF), HALF), :] = own[...]
-    column[pl.ds(pl.multiple_of((1 - core) * HALF, HALF), HALF), :] = quadratic(dirs, dense, 1, factors, rows)
-    column[ROWS:, :] = jnp.zeros((3 * TILE, TILE), F32)
-    spot = (place[0] % 4) * OWN
-    for k in range(3):
-        at = pl.ds(pl.multiple_of(ROWS + k * TILE + spot, OWN), OWN)
-        column[at, :] = scalars[k + 1]
-    for k in range(7):
-        turned = column[k * TILE : (k + 1) * TILE, :].T
-        for copy in range(N_ITEM):
-            sent[copy, k : k + 1, :] = turned[:1, :]
+    for k in range(2):
+        turned = lanes[k * TILE : (k + 1) * TILE, :].T
+        out[2 * half + k : 2 * half + k + 1, :] = jnp.sum(turned, axis=0, keepdims=True)
+
+
+def own_quad_body(
+    dirs, dense, factors, gram, direction, norm, step_one, step_two, out, rows, column
+):
+    quadratic(dirs, dense, 0, factors, rows, out)
+    out[2:4, :] = jnp.zeros((2, TILE), F32)
+    new = direction[...]
+    gram_term = row_sum(
+        new * jnp.dot(new, gram[...], precision=HIGHEST, preferred_element_type=F32)
+    )
+    spot = pl.ds(pl.multiple_of((lax.axis_index("z") % 4) * OWN, OWN), OWN)
+    for k, value in enumerate([norm[...], step_one[...], step_two[...], gram_term]):
+        column[k] = jnp.zeros((TILE, TILE), F32)
+        column[k, spot, :] = jnp.broadcast_to(value, (OWN, TILE))
+        out[4 + k : 5 + k, :] = column[k].T[:1, :]
+
+
+def other_quad_body(dirs, dense, factors, own, sent, rows, both, turned):
+    both[...] = own[...]
+    quadratic(dirs, dense, 1, factors, rows, both)
+    turned[...] = both[...]
+    turned[0:2, :] = both[2:4, :]
+    turned[2:4, :] = both[0:2, :]
+    message = jnp.where(lax.axis_index("core") == 0, both[...], turned[...])
     for copy in range(N_ITEM):
-        sent[copy, 7:8, :] = jnp.zeros((1, TILE), F32)
+        sent[copy] = message
 
 
 def close_body(
-    place, arrived, zero_own, zero_other, one_own, one_other, two_own, two_other,
-    conf_own, conf_other, partial, direction, user_out, sent, rows, alphas,
+    arrived, zero_own, zero_other, one_own, one_other, two_own, two_other,
+    conf_own, conf_other, own_step, sent, rows, alphas,
 ):
-    core = place[1]
+    core = lax.axis_index("core")
     summed = arrived[0]
     for o in range(1, N_ITEM):
         summed = summed + arrived[o]
@@ -232,7 +240,7 @@
             for z in range(4 * part + 1, 4 * part + 4):
                 block = block + arrived[2 * z + c]
             row = 2 * c + part
-            last = block[4:5, :] / (summed[row : row + 1, :] + EPS)
+            last = block[4:5, :] / (summed[row : row + 1, :] + block[7:8, :] + EPS)
             at = slice(row * TILE, (row + 1) * TILE)
             alphas[0, at, :] = jnp.broadcast_to(block[5:6, :], (TILE, TILE)).T
             alphas[1, at, :] = jnp.broadcast_to(block[6:7, :], (TILE, TILE)).T
@@ -251,9 +259,8 @@
                     + two[z, OWN:, lanes].astype(F32)
                     + alphas[2, at, :] * two[z, :OWN, lanes].astype(F32)
                 )
-    mine = alphas[2, pl.ds(pl.multiple_of(core * HALF + place[0] * OWN, OWN), OWN), :]
-    for h in range(0, RANK, TILE):
-        user_out[:, h : h + TILE] = partial[:, h : h + TILE] + mine * direction[:, h : h + TILE]
+    mine = core * HALF + lax.axis_index("z") * OWN
+    own_step[...] = alphas[2, pl.ds(pl.multiple_of(mine, OWN), OWN), :]
     turned = rows[...].T.astype(BF16)
     for j in range(0, ITEMS, CHUNK):
         block = jnp.dot(
@@ -263,7 +270,9 @@
             sent[(j + h) // TILE] = block[:, h : h + TILE].astype(RHS_SEND)
 
 
-def item_body(arrived, out):
+def item_body(arrived, partial, direction, own_step, user_out, out):
+    for h in range(0, RANK, TILE):
+        user_out[:, h : h + TILE] = partial[:, h : h + TILE] + own_step[...] * direction[:, h : h + TILE]
     total = arrived[0].astype(F32)
     for g in range(1, N_USER):
         total = total + arrived[g].astype(F32)
@@ -282,15 +291,18 @@
 
 
 def local(item_factors, item_gram, tile_users, tile_items, tile_counts, tile_values):
-    core = lax.axis_index("core")
-    place = jnp.stack([lax.axis_index("z"), core]).astype(jnp.int32)
     half = shape((N_Z, OWN, RANK), F32)
     half_conf = shape((HALF, ITEMS), BF16)
     slots = tile_users.shape[2]
     dense, factors, conf_other, other = call(
         load_body,
-        [pltpu.VMEM((N_CORE, HALF, ITEMS), BF16), pltpu.VMEM((ITEMS, RANK), BF16), pltpu.VMEM((HALF, ITEMS), BF16), pltpu.VMEM((N_Z, OWN, RANK), F32)],
-        [SMEM] + [HBM] * 5,
+        [
+            pltpu.VMEM((N_CORE, HALF, ITEMS), BF16),
+            pltpu.VMEM((ITEMS, RANK), BF16),
+            pltpu.VMEM((HALF, ITEMS), BF16),
+            pltpu.VMEM((N_Z, OWN, RANK), F32),
+        ],
+        [HBM] * 5,
         [
             pltpu.SMEM((slots,), jnp.int32),
             pltpu.SMEM((slots,), jnp.int32),
@@ -299,17 +311,10 @@
             pltpu.SemaphoreType.DMA((5,)),
         ],
         54,
-    )(
-        place,
-        tile_users[0, 0],
-        tile_items[0, 0],
-        tile_counts[0],
-        tile_values[0, 0],
-        item_factors,
-    )
+    )(tile_users[0, 0], tile_items[0, 0], tile_counts[0], tile_values[0, 0], item_factors)
     swapped = swap(other)
     conf_own, mine = call(own_rhs_body, [half_conf, half], [VMEM] * 2)(dense, factors)
-    arrived = exchange(mine + swapped, "z")
+    arrived = exchange((mine + swapped).astype(SUM_SEND), "z")
 
     own = shape((OWN, RANK), F32)
     column = shape((OWN, 1), F32)
@@ -319,11 +324,14 @@
         (weighted,) = call(own_scores_body, [half_conf], [VMEM] * 3)(dirs_own, dense, factors)
         weighted, dirs_other = lax.optimization_barrier((weighted, dirs_other))
         (other,) = call(
-            other_apply_body, [half], [VMEM] * 3, [pltpu.VMEM((HALF, ITEMS), BF16)]
+            other_apply_body,
+            [shape((N_Z, OWN, RANK), IMAGE_SWAP)],
+            [VMEM] * 3,
+            [pltpu.VMEM((HALF, ITEMS), BF16)],
         )(dirs_other, dense, factors)
         swapped = swap(other)
         (mine,) = call(own_sums_body, [half], [VMEM] * 2)(weighted, factors)
-        return exchange((mine + swapped).astype(IMAGE_SEND), "z")
+        return exchange((mine + swapped).astype(SUM_SEND), "z")
 
     rhs, sent = call(first_body, [own, spread], [VMEM])(arrived)
     zero_own = exchange(sent, "z")
@@ -333,33 +341,34 @@
     )
     one_own = exchange(sent, "z")
     one_other = swap(one_own)
-    dir_two, partial, scalars, sent = call(
+    dir_two, partial, norm, step_two, sent = call(
         third_body,
-        [own, own, shape((4, OWN, TILE), F32), shape((N_Z, 2 * OWN, RANK), BF16)],
+        [own, own, column, column, shape((N_Z, 2 * OWN, RANK), BF16)],
         [VMEM] * 6,
     )(apply_tiles(one_own, one_other), item_gram, rhs, dir_one, res_one, step_one)
     two_own = exchange(sent, "z")
     two_other = swap(two_own)
     rows = pltpu.VMEM((HALF, RANK), BF16)
-    (quad_own,) = call(own_quad_body, [shape((HALF, TILE), F32)], [SMEM] + [VMEM] * 4, [rows])(
-        place, two_own, dense, factors, scalars
-    )
+    message = pltpu.VMEM((8, TILE), F32)
+    (quad_own,) = call(
+        own_quad_body, [shape((8, TILE), F32)], [VMEM] * 8, [rows, pltpu.VMEM((4, TILE, TILE), F32)]
+    )(two_own, dense, factors, item_gram, dir_two, norm, step_one, step_two)
+    quad_own, two_other = lax.optimization_barrier((quad_own, two_other))
     (sent,) = call(
-        other_quad_body,
-        [shape((N_ITEM, 8, TILE), F32)],
-        [SMEM] + [VMEM] * 5,
-        [rows, pltpu.VMEM((ROWS + 3 * TILE, TILE), F32)],
-    )(place, two_other, dense, factors, scalars, quad_own)
-    user_out, sent = call(
+        other_quad_body, [shape((N_ITEM, 8, TILE), F32)], [VMEM] * 4, [rows, message, message]
+    )(two_other, dense, factors, quad_own)
+    own_step, sent = call(
         close_body,
-        [own, shape((N_ITEM, RANK, TILE), RHS_SEND)],
-        [SMEM] + [VMEM] * 11,
+        [shape((OWN, TILE), F32), shape((N_ITEM, RANK, TILE), RHS_SEND)],
+        [VMEM] * 9,
         [pltpu.VMEM((ROWS, RANK), F32), pltpu.VMEM((3, ROWS, TILE), F32)],
     )(
-        place, exchange(sent, ITEM_AXES), zero_own, zero_other, one_own, one_other, two_own, two_other,
-        conf_own, conf_other, partial, dir_two,
-    )
-    (item_out,) = call(item_body, [shape((1, TILE, RANK), F32)], [VMEM])(exchange(sent, ("x", "y")))
+        exchange(sent, ITEM_AXES), zero_own, zero_other, one_own, one_other, two_own, two_other,
+        conf_own, conf_other,
+    )
+    user_out, item_out = call(item_body, [own, shape((1, TILE, RANK), F32)], [VMEM] * 4)(
+        exchange(sent, ("x", "y")), partial, dir_two, own_step
+    )
     return user_out, item_out
 
 

time: 137 us -> 131 us (0.956)
  blocking collectives: 105 us -> 102 us
  Pallas kernels: 13.5 us -> 10.8 us
    all_to_all x8, blocking collectives: 105 us -> 102 us  [exchange(): return lax.all_to_all(value, axes, split_axis=0, concat_axis=0, tiled=True)]
    pallas_call x7, Pallas kernels: 7.7 us -> 5.45 us  [the longest x2 1.68 us: apply_tiles(): call(other_apply_body, [shape((N_Z, OWN, RANK), IMAGE_SWAP)], [VMEM] * 3,...]
  transfers between devices with their start and end apart: 6 -> 6, of which waited for: 5 -> 6; matrix products, arithmetic and copies ran while one was open for 0% -> 0% of each run, Pallas kernels for 3% -> 2%
where the time goes in v2:
time: 131 us; the launch traced here: 130 us
  blocking collectives  102 us (78%)
  starting transfers between devices  13.2 us (10%)
  Pallas kernels  10.8 us (8%)
  waiting for transfers between devices  3.18 us (2%)
  between operations  1.38 us (1%)
    all_to_all x8, blocking collectives, exchange(): return lax.all_to_all(value, axes, split_axis=0, concat_axis=0, tiled=True)  102 us
    ppermute x6, starting transfers between devices, swap(): return lax.ppermute(value, 'core', [(0, 1), (1, 0)])  13.2 us
    ppermute x6, waiting for transfers between devices, swap(): return lax.ppermute(value, 'core', [(0, 1), (1, 0)])  3.18 us
  transfers between devices with their start and end apart: 6, of which 6 were waited for; matrix products, arithmetic and copies ran while one was open for 0% of the time, Pallas kernels for 2%

profile of v2, /device:TPU:1, one launch (start us, length us, event | category | flops | bytes accessed | tf_op | source)
XLA Modules:
  0.0 130.5 jit_solution(5441322155515479128)
XLA Ops:
  1.3 2.6 %shard_map.77 = (bf16[2,256,2048]{2,1,0:T(8,128)(2,1)S(1)}, bf16[2048,256]{1,0:T(8,128)(2,1)S(1)}, bf16[256,2048]{1,0:T(8,128)(2,1)S(1)}, f32[8,32,256]{2,1,0:T(8,128)S(1)}) custom-call(s32[48]{0:T(128)} %bitcast.6, s32[48]{0:T(128)} %bitcast.7, s32[1]{0:T(128)} %bitcast.4.count_in, bf16[48,128,128]{2,1,0:T(8,128)(2,1)} %bitcast.5, bf16[2048,256]{1,0:T(8,128)(2,1)} %factors_in.1), custom_call_target="tpu_custom_call" | custom-call | tf_op jit(solution)/shard_map/pallas_call | solution.py:297
  3.9 3.3 %collective-permute-start = (f32[8,32,256]{2,1,0:T(8,128)S(1)}, f32[8,32,256]{2,1,0:T(8,128)S(1)}, u32[]{:S(2)}, u32[]{:S(2)}) collective-permute-start(f32[8,32,256]{2,1,0:T(8,128)S(1)} %get-tuple-element.30), channel_id=1, source_target_pairs={{0,1},{1,0},{2,3},{3,2},{4,5},{5,4},{6,7},{7,6},{8,9},{9,8},{10,11... | collective-permute-start | bytes 786440 | tf_op jit(solution)/shard_map/ppermute | solution.py:287
  7.2 0.5 shard_map.78
  7.7 0.7 collective-permute-done
  8.4 14.0 %all_to_all.40.arrived = bf16[8,32,256]{2,1,0:T(8,128)(2,1)S(1)} all-to-all(bf16[8,32,256]{2,1,0:T(8,128)(2,1)S(1)} %add_convert_fusion.2), channel_id=1, replica_groups=mesh['x'=4,'y'=4,'z'=8,'core'=2] {'z'}, dimensions={0} | all-to-all | bytes 262144 | tf_op jit(solution)/shard_map/all_to_all | solution.py:283
  22.4 10.4 %all_to_all.41.dirs.zero_own = bf16[8,32,256]{2,1,0:T(8,128)(2,1)S(1)} all-to-all(bf16[8,32,256]{2,1,0:T(8,128)(2,1)S(1)} %get-tuple-element.31), channel_id=1, replica_groups=mesh['x'=4,'y'=4,'z'=8,'core'=2] {'z'}, dimensions={0} | all-to-all | bytes 262144 | tf_op jit(solution)/shard_map/all_to_all | solution.py:283
  32.9 3.2 %collective-permute-start.1 = (bf16[8,32,256]{2,1,0:T(8,128)(2,1)S(1)}, bf16[8,32,256]{2,1,0:T(8,128)(2,1)S(1)}, u32[]{:S(2)}, u32[]{:S(2)}) collective-permute-start(bf16[8,32,256]{2,1,0:T(8,128)(2,1)S(1)} %all_to_all.41.dirs.zero_own), channel_id=1, source_target_pairs={{0,1},{1,0},{2,3},{3,2},{4,5},{5,4},{6,7},{7,6},{8,9},{9,8},{10,11... | collective-permute-start | bytes 393224 | tf_op jit(solution)/shard_map/ppermute | solution.py:287
  36.0 0.5 shard_map.80.weighted
  36.5 0.5 collective-permute-done.1.dirs.zero_other
  37.0 0.8 shard_map.82
  37.9 0.4 collective-permute-start.2
  38.3 0.4 shard_map.81
  38.8 0.5 collective-permute-done.2
  39.4 10.8 %all_to_all.42.arrived = bf16[8,32,256]{2,1,0:T(8,128)(2,1)S(1)} all-to-all(bf16[8,32,256]{2,1,0:T(8,128)(2,1)S(1)} %add_convert_fusion.1), channel_id=1, replica_groups=mesh['x'=4,'y'=4,'z'=8,'core'=2] {'z'}, dimensions={0} | all-to-all | bytes 262144 | tf_op jit(solution)/shard_map/all_to_all | solution.py:283
  50.6 10.3 %all_to_all.43.dirs.one_own = bf16[8,32,256]{2,1,0:T(8,128)(2,1)S(1)} all-to-all(bf16[8,32,256]{2,1,0:T(8,128)(2,1)S(1)} %get-tuple-element.35), channel_id=1, replica_groups=mesh['x'=4,'y'=4,'z'=8,'core'=2] {'z'}, dimensions={0} | all-to-all | bytes 262144 | tf_op jit(solution)/shard_map/all_to_all | solution.py:283
  60.9 2.7 %collective-permute-start.3 = (bf16[8,32,256]{2,1,0:T(8,128)(2,1)S(1)}, bf16[8,32,256]{2,1,0:T(8,128)(2,1)S(1)}, u32[]{:S(2)}, u32[]{:S(2)}) collective-permute-start(bf16[8,32,256]{2,1,0:T(8,128)(2,1)S(1)} %all_to_all.43.dirs.one_own), channel_id=1, source_target_pairs={{0,1},{1,0},{2,3},{3,2},{4,5},{5,4},{6,7},{7,6},{8,9},{9,8},{10,11... | collective-permute-start | bytes 393224 | tf_op jit(solution)/shard_map/ppermute | solution.py:287
  63.6 0.5 shard_map.84.weighted
  64.1 0.5 collective-permute-done.3.dirs.one_other
  64.6 0.8 shard_map.86
  65.5 0.4 collective-permute-start.4
  65.9 0.4 shard_map.85
  66.4 0.5 collective-permute-done.4
  66.9 10.8 %all_to_all.44.arrived = bf16[8,32,256]{2,1,0:T(8,128)(2,1)S(1)} all-to-all(bf16[8,32,256]{2,1,0:T(8,128)(2,1)S(1)} %add_convert_fusion), channel_id=1, replica_groups=mesh['x'=4,'y'=4,'z'=8,'core'=2] {'z'}, dimensions={0} | all-to-all | bytes 262144 | tf_op jit(solution)/shard_map/all_to_all | solution.py:283
  77.7 0.4 shard_map.87
  78.2 12.2 %all_to_all.45.dirs.two_own = bf16[8,64,256]{2,1,0:T(8,128)(2,1)S(1)} all-to-all(bf16[8,64,256]{2,1,0:T(8,128)(2,1)S(1)} %get-tuple-element.41), channel_id=1, replica_groups=mesh['x'=4,'y'=4,'z'=8,'core'=2] {'z'}, dimensions={0} | all-to-all | bytes 524288 | tf_op jit(solution)/shard_map/all_to_all | solution.py:283
  90.4 3.0 %collective-permute-start.5 = (bf16[8,64,256]{2,1,0:T(8,128)(2,1)S(1)}, bf16[8,64,256]{2,1,0:T(8,128)(2,1)S(1)}, u32[]{:S(2)}, u32[]{:S(2)}) collective-permute-start(bf16[8,64,256]{2,1,0:T(8,128)(2,1)S(1)} %all_to_all.45.dirs.two_own), channel_id=1, source_target_pairs={{0,1},{1,0},{2,3},{3,2},{4,5},{5,4},{6,7},{7,6},{8,9},{9,8},{10,11... | collective-permute-start | bytes 786440 | tf_op jit(solution)/shard_map/ppermute | solution.py:287
  93.4 0.8 shard_map.88.own
  94.6 0.6 shard_map.89
  95.1 10.6 %all_to_all.46.arrived = f32[16,8,128]{2,1,0:T(8,128)S(1)} all-to-all(f32[16,8,128]{2,1,0:T(8,128)S(1)} %shard_map.89), channel_id=1, replica_groups=mesh['x'=4,'y'=4,'z'=8,'core'=2] {'z','core'}, dimensions={0} | all-to-all | bytes 131072 | tf_op jit(solution)/shard_map/all_to_all | solution.py:283
  105.7 1.1 shard_map.90
  106.9 22.7 %all_to_all.47.arrived = bf16[16,256,128]{2,1,0:T(8,128)(2,1)S(1)} all-to-all(bf16[16,256,128]{2,1,0:T(8,128)(2,1)S(1)} %get-tuple-element.49), channel_id=1, replica_groups=mesh['x'=4,'y'=4,'z'=8,'core'=2] {'x','y'}, dimensions={0} | all-to-all | bytes 2097152 | tf_op jit(solution)/shard_map/all_to_all | solution.py:283
  129.6 0.9 shard_map.91
  (8 shorter events, 0.9 us)
Async XLA Ops:
  3.9 4.5 %collective-permute-start = (f32[8,32,256]{2,1,0:T(8,128)S(1)}, f32[8,32,256]{2,1,0:T(8,128)S(1)}, u32[]{:S(2)}, u32[]{:S(2)}) collective-permute-start(f32[8,32,256]{2,1,0:T(8,128)S(1)} %get-tuple-element.30), channel_id=1, source_target_pairs={{0,1},{1,0},{2,3},{3,2},{4,5},{5,4},{6,7},{7,6},{8,9},{9,8},{10,11... | collective-permute-start | bytes 786440 | tf_op jit(solution)/shard_map/ppermute | solution.py:287
  32.9 4.2 %collective-permute-start.1 = (bf16[8,32,256]{2,1,0:T(8,128)(2,1)S(1)}, bf16[8,32,256]{2,1,0:T(8,128)(2,1)S(1)}, u32[]{:S(2)}, u32[]{:S(2)}) collective-permute-start(bf16[8,32,256]{2,1,0:T(8,128)(2,1)S(1)} %all_to_all.41.dirs.zero_own), channel_id=1, source_target_pairs={{0,1},{1,0},{2,3},{3,2},{4,5},{5,4},{6,7},{7,6},{8,9},{9,8},{10,11... | collective-permute-start | bytes 393224 | tf_op jit(solution)/shard_map/ppermute | solution.py:287
  37.9 12.3 %copy-start = (f32[256,256]{1,0:T(8,128)S(1)}, f32[256,256]{1,0:T(8,128)}, u32[]{:S(2)}) copy-start(f32[256,256]{1,0:T(8,128)} %gram.5) | copy-start | bytes 786436
  37.9 1.4 %collective-permute-start.2 = (bf16[8,32,256]{2,1,0:T(8,128)(2,1)S(1)}, bf16[8,32,256]{2,1,0:T(8,128)(2,1)S(1)}, u32[]{:S(2)}, u32[]{:S(2)}) collective-permute-start(bf16[8,32,256]{2,1,0:T(8,128)(2,1)S(1)} %shard_map.82), channel_id=1, source_target_pairs={{0,1},{1,0},{2,3},{3,2},{4,5},{5,4},{6,7},{7,6},{8,9},{9,8},{10,11... | collective-permute-start | bytes 393224 | tf_op jit(solution)/shard_map/ppermute | solution.py:287
  60.9 3.7 %collective-permute-start.3 = (bf16[8,32,256]{2,1,0:T(8,128)(2,1)S(1)}, bf16[8,32,256]{2,1,0:T(8,128)(2,1)S(1)}, u32[]{:S(2)}, u32[]{:S(2)}) collective-permute-start(bf16[8,32,256]{2,1,0:T(8,128)(2,1)S(1)} %all_to_all.43.dirs.one_own), channel_id=1, source_target_pairs={{0,1},{1,0},{2,3},{3,2},{4,5},{5,4},{6,7},{7,6},{8,9},{9,8},{10,11... | collective-permute-start | bytes 393224 | tf_op jit(solution)/shard_map/ppermute | solution.py:287
  65.5 1.4 %collective-permute-start.4 = (bf16[8,32,256]{2,1,0:T(8,128)(2,1)S(1)}, bf16[8,32,256]{2,1,0:T(8,128)(2,1)S(1)}, u32[]{:S(2)}, u32[]{:S(2)}) collective-permute-start(bf16[8,32,256]{2,1,0:T(8,128)(2,1)S(1)} %shard_map.86), channel_id=1, source_target_pairs={{0,1},{1,0},{2,3},{3,2},{4,5},{5,4},{6,7},{7,6},{8,9},{9,8},{10,11... | collective-permute-start | bytes 393224 | tf_op jit(solution)/shard_map/ppermute | solution.py:287
  90.4 4.2 %collective-permute-start.5 = (bf16[8,64,256]{2,1,0:T(8,128)(2,1)S(1)}, bf16[8,64,256]{2,1,0:T(8,128)(2,1)S(1)}, u32[]{:S(2)}, u32[]{:S(2)}) collective-permute-start(bf16[8,64,256]{2,1,0:T(8,128)(2,1)S(1)} %all_to_all.45.dirs.two_own), channel_id=1, source_target_pairs={{0,1},{1,0},{2,3},{3,2},{4,5},{5,4},{6,7},{7,6},{8,9},{9,8},{10,11... | collective-permute-start | bytes 786440 | tf_op jit(solution)/shard_map/ppermute | solution.py:287

commit v3 on v2

--- a/solution.py
+++ b/solution.py
@@ -23,15 +23,15 @@
 HIGHEST = lax.Precision.HIGHEST
 F32 = jnp.float32
 BF16 = jnp.bfloat16
-SUM_SEND = jnp.bfloat16
-IMAGE_SWAP = jnp.bfloat16
+RHS_SUM = jnp.float32
+IMAGE_SUM = jnp.bfloat16
 RHS_SEND = jnp.bfloat16
 
 VMEM = pl.BlockSpec(memory_space=pltpu.VMEM)
 HBM = pl.BlockSpec(memory_space=pltpu.HBM)
 
 
-def call(body, outs, specs, scratch=(), limit=40):
+def call(body, outs, specs, scratch=(), limit=12):
     return pl.pallas_call(
         body,
         out_shape=outs,
@@ -55,14 +55,14 @@
     return jnp.where(w > 0, 1.0 + w, 0.0).astype(BF16)
 
 
-def confidence_into(conf, dense, half):
+def confidence_into(conf, dense):
     for j in range(0, ITEMS, CHUNK):
-        conf[:, j : j + CHUNK] = confidence_of(dense[half, :, j : j + CHUNK])
+        conf[:, j : j + CHUNK] = confidence_of(dense[:, j : j + CHUNK])
 
 
 def load_body(
     users_in, items_in, count_in, vals_in, factors_in,
-    dense, factors, conf, other, users, items, count, vals, sems,
+    near, away, factors, users, items, count, vals, sems,
 ):
     copies = [
         pltpu.make_async_copy(source, target, sems.at[k])
@@ -72,18 +72,21 @@
     ]
     for copy in copies:
         copy.start()
-    dense[...] = jnp.zeros_like(dense)
+    near[...] = jnp.zeros_like(near)
+    away[...] = jnp.zeros_like(away)
     for copy in copies[:4]:
         copy.wait()
     core = lax.axis_index("core")
+    mine = pl.multiple_of(core * OWN, OWN)
+    theirs = pl.multiple_of((1 - core) * OWN, OWN)
 
     def put(s, carry):
         user = users[s]
-        col = pl.multiple_of(items[s] * TILE, TILE)
-        for q in range(4):
-            half = (q + core) % 2
-            row = pl.multiple_of((2 * user + q // 2) * OWN, OWN)
-            dense[half, pl.ds(row, OWN), pl.ds(col, TILE)] = vals[s, q * OWN : (q + 1) * OWN, :]
+        col = pl.ds(pl.multiple_of(items[s] * TILE, TILE), TILE)
+        for p in range(2):
+            row = pl.ds(pl.multiple_of((2 * user + p) * OWN, OWN), OWN)
+            near[row, col] = vals[s, pl.ds(mine + 2 * p * OWN, OWN), :]
+            away[row, col] = vals[s, pl.ds(theirs + 2 * p * OWN, OWN), :]
         return carry
 
     def put_group(group, carry):
@@ -91,17 +94,22 @@
             put(group * GROUP + k, carry)
         return carry
 
-    groups = count[0] // GROUP
+    used = count[0, 0]
+    groups = used // GROUP
     lax.fori_loop(0, groups, put_group, 0)
-    lax.fori_loop(groups * GROUP, count[0], put, 0)
-    confidence_into(conf, dense, 1)
+    lax.fori_loop(groups * GROUP, used, put, 0)
     copies[4].wait()
-    halves_of(jnp.dot(conf[...], factors[...], preferred_element_type=F32), other)
-
-
-def own_rhs_body(dense, factors, conf, mine):
-    confidence_into(conf, dense, 0)
-    halves_of(jnp.dot(conf[...], factors[...], preferred_element_type=F32), mine)
+
+
+def near_rhs_body(near, away, factors, conf_own, conf_other, sums):
+    confidence_into(conf_own, near)
+    sums[...] = jnp.dot(conf_own[...], factors[...], preferred_element_type=F32)
+    confidence_into(conf_other, away)
+
+
+def far_rhs_body(far, distant, sums, out, conf):
+    confidence_into(conf, far)
+    halves_of(sums[...] + jnp.dot(conf[...], distant[...], preferred_element_type=F32), out)
 
 
 def scores_of(rows, factors, j):
@@ -110,24 +118,17 @@
     )
 
 
-def weigh(dirs, dense, half, factors, weighted):
+def apply_body(dirs, near, far, factors, distant, out, weighted):
     rows = dirs[...].reshape(HALF, RANK)
-    for j in range(0, ITEMS, CHUNK):
-        scores = scores_of(rows, factors, j)
-        weighted[:, j : j + CHUNK] = (scores * dense[half, :, j : j + CHUNK].astype(F32)).astype(BF16)
-
-
-def own_scores_body(dirs, dense, factors, weighted):
-    weigh(dirs, dense, 0, factors, weighted)
-
-
-def other_apply_body(dirs, dense, factors, other, weighted):
-    weigh(dirs, dense, 1, factors, weighted)
-    halves_of(jnp.dot(weighted[...], factors[...], preferred_element_type=F32), other)
-
-
-def own_sums_body(weighted, factors, mine):
-    halves_of(jnp.dot(weighted[...], factors[...], preferred_element_type=F32), mine)
+    for k, (dense, items) in enumerate([(near, factors), (far, distant)]):
+        for j in range(0, ITEMS, CHUNK):
+            product = scores_of(rows, items, j) * dense[:, j : j + CHUNK].astype(F32)
+            weighted[k, :, j : j + CHUNK] = product.astype(BF16)
+    halves_of(
+        jnp.dot(weighted[0], factors[...], preferred_element_type=F32)
+        + jnp.dot(weighted[1], distant[...], preferred_element_type=F32),
+        out,
+    )
 
 
 def row_sum(value):
@@ -186,24 +187,24 @@
         sent[k, OWN:] = rest
 
 
-def quadratic(dirs, dense, half, factors, rows, out):
+def quad_body(
+    dirs, near, far, factors, distant, gram, direction, norm, step_one, step_two,
+    sent, rows, column, first, second,
+):
     for z in range(N_Z):
         rows[z * OWN : (z + 1) * OWN, :] = dirs[z, :OWN]
     lanes = jnp.zeros((HALF, TILE), F32)
-    for j in range(0, ITEMS, CHUNK):
-        scores = scores_of(rows[...], factors, j)
-        both = scores * dense[half, :, j : j + CHUNK].astype(F32) * scores
-        lanes = lanes + both[:, :TILE] + both[:, TILE:]
+    for dense, items in [(near, factors), (far, distant)]:
+        for j in range(0, ITEMS, CHUNK):
+            scores = scores_of(rows[...], items, j)
+            both = scores * dense[:, j : j + CHUNK].astype(F32) * scores
+            lanes = lanes + both[:, :TILE] + both[:, TILE:]
+    first[...] = jnp.zeros((8, TILE), F32)
+    second[...] = jnp.zeros((8, TILE), F32)
     for k in range(2):
-        turned = lanes[k * TILE : (k + 1) * TILE, :].T
-        out[2 * half + k : 2 * half + k + 1, :] = jnp.sum(turned, axis=0, keepdims=True)
-
-
-def own_quad_body(
-    dirs, dense, factors, gram, direction, norm, step_one, step_two, out, rows, column
-):
-    quadratic(dirs, dense, 0, factors, rows, out)
-    out[2:4, :] = jnp.zeros((2, TILE), F32)
+        summed = jnp.sum(lanes[k * TILE : (k + 1) * TILE, :].T, axis=0, keepdims=True)
+        first[k : k + 1, :] = summed
+        second[2 + k : 3 + k, :] = summed
     new = direction[...]
     gram_term = row_sum(
         new * jnp.dot(new, gram[...], precision=HIGHEST, preferred_element_type=F32)
@@ -212,16 +213,10 @@
     for k, value in enumerate([norm[...], step_one[...], step_two[...], gram_term]):
         column[k] = jnp.zeros((TILE, TILE), F32)
         column[k, spot, :] = jnp.broadcast_to(value, (OWN, TILE))
-        out[4 + k : 5 + k, :] = column[k].T[:1, :]
-
-
-def other_quad_body(dirs, dense, factors, own, sent, rows, both, turned):
-    both[...] = own[...]
-    quadratic(dirs, dense, 1, factors, rows, both)
-    turned[...] = both[...]
-    turned[0:2, :] = both[2:4, :]
-    turned[2:4, :] = both[0:2, :]
-    message = jnp.where(lax.axis_index("core") == 0, both[...], turned[...])
+        row = column[k].T[:1, :]
+        first[4 + k : 5 + k, :] = row
+        second[4 + k : 5 + k, :] = row
+    message = jnp.where(lax.axis_index("core") == 0, first[...], second[...])
     for copy in range(N_ITEM):
         sent[copy] = message
 
@@ -291,72 +286,68 @@
 
 
 def local(item_factors, item_gram, tile_users, tile_items, tile_counts, tile_values):
-    half = shape((N_Z, OWN, RANK), F32)
-    half_conf = shape((HALF, ITEMS), BF16)
+    half_tiles = shape((HALF, ITEMS), BF16)
     slots = tile_users.shape[2]
-    dense, factors, conf_other, other = call(
+    distant = swap(item_factors)
+    near, away, factors = call(
         load_body,
-        [
-            pltpu.VMEM((N_CORE, HALF, ITEMS), BF16),
-            pltpu.VMEM((ITEMS, RANK), BF16),
-            pltpu.VMEM((HALF, ITEMS), BF16),
-            pltpu.VMEM((N_Z, OWN, RANK), F32),
-        ],
+        [pltpu.VMEM((HALF, ITEMS), BF16), pltpu.VMEM((HALF, ITEMS), BF16), pltpu.VMEM((ITEMS, RANK), BF16)],
         [HBM] * 5,
         [
             pltpu.SMEM((slots,), jnp.int32),
             pltpu.SMEM((slots,), jnp.int32),
-            pltpu.SMEM((1,), jnp.int32),
+            pltpu.SMEM((1, 1), jnp.int32),
             pltpu.VMEM((slots, TILE, TILE), BF16),
             pltpu.SemaphoreType.DMA((5,)),
         ],
         54,
-    )(tile_users[0, 0], tile_items[0, 0], tile_counts[0], tile_values[0, 0], item_factors)
-    swapped = swap(other)
-    conf_own, mine = call(own_rhs_body, [half_conf, half], [VMEM] * 2)(dense, factors)
-    arrived = exchange((mine + swapped).astype(SUM_SEND), "z")
+    )(tile_users[0, 0], tile_items[0, 0], tile_counts, tile_values[0, 0], item_factors)
+    far = swap(away)
+    distant, near = lax.optimization_barrier((distant, near))
+    conf_own, conf_other, sums = call(
+        near_rhs_body, [half_tiles, half_tiles, shape((HALF, RANK), F32)], [VMEM] * 3
+    )(near, away, factors)
+    sums, far = lax.optimization_barrier((sums, far))
+    (rhs_sums,) = call(
+        far_rhs_body, [shape((N_Z, OWN, RANK), RHS_SUM)], [VMEM] * 3, [pltpu.VMEM((HALF, ITEMS), BF16)]
+    )(far, distant, sums)
 
     own = shape((OWN, RANK), F32)
     column = shape((OWN, 1), F32)
     spread = shape((N_Z, OWN, RANK), BF16)
 
-    def apply_tiles(dirs_own, dirs_other):
-        (weighted,) = call(own_scores_body, [half_conf], [VMEM] * 3)(dirs_own, dense, factors)
-        weighted, dirs_other = lax.optimization_barrier((weighted, dirs_other))
-        (other,) = call(
-            other_apply_body,
-            [shape((N_Z, OWN, RANK), IMAGE_SWAP)],
-            [VMEM] * 3,
-            [pltpu.VMEM((HALF, ITEMS), BF16)],
-        )(dirs_other, dense, factors)
-        swapped = swap(other)
-        (mine,) = call(own_sums_body, [half], [VMEM] * 2)(weighted, factors)
-        return exchange((mine + swapped).astype(SUM_SEND), "z")
-
-    rhs, sent = call(first_body, [own, spread], [VMEM])(arrived)
+    def apply_tiles(dirs):
+        (image,) = call(
+            apply_body,
+            [shape((N_Z, OWN, RANK), IMAGE_SUM)],
+            [VMEM] * 5,
+            [pltpu.VMEM((N_CORE, HALF, ITEMS), BF16)],
+        )(dirs, near, far, factors, distant)
+        image, other = lax.optimization_barrier((image, swap(dirs)))
+        return exchange(image, "z"), other
+
+    rhs, sent = call(first_body, [own, spread], [VMEM])(exchange(rhs_sums, "z"))
     zero_own = exchange(sent, "z")
-    zero_other = swap(zero_own)
+    arrived, zero_other = apply_tiles(zero_own)
     dir_one, res_one, step_one, sent = call(second_body, [own, own, column, spread], [VMEM] * 3)(
-        apply_tiles(zero_own, zero_other), item_gram, rhs
+        arrived, item_gram, rhs
     )
     one_own = exchange(sent, "z")
-    one_other = swap(one_own)
+    arrived, one_other = apply_tiles(one_own)
     dir_two, partial, norm, step_two, sent = call(
         third_body,
         [own, own, column, column, shape((N_Z, 2 * OWN, RANK), BF16)],
         [VMEM] * 6,
-    )(apply_tiles(one_own, one_other), item_gram, rhs, dir_one, res_one, step_one)
+    )(arrived, item_gram, rhs, dir_one, res_one, step_one)
     two_own = exchange(sent, "z")
-    two_other = swap(two_own)
-    rows = pltpu.VMEM((HALF, RANK), BF16)
     message = pltpu.VMEM((8, TILE), F32)
-    (quad_own,) = call(
-        own_quad_body, [shape((8, TILE), F32)], [VMEM] * 8, [rows, pltpu.VMEM((4, TILE, TILE), F32)]
-    )(two_own, dense, factors, item_gram, dir_two, norm, step_one, step_two)
-    quad_own, two_other = lax.optimization_barrier((quad_own, two_other))
     (sent,) = call(
-        other_quad_body, [shape((N_ITEM, 8, TILE), F32)], [VMEM] * 4, [rows, message, message]
-    )(two_other, dense, factors, quad_own)
+        quad_body,
+        [shape((N_ITEM, 8, TILE), F32)],
+        [VMEM] * 10,
+        [pltpu.VMEM((HALF, RANK), BF16), pltpu.VMEM((4, TILE, TILE), F32), message, message],
+    )(two_own, near, far, factors, distant, item_gram, dir_two, norm, step_one, step_two)
+    sent, two_other = lax.optimization_barrier((sent, swap(two_own)))
     own_step, sent = call(
         close_body,
         [shape((OWN, TILE), F32), shape((N_ITEM, RANK, TILE), RHS_SEND)],

time: 131 us -> 133 us (1.015)
  blocking collectives: 102 us -> 110 us
  starting transfers between devices: 13.2 us -> 8.47 us
  waiting for transfers between devices: 3.18 us -> 1.59 us
    all_to_all x8, blocking collectives: 102 us -> 110 us  [exchange(): return lax.all_to_all(value, axes, split_axis=0, concat_axis=0, tiled=True)]
    ppermute x6 -> x5, starting transfers between devices: 13.2 us -> 8.47 us  [swap(): return lax.ppermute(value, 'core', [(0, 1), (1, 0)])]
    ppermute x6 -> x5, waiting for transfers between devices: 3.18 us -> 1.59 us  [swap(): return lax.ppermute(value, 'core', [(0, 1), (1, 0)])]
    pallas_call x11 -> x7, Pallas kernels: 7.91 us -> 8.4 us  [the longest x2 3.85 us: apply_tiles(): call(apply_body, [shape((N_Z, OWN, RANK), IMAGE_SUM)], [VMEM] * 5, [pltpu...]
  transfers between devices with their start and end apart: 6 -> 5, of which waited for: 6 -> 2; matrix products, arithmetic and copies ran while one was open for 0% -> 0% of each run, Pallas kernels for 2% -> 6%
where the time goes in v3:
time: 133 us
  blocking collectives  110 us (83%)
  Pallas kernels  11.2 us (8%)
  starting transfers between devices  8.47 us (6%)
  waiting for transfers between devices  1.59 us (1%)
  between operations  1.38 us (1%)
    all_to_all x8, blocking collectives, exchange(): return lax.all_to_all(value, axes, split_axis=0, concat_axis=0, tiled=True)  110 us
    ppermute x5, starting transfers between devices, swap(): return lax.ppermute(value, 'core', [(0, 1), (1, 0)])  8.47 us
    pallas_call x2, Pallas kernels, apply_tiles(): call(apply_body, [shape((N_Z, OWN, RANK), IMAGE_SUM)], [VMEM] * 5, [pltpu...  3.85 us
  transfers between devices with their start and end apart: 5, of which 2 were waited for; matrix products, arithmetic and copies ran while one was open for 0% of the time, Pallas kernels for 6%

profile of v3, /device:TPU:1, one launch (start us, length us, event | category | flops | bytes accessed | tf_op | source)
XLA Modules:
  0.0 133.1 jit_solution(4916271699774417238)
XLA Ops:
  0.6 3.3 %collective-permute-start = (bf16[2048,256]{1,0:T(8,128)(2,1)}, bf16[2048,256]{1,0:T(8,128)(2,1)S(1)}, u32[]{:S(2)}, u32[]{:S(2)}) collective-permute-start(bf16[2048,256]{1,0:T(8,128)(2,1)} %factors_in.1), channel_id=1, source_target_pairs={{0,1},{1,0},{2,3},{3,2},{4,5},{5,4},{6,7},{7,6},{8,9},{9,8},{10,11... | collective-permute-start | bytes 3145736 | tf_op jit(solution)/shard_map/ppermute | solution.py:282
  4.6 1.9 %shard_map.77 = (bf16[256,2048]{1,0:T(8,128)(2,1)S(1)}, bf16[256,2048]{1,0:T(8,128)(2,1)S(1)}, bf16[2048,256]{1,0:T(8,128)(2,1)S(1)}) custom-call(s32[48]{0:T(128)} %bitcast.4, s32[48]{0:T(128)} %bitcast.5, s32[1,1]{1,0:T(1,128)S(6)} %copy.8.count_in, bf16[48,128,128]{2,1,0:T(8,128)(2,1)} %bitcast.3, bf16[2048,256]{1,0:T(8,128)(2,1)} %factors_in.1), custom_call_target="tpu_custom_call" | custom-call | tf_op jit(solution)/shard_map/pallas_call | solution.py:292
  6.5 0.1 collective-permute-start.1
  6.6 0.0 collective-permute-done.distant
  6.6 1.1 shard_map.78
  7.7 1.5 %collective-permute-done.1.far = bf16[256,2048]{1,0:T(8,128)(2,1)S(1)} collective-permute-done((bf16[256,2048]{1,0:T(8,128)(2,1)S(1)}, bf16[256,2048]{1,0:T(8,128)(2,1)S(1)}, u32[]{:S(2)}, u32[]{:S(2)}) %collective-permute-start.1) | collective-permute-done | bytes 1048608 | tf_op jit(solution)/shard_map/ppermute | solution.py:282
  9.2 0.4 shard_map.79
  9.7 18.5 %all_to_all.40.arrived = f32[8,32,256]{2,1,0:T(8,128)S(1)} all-to-all(f32[8,32,256]{2,1,0:T(8,128)S(1)} %shard_map.79), channel_id=1, replica_groups=mesh['x'=4,'y'=4,'z'=8,'core'=2] {'z'}, dimensions={0} | all-to-all | bytes 524288 | tf_op jit(solution)/shard_map/all_to_all | solution.py:278
  28.2 10.3 %all_to_all.41.dirs.zero_own = bf16[8,32,256]{2,1,0:T(8,128)(2,1)S(1)} all-to-all(bf16[8,32,256]{2,1,0:T(8,128)(2,1)S(1)} %get-tuple-element.39), channel_id=1, replica_groups=mesh['x'=4,'y'=4,'z'=8,'core'=2] {'z'}, dimensions={0} | all-to-all | bytes 262144 | tf_op jit(solution)/shard_map/all_to_all | solution.py:278
  38.5 0.0 copy-start
  38.5 2.1 %collective-permute-start.2 = (bf16[8,32,256]{2,1,0:T(8,128)(2,1)S(1)}, bf16[8,32,256]{2,1,0:T(8,128)(2,1)S(1)}, u32[]{:S(2)}, u32[]{:S(2)}) collective-permute-start(bf16[8,32,256]{2,1,0:T(8,128)(2,1)S(1)} %all_to_all.41.dirs.zero_own), channel_id=1, source_target_pairs={{0,1},{1,0},{2,3},{3,2},{4,5},{5,4},{6,7},{7,6},{8,9},{9,8},{10,11... | collective-permute-start | bytes 393224 | tf_op jit(solution)/shard_map/ppermute | solution.py:282
  40.6 1.9 %shard_map.81 = bf16[8,32,256]{2,1,0:T(8,128)(2,1)S(1)} custom-call(bf16[8,32,256]{2,1,0:T(8,128)(2,1)S(1)} %all_to_all.41.dirs.zero_own, bf16[256,2048]{1,0:T(8,128)(2,1)S(1)} %get-tuple-element.32.near, bf16[256,2048]{1,0:T(8,128)(2,1)S(1)} %collective-permute-done.1.far, bf16[2048,256]{1,0:T(8,128)(2,1)S(1)} %get-tuple-element.34.factors, ...), custom_call_target="tpu_custom_call" | custom-call | tf_op jit(solution)/shard_map/pallas_call | solution.py:320
  42.5 0.0 collective-permute-done.2.zero_other
  42.5 11.9 %all_to_all.42.arrived = bf16[8,32,256]{2,1,0:T(8,128)(2,1)S(1)} all-to-all(bf16[8,32,256]{2,1,0:T(8,128)(2,1)S(1)} %shard_map.81), channel_id=1, replica_groups=mesh['x'=4,'y'=4,'z'=8,'core'=2] {'z'}, dimensions={0} | all-to-all | bytes 262144 | tf_op jit(solution)/shard_map/all_to_all | solution.py:278
  54.4 0.0 copy-done
  54.4 0.4 shard_map.82
  54.8 10.5 %all_to_all.43.dirs.one_own = bf16[8,32,256]{2,1,0:T(8,128)(2,1)S(1)} all-to-all(bf16[8,32,256]{2,1,0:T(8,128)(2,1)S(1)} %get-tuple-element.42), channel_id=1, replica_groups=mesh['x'=4,'y'=4,'z'=8,'core'=2] {'z'}, dimensions={0} | all-to-all | bytes 262144 | tf_op jit(solution)/shard_map/all_to_all | solution.py:278
  65.3 1.9 %collective-permute-start.3 = (bf16[8,32,256]{2,1,0:T(8,128)(2,1)S(1)}, bf16[8,32,256]{2,1,0:T(8,128)(2,1)S(1)}, u32[]{:S(2)}, u32[]{:S(2)}) collective-permute-start(bf16[8,32,256]{2,1,0:T(8,128)(2,1)S(1)} %all_to_all.43.dirs.one_own), channel_id=1, source_target_pairs={{0,1},{1,0},{2,3},{3,2},{4,5},{5,4},{6,7},{7,6},{8,9},{9,8},{10,11... | collective-permute-start | bytes 393224 | tf_op jit(solution)/shard_map/ppermute | solution.py:282
  67.2 1.9 %shard_map.83 = bf16[8,32,256]{2,1,0:T(8,128)(2,1)S(1)} custom-call(bf16[8,32,256]{2,1,0:T(8,128)(2,1)S(1)} %all_to_all.43.dirs.one_own, bf16[256,2048]{1,0:T(8,128)(2,1)S(1)} %get-tuple-element.32.near, bf16[256,2048]{1,0:T(8,128)(2,1)S(1)} %collective-permute-done.1.far, bf16[2048,256]{1,0:T(8,128)(2,1)S(1)} %get-tuple-element.34.factors, ...), custom_call_target="tpu_custom_call" | custom-call | tf_op jit(solution)/shard_map/pallas_call | solution.py:320
  69.1 0.0 collective-permute-done.3.one_other
  69.1 11.9 %all_to_all.44.arrived = bf16[8,32,256]{2,1,0:T(8,128)(2,1)S(1)} all-to-all(bf16[8,32,256]{2,1,0:T(8,128)(2,1)S(1)} %shard_map.83), channel_id=1, replica_groups=mesh['x'=4,'y'=4,'z'=8,'core'=2] {'z'}, dimensions={0} | all-to-all | bytes 262144 | tf_op jit(solution)/shard_map/all_to_all | solution.py:278
  81.0 0.4 shard_map.84
  81.5 14.2 %all_to_all.45.dirs.two_own = bf16[8,64,256]{2,1,0:T(8,128)(2,1)S(1)} all-to-all(bf16[8,64,256]{2,1,0:T(8,128)(2,1)S(1)} %get-tuple-element.47), channel_id=1, replica_groups=mesh['x'=4,'y'=4,'z'=8,'core'=2] {'z'}, dimensions={0} | all-to-all | bytes 524288 | tf_op jit(solution)/shard_map/all_to_all | solution.py:278
  95.7 1.0 collective-permute-start.4
  96.7 1.1 shard_map.85
  97.8 0.1 collective-permute-done.4.two_other
  97.9 10.6 %all_to_all.46.arrived = f32[16,8,128]{2,1,0:T(8,128)S(1)} all-to-all(f32[16,8,128]{2,1,0:T(8,128)S(1)} %shard_map.85), channel_id=1, replica_groups=mesh['x'=4,'y'=4,'z'=8,'core'=2] {'z','core'}, dimensions={0} | all-to-all | bytes 131072 | tf_op jit(solution)/shard_map/all_to_all | solution.py:278
  108.5 1.1 shard_map.86
  109.6 22.6 %all_to_all.47.arrived = bf16[16,256,128]{2,1,0:T(8,128)(2,1)S(1)} all-to-all(bf16[16,256,128]{2,1,0:T(8,128)(2,1)S(1)} %get-tuple-element.57), channel_id=1, replica_groups=mesh['x'=4,'y'=4,'z'=8,'core'=2] {'x','y'}, dimensions={0} | all-to-all | bytes 2097152 | tf_op jit(solution)/shard_map/all_to_all | solution.py:278
  132.2 0.9 shard_map.87
  (1 shorter events, 0.0 us)
Async XLA Ops:
  0.6 6.0 %collective-permute-start = (bf16[2048,256]{1,0:T(8,128)(2,1)}, bf16[2048,256]{1,0:T(8,128)(2,1)S(1)}, u32[]{:S(2)}, u32[]{:S(2)}) collective-permute-start(bf16[2048,256]{1,0:T(8,128)(2,1)} %factors_in.1), channel_id=1, source_target_pairs={{0,1},{1,0},{2,3},{3,2},{4,5},{5,4},{6,7},{7,6},{8,9},{9,8},{10,11... | collective-permute-start | bytes 3145736 | tf_op jit(solution)/shard_map/ppermute | solution.py:282
  6.5 2.7 %collective-permute-start.1 = (bf16[256,2048]{1,0:T(8,128)(2,1)S(1)}, bf16[256,2048]{1,0:T(8,128)(2,1)S(1)}, u32[]{:S(2)}, u32[]{:S(2)}) collective-permute-start(bf16[256,2048]{1,0:T(8,128)(2,1)S(1)} %get-tuple-element.33.away), channel_id=1, source_target_pairs={{0,1},{1,0},{2,3},{3,2},{4,5},{5,4},{6,7},{7,6},{8,9},{9,8},{10,11... | collective-permute-start | bytes 3145736 | tf_op jit(solution)/shard_map/ppermute | solution.py:282
  38.5 15.9 %copy-start = (f32[256,256]{1,0:T(8,128)S(1)}, f32[256,256]{1,0:T(8,128)}, u32[]{:S(2)}) copy-start(f32[256,256]{1,0:T(8,128)} %gram.5) | copy-start | bytes 786436
  38.5 4.0 %collective-permute-start.2 = (bf16[8,32,256]{2,1,0:T(8,128)(2,1)S(1)}, bf16[8,32,256]{2,1,0:T(8,128)(2,1)S(1)}, u32[]{:S(2)}, u32[]{:S(2)}) collective-permute-start(bf16[8,32,256]{2,1,0:T(8,128)(2,1)S(1)} %all_to_all.41.dirs.zero_own), channel_id=1, source_target_pairs={{0,1},{1,0},{2,3},{3,2},{4,5},{5,4},{6,7},{7,6},{8,9},{9,8},{10,11... | collective-permute-start | bytes 393224 | tf_op jit(solution)/shard_map/ppermute | solution.py:282
  65.3 3.9 %collective-permute-start.3 = (bf16[8,32,256]{2,1,0:T(8,128)(2,1)S(1)}, bf16[8,32,256]{2,1,0:T(8,128)(2,1)S(1)}, u32[]{:S(2)}, u32[]{:S(2)}) collective-permute-start(bf16[8,32,256]{2,1,0:T(8,128)(2,1)S(1)} %all_to_all.43.dirs.one_own), channel_id=1, source_target_pairs={{0,1},{1,0},{2,3},{3,2},{4,5},{5,4},{6,7},{7,6},{8,9},{9,8},{10,11... | collective-permute-start | bytes 393224 | tf_op jit(solution)/shard_map/ppermute | solution.py:282
  95.7 2.2 %collective-permute-start.4 = (bf16[8,64,256]{2,1,0:T(8,128)(2,1)S(1)}, bf16[8,64,256]{2,1,0:T(8,128)(2,1)S(1)}, u32[]{:S(2)}, u32[]{:S(2)}) collective-permute-start(bf16[8,64,256]{2,1,0:T(8,128)(2,1)S(1)} %all_to_all.45.dirs.two_own), channel_id=1, source_target_pairs={{0,1},{1,0},{2,3},{3,2},{4,5},{5,4},{6,7},{7,6},{8,9},{9,8},{10,11... | collective-permute-start | bytes 786440 | tf_op jit(solution)/shard_map/ppermute | solution.py:282

commit v4 on v3

--- a/solution.py
+++ b/solution.py
@@ -18,12 +18,13 @@
 HALF = 256
 ITEMS = 2048
 CHUNK = 256
-GROUP = 4
+BATCH = 12
+RHS_SCALE = 8.0
 
 HIGHEST = lax.Precision.HIGHEST
 F32 = jnp.float32
 BF16 = jnp.bfloat16
-RHS_SUM = jnp.float32
+RHS_SUM = jnp.float16
 IMAGE_SUM = jnp.bfloat16
 RHS_SEND = jnp.bfloat16
 
@@ -55,30 +56,25 @@
     return jnp.where(w > 0, 1.0 + w, 0.0).astype(BF16)
 
 
-def confidence_into(conf, dense):
-    for j in range(0, ITEMS, CHUNK):
-        conf[:, j : j + CHUNK] = confidence_of(dense[:, j : j + CHUNK])
-
-
 def load_body(
     users_in, items_in, count_in, vals_in, factors_in,
     near, away, factors, users, items, count, vals, sems,
 ):
-    copies = [
-        pltpu.make_async_copy(source, target, sems.at[k])
-        for k, (source, target) in enumerate(
-            [(users_in, users), (items_in, items), (count_in, count), (vals_in, vals), (factors_in, factors)]
-        )
-    ]
+    batches = vals.shape[0] // BATCH
+    pairs = [(users_in, users), (items_in, items), (count_in, count)]
+    pairs += [(vals_in.at[pl.ds(k * BATCH, BATCH)], vals.at[pl.ds(k * BATCH, BATCH)]) for k in range(batches)]
+    pairs += [(factors_in, factors)]
+    copies = [pltpu.make_async_copy(source, target, sems.at[k]) for k, (source, target) in enumerate(pairs)]
     for copy in copies:
         copy.start()
     near[...] = jnp.zeros_like(near)
     away[...] = jnp.zeros_like(away)
-    for copy in copies[:4]:
+    for copy in copies[:3]:
         copy.wait()
     core = lax.axis_index("core")
     mine = pl.multiple_of(core * OWN, OWN)
     theirs = pl.multiple_of((1 - core) * OWN, OWN)
+    used = count[0, 0]
 
     def put(s, carry):
         user = users[s]
@@ -89,27 +85,39 @@
             away[row, col] = vals[s, pl.ds(theirs + 2 * p * OWN, OWN), :]
         return carry
 
-    def put_group(group, carry):
-        for k in range(GROUP):
-            put(group * GROUP + k, carry)
-        return carry
-
-    used = count[0, 0]
-    groups = used // GROUP
-    lax.fori_loop(0, groups, put_group, 0)
-    lax.fori_loop(groups * GROUP, used, put, 0)
-    copies[4].wait()
+    for k in range(batches):
+        copies[3 + k].wait()
+        end = (k + 1) * BATCH
+
+        @pl.when(used >= end)
+        def _():
+            for s in range(k * BATCH, end):
+                put(s, 0)
+
+        @pl.when(used < end)
+        def _():
+            lax.fori_loop(k * BATCH, used, put, 0)
+
+    copies[-1].wait()
 
 
 def near_rhs_body(near, away, factors, conf_own, conf_other, sums):
-    confidence_into(conf_own, near)
-    sums[...] = jnp.dot(conf_own[...], factors[...], preferred_element_type=F32)
-    confidence_into(conf_other, away)
-
-
-def far_rhs_body(far, distant, sums, out, conf):
-    confidence_into(conf, far)
-    halves_of(sums[...] + jnp.dot(conf[...], distant[...], preferred_element_type=F32), out)
+    total = jnp.zeros((HALF, RANK), F32)
+    for j in range(0, ITEMS, CHUNK):
+        conf = confidence_of(near[:, j : j + CHUNK])
+        conf_own[:, j : j + CHUNK] = conf
+        total = total + jnp.dot(conf, factors[j : j + CHUNK, :], preferred_element_type=F32)
+    sums[...] = total
+    for j in range(0, ITEMS, CHUNK):
+        conf_other[:, j : j + CHUNK] = confidence_of(away[:, j : j + CHUNK])
+
+
+def far_rhs_body(far, distant, sums, out):
+    total = sums[...]
+    for j in range(0, ITEMS, CHUNK):
+        conf = confidence_of(far[:, j : j + CHUNK])
+        total = total + jnp.dot(conf, distant[j : j + CHUNK, :], preferred_element_type=F32)
+    halves_of(total * RHS_SCALE, out)
 
 
 def scores_of(rows, factors, j):
@@ -118,17 +126,14 @@
     )
 
 
-def apply_body(dirs, near, far, factors, distant, out, weighted):
+def apply_body(dirs, near, far, factors, distant, out):
     rows = dirs[...].reshape(HALF, RANK)
-    for k, (dense, items) in enumerate([(near, factors), (far, distant)]):
+    total = jnp.zeros((HALF, RANK), F32)
+    for dense, items in [(near, factors), (far, distant)]:
         for j in range(0, ITEMS, CHUNK):
-            product = scores_of(rows, items, j) * dense[:, j : j + CHUNK].astype(F32)
-            weighted[k, :, j : j + CHUNK] = product.astype(BF16)
-    halves_of(
-        jnp.dot(weighted[0], factors[...], preferred_element_type=F32)
-        + jnp.dot(weighted[1], distant[...], preferred_element_type=F32),
-        out,
-    )
+            weighted = (scores_of(rows, items, j) * dense[:, j : j + CHUNK].astype(F32)).astype(BF16)
+            total = total + jnp.dot(weighted, items[j : j + CHUNK, :], preferred_element_type=F32)
+    halves_of(total, out)
 
 
 def row_sum(value):
@@ -143,7 +148,7 @@
 
 
 def first_body(arrived, direction, sent):
-    rhs = arrived_sum(arrived)
+    rhs = arrived_sum(arrived) * (1.0 / RHS_SCALE)
     direction[...] = rhs
     low = rhs.astype(BF16)
     for k in range(N_Z):
@@ -298,7 +303,7 @@
             pltpu.SMEM((slots,), jnp.int32),
             pltpu.SMEM((1, 1), jnp.int32),
             pltpu.VMEM((slots, TILE, TILE), BF16),
-            pltpu.SemaphoreType.DMA((5,)),
+            pltpu.SemaphoreType.DMA((4 + slots // BATCH,)),
         ],
         54,
     )(tile_users[0, 0], tile_items[0, 0], tile_counts, tile_values[0, 0], item_factors)
@@ -309,7 +314,7 @@
     )(near, away, factors)
     sums, far = lax.optimization_barrier((sums, far))
     (rhs_sums,) = call(
-        far_rhs_body, [shape((N_Z, OWN, RANK), RHS_SUM)], [VMEM] * 3, [pltpu.VMEM((HALF, ITEMS), BF16)]
+        far_rhs_body, [shape((N_Z, OWN, RANK), F32)], [VMEM] * 3
     )(far, distant, sums)
 
     own = shape((OWN, RANK), F32)
@@ -321,12 +326,13 @@
             apply_body,
             [shape((N_Z, OWN, RANK), IMAGE_SUM)],
             [VMEM] * 5,
-            [pltpu.VMEM((N_CORE, HALF, ITEMS), BF16)],
         )(dirs, near, far, factors, distant)
         image, other = lax.optimization_barrier((image, swap(dirs)))
         return exchange(image, "z"), other
 
-    rhs, sent = call(first_body, [own, spread], [VMEM])(exchange(rhs_sums, "z"))
+    rhs, sent = call(first_body, [own, spread], [VMEM])(
+        exchange(rhs_sums.astype(RHS_SUM), "z").astype(F32)
+    )
     zero_own = exchange(sent, "z")
     arrived, zero_other = apply_tiles(zero_own)
     dir_one, res_one, step_one, sent = call(second_body, [own, own, column, spread], [VMEM] * 3)(

time: 133 us -> 129 us (0.970)
  blocking collectives: 110 us -> 106 us
    all_to_all x8, blocking collectives: 110 us -> 106 us  [exchange(): return lax.all_to_all(value, axes, split_axis=0, concat_axis=0, tiled=True)]
  transfers between devices with their start and end apart: 5 -> 5, of which waited for: 2 -> 2; matrix products, arithmetic and copies ran while one was open for 0% -> 0% of each run, Pallas kernels for 6% -> 5%
where the time goes in v4:
time: 129 us
  blocking collectives  106 us (82%)
  Pallas kernels  10.4 us (8%)
  starting transfers between devices  9.17 us (7%)
  waiting for transfers between devices  1.58 us (1%)
  between operations  1.4 us (1%)
    all_to_all x8, blocking collectives, exchange(): return lax.all_to_all(value, axes, split_axis=0, concat_axis=0, tiled=True)  106 us
    ppermute x5, starting transfers between devices, swap(): return lax.ppermute(value, 'core', [(0, 1), (1, 0)])  9.17 us
    pallas_call x2, Pallas kernels, apply_tiles(): call(apply_body, [shape((N_Z, OWN, RANK), IMAGE_SUM)], [VMEM] * 5)  2.91 us
  transfers between devices with their start and end apart: 5, of which 2 were waited for; matrix products, arithmetic and copies ran while one was open for 0% of the time, Pallas kernels for 5%

profile of v4, /device:TPU:1, one launch (start us, length us, event | category | flops | bytes accessed | tf_op | source)
XLA Modules:
  0.0 128.8 jit_solution(15076710398283581394)
XLA Ops:
  0.6 3.3 %collective-permute-start = (bf16[2048,256]{1,0:T(8,128)(2,1)}, bf16[2048,256]{1,0:T(8,128)(2,1)S(1)}, u32[]{:S(2)}, u32[]{:S(2)}) collective-permute-start(bf16[2048,256]{1,0:T(8,128)(2,1)} %factors_in.1), channel_id=1, source_target_pairs={{0,1},{1,0},{2,3},{3,2},{4,5},{5,4},{6,7},{7,6},{8,9},{9,8},{10,11... | collective-permute-start | bytes 3145736 | tf_op jit(solution)/shard_map/ppermute | solution.py:287
  4.6 1.9 %shard_map.77 = (bf16[256,2048]{1,0:T(8,128)(2,1)S(1)}, bf16[256,2048]{1,0:T(8,128)(2,1)S(1)}, bf16[2048,256]{1,0:T(8,128)(2,1)S(1)}) custom-call(s32[48]{0:T(128)} %bitcast.4, s32[48]{0:T(128)} %bitcast.5, s32[1,1]{1,0:T(1,128)S(6)} %copy.8.count_in, bf16[48,128,128]{2,1,0:T(8,128)(2,1)} %bitcast.3, bf16[2048,256]{1,0:T(8,128)(2,1)} %factors_in.1), custom_call_target="tpu_custom_call" | custom-call | tf_op jit(solution)/shard_map/pallas_call | solution.py:297
  6.5 0.1 collective-permute-start.1
  6.6 0.0 collective-permute-done.distant
  6.6 1.1 shard_map.78
  7.8 1.5 %collective-permute-done.1.far = bf16[256,2048]{1,0:T(8,128)(2,1)S(1)} collective-permute-done((bf16[256,2048]{1,0:T(8,128)(2,1)S(1)}, bf16[256,2048]{1,0:T(8,128)(2,1)S(1)}, u32[]{:S(2)}, u32[]{:S(2)}) %collective-permute-start.1) | collective-permute-done | bytes 1048608 | tf_op jit(solution)/shard_map/ppermute | solution.py:287
  9.3 0.4 shard_map.79
  9.8 14.6 %all_to_all.40 = f16[8,32,256]{2,1,0:T(8,128)(2,1)S(1)} all-to-all(f16[8,32,256]{2,1,0:T(8,128)(2,1)S(1)} %convert_element_type.6), channel_id=1, replica_groups=mesh['x'=4,'y'=4,'z'=8,'core'=2] {'z'}, dimensions={0} | all-to-all | bytes 262144 | tf_op jit(solution)/shard_map/all_to_all | solution.py:283
  24.4 10.3 %all_to_all.41.dirs.zero_own = bf16[8,32,256]{2,1,0:T(8,128)(2,1)S(1)} all-to-all(bf16[8,32,256]{2,1,0:T(8,128)(2,1)S(1)} %get-tuple-element.39), channel_id=1, replica_groups=mesh['x'=4,'y'=4,'z'=8,'core'=2] {'z'}, dimensions={0} | all-to-all | bytes 262144 | tf_op jit(solution)/shard_map/all_to_all | solution.py:283
  34.8 0.0 copy-start
  34.8 2.8 %collective-permute-start.2 = (bf16[8,32,256]{2,1,0:T(8,128)(2,1)S(1)}, bf16[8,32,256]{2,1,0:T(8,128)(2,1)S(1)}, u32[]{:S(2)}, u32[]{:S(2)}) collective-permute-start(bf16[8,32,256]{2,1,0:T(8,128)(2,1)S(1)} %all_to_all.41.dirs.zero_own), channel_id=1, source_target_pairs={{0,1},{1,0},{2,3},{3,2},{4,5},{5,4},{6,7},{7,6},{8,9},{9,8},{10,11... | collective-permute-start | bytes 393224 | tf_op jit(solution)/shard_map/ppermute | solution.py:287
  37.5 1.5 %shard_map.81 = bf16[8,32,256]{2,1,0:T(8,128)(2,1)S(1)} custom-call(bf16[8,32,256]{2,1,0:T(8,128)(2,1)S(1)} %all_to_all.41.dirs.zero_own, bf16[256,2048]{1,0:T(8,128)(2,1)S(1)} %get-tuple-element.32.near, bf16[256,2048]{1,0:T(8,128)(2,1)S(1)} %collective-permute-done.1.far, bf16[2048,256]{1,0:T(8,128)(2,1)S(1)} %get-tuple-element.34.factors, ...), custom_call_target="tpu_custom_call" | custom-call | tf_op jit(solution)/shard_map/pallas_call | solution.py:325
  39.0 0.0 collective-permute-done.2.zero_other
  39.0 11.9 %all_to_all.42.arrived = bf16[8,32,256]{2,1,0:T(8,128)(2,1)S(1)} all-to-all(bf16[8,32,256]{2,1,0:T(8,128)(2,1)S(1)} %shard_map.81), channel_id=1, replica_groups=mesh['x'=4,'y'=4,'z'=8,'core'=2] {'z'}, dimensions={0} | all-to-all | bytes 262144 | tf_op jit(solution)/shard_map/all_to_all | solution.py:283
  50.9 0.0 copy-done
  50.9 0.4 shard_map.82
  51.3 10.5 %all_to_all.43.dirs.one_own = bf16[8,32,256]{2,1,0:T(8,128)(2,1)S(1)} all-to-all(bf16[8,32,256]{2,1,0:T(8,128)(2,1)S(1)} %get-tuple-element.42), channel_id=1, replica_groups=mesh['x'=4,'y'=4,'z'=8,'core'=2] {'z'}, dimensions={0} | all-to-all | bytes 262144 | tf_op jit(solution)/shard_map/all_to_all | solution.py:283
  61.8 1.9 %collective-permute-start.3 = (bf16[8,32,256]{2,1,0:T(8,128)(2,1)S(1)}, bf16[8,32,256]{2,1,0:T(8,128)(2,1)S(1)}, u32[]{:S(2)}, u32[]{:S(2)}) collective-permute-start(bf16[8,32,256]{2,1,0:T(8,128)(2,1)S(1)} %all_to_all.43.dirs.one_own), channel_id=1, source_target_pairs={{0,1},{1,0},{2,3},{3,2},{4,5},{5,4},{6,7},{7,6},{8,9},{9,8},{10,11... | collective-permute-start | bytes 393224 | tf_op jit(solution)/shard_map/ppermute | solution.py:287
  63.7 1.5 %shard_map.83 = bf16[8,32,256]{2,1,0:T(8,128)(2,1)S(1)} custom-call(bf16[8,32,256]{2,1,0:T(8,128)(2,1)S(1)} %all_to_all.43.dirs.one_own, bf16[256,2048]{1,0:T(8,128)(2,1)S(1)} %get-tuple-element.32.near, bf16[256,2048]{1,0:T(8,128)(2,1)S(1)} %collective-permute-done.1.far, bf16[2048,256]{1,0:T(8,128)(2,1)S(1)} %get-tuple-element.34.factors, ...), custom_call_target="tpu_custom_call" | custom-call | tf_op jit(solution)/shard_map/pallas_call | solution.py:325
  65.2 0.0 collective-permute-done.3.one_other
  65.2 11.9 %all_to_all.44.arrived = bf16[8,32,256]{2,1,0:T(8,128)(2,1)S(1)} all-to-all(bf16[8,32,256]{2,1,0:T(8,128)(2,1)S(1)} %shard_map.83), channel_id=1, replica_groups=mesh['x'=4,'y'=4,'z'=8,'core'=2] {'z'}, dimensions={0} | all-to-all | bytes 262144 | tf_op jit(solution)/shard_map/all_to_all | solution.py:283
  77.0 0.4 shard_map.84
  77.5 14.2 %all_to_all.45.dirs.two_own = bf16[8,64,256]{2,1,0:T(8,128)(2,1)S(1)} all-to-all(bf16[8,64,256]{2,1,0:T(8,128)(2,1)S(1)} %get-tuple-element.47), channel_id=1, replica_groups=mesh['x'=4,'y'=4,'z'=8,'core'=2] {'z'}, dimensions={0} | all-to-all | bytes 524288 | tf_op jit(solution)/shard_map/all_to_all | solution.py:283
  91.7 1.0 collective-permute-start.4
  92.7 1.1 shard_map.85
  93.8 0.1 collective-permute-done.4.two_other
  93.9 10.6 %all_to_all.46.arrived = f32[16,8,128]{2,1,0:T(8,128)S(1)} all-to-all(f32[16,8,128]{2,1,0:T(8,128)S(1)} %shard_map.85), channel_id=1, replica_groups=mesh['x'=4,'y'=4,'z'=8,'core'=2] {'z','core'}, dimensions={0} | all-to-all | bytes 131072 | tf_op jit(solution)/shard_map/all_to_all | solution.py:283
  104.5 1.1 shard_map.86
  105.6 22.4 %all_to_all.47.arrived = bf16[16,256,128]{2,1,0:T(8,128)(2,1)S(1)} all-to-all(bf16[16,256,128]{2,1,0:T(8,128)(2,1)S(1)} %get-tuple-element.57), channel_id=1, replica_groups=mesh['x'=4,'y'=4,'z'=8,'core'=2] {'x','y'}, dimensions={0} | all-to-all | bytes 2097152 | tf_op jit(solution)/shard_map/all_to_all | solution.py:283
  128.0 0.9 shard_map.87
  (3 shorter events, 0.1 us)
Async XLA Ops:
  0.6 6.0 %collective-permute-start = (bf16[2048,256]{1,0:T(8,128)(2,1)}, bf16[2048,256]{1,0:T(8,128)(2,1)S(1)}, u32[]{:S(2)}, u32[]{:S(2)}) collective-permute-start(bf16[2048,256]{1,0:T(8,128)(2,1)} %factors_in.1), channel_id=1, source_target_pairs={{0,1},{1,0},{2,3},{3,2},{4,5},{5,4},{6,7},{7,6},{8,9},{9,8},{10,11... | collective-permute-start | bytes 3145736 | tf_op jit(solution)/shard_map/ppermute | solution.py:287
  6.5 2.7 %collective-permute-start.1 = (bf16[256,2048]{1,0:T(8,128)(2,1)S(1)}, bf16[256,2048]{1,0:T(8,128)(2,1)S(1)}, u32[]{:S(2)}, u32[]{:S(2)}) collective-permute-start(bf16[256,2048]{1,0:T(8,128)(2,1)S(1)} %get-tuple-element.33.away), channel_id=1, source_target_pairs={{0,1},{1,0},{2,3},{3,2},{4,5},{5,4},{6,7},{7,6},{8,9},{9,8},{10,11... | collective-permute-start | bytes 3145736 | tf_op jit(solution)/shard_map/ppermute | solution.py:287
  34.8 16.1 %copy-start = (f32[256,256]{1,0:T(8,128)S(1)}, f32[256,256]{1,0:T(8,128)}, u32[]{:S(2)}) copy-start(f32[256,256]{1,0:T(8,128)} %gram.5) | copy-start | bytes 786436
  34.8 4.3 %collective-permute-start.2 = (bf16[8,32,256]{2,1,0:T(8,128)(2,1)S(1)}, bf16[8,32,256]{2,1,0:T(8,128)(2,1)S(1)}, u32[]{:S(2)}, u32[]{:S(2)}) collective-permute-start(bf16[8,32,256]{2,1,0:T(8,128)(2,1)S(1)} %all_to_all.41.dirs.zero_own), channel_id=1, source_target_pairs={{0,1},{1,0},{2,3},{3,2},{4,5},{5,4},{6,7},{7,6},{8,9},{9,8},{10,11... | collective-permute-start | bytes 393224 | tf_op jit(solution)/shard_map/ppermute | solution.py:287
  61.8 3.4 %collective-permute-start.3 = (bf16[8,32,256]{2,1,0:T(8,128)(2,1)S(1)}, bf16[8,32,256]{2,1,0:T(8,128)(2,1)S(1)}, u32[]{:S(2)}, u32[]{:S(2)}) collective-permute-start(bf16[8,32,256]{2,1,0:T(8,128)(2,1)S(1)} %all_to_all.43.dirs.one_own), channel_id=1, source_target_pairs={{0,1},{1,0},{2,3},{3,2},{4,5},{5,4},{6,7},{7,6},{8,9},{9,8},{10,11... | collective-permute-start | bytes 393224 | tf_op jit(solution)/shard_map/ppermute | solution.py:287
  91.7 2.2 %collective-permute-start.4 = (bf16[8,64,256]{2,1,0:T(8,128)(2,1)S(1)}, bf16[8,64,256]{2,1,0:T(8,128)(2,1)S(1)}, u32[]{:S(2)}, u32[]{:S(2)}) collective-permute-start(bf16[8,64,256]{2,1,0:T(8,128)(2,1)S(1)} %all_to_all.45.dirs.two_own), channel_id=1, source_target_pairs={{0,1},{1,0},{2,3},{3,2},{4,5},{5,4},{6,7},{7,6},{8,9},{9,8},{10,11... | collective-permute-start | bytes 786440 | tf_op jit(solution)/shard_map/ppermute | solution.py:287

commit v5 on v4

--- a/solution.py
+++ b/solution.py
@@ -327,19 +327,18 @@
             [shape((N_Z, OWN, RANK), IMAGE_SUM)],
             [VMEM] * 5,
         )(dirs, near, far, factors, distant)
-        image, other = lax.optimization_barrier((image, swap(dirs)))
-        return exchange(image, "z"), other
+        return exchange(image, "z")
 
     rhs, sent = call(first_body, [own, spread], [VMEM])(
         exchange(rhs_sums.astype(RHS_SUM), "z").astype(F32)
     )
     zero_own = exchange(sent, "z")
-    arrived, zero_other = apply_tiles(zero_own)
+    arrived = apply_tiles(zero_own)
     dir_one, res_one, step_one, sent = call(second_body, [own, own, column, spread], [VMEM] * 3)(
         arrived, item_gram, rhs
     )
     one_own = exchange(sent, "z")
-    arrived, one_other = apply_tiles(one_own)
+    arrived = apply_tiles(one_own)
     dir_two, partial, norm, step_two, sent = call(
         third_body,
         [own, own, column, column, shape((N_Z, 2 * OWN, RANK), BF16)],
@@ -353,7 +352,10 @@
         [VMEM] * 10,
         [pltpu.VMEM((HALF, RANK), BF16), pltpu.VMEM((4, TILE, TILE), F32), message, message],
     )(two_own, near, far, factors, distant, item_gram, dir_two, norm, step_one, step_two)
-    sent, two_other = lax.optimization_barrier((sent, swap(two_own)))
+    zero_two, one_two = lax.optimization_barrier((zero_own, one_own, two_own))[:2]
+    sent, zero_other, one_other, two_other = lax.optimization_barrier(
+        (sent, swap(zero_two), swap(one_two), swap(two_own))
+    )
     own_step, sent = call(
         close_body,
         [shape((OWN, TILE), F32), shape((N_ITEM, RANK, TILE), RHS_SEND)],

time: 129 us -> 126 us (0.977)
  blocking collectives: 106 us -> 100 us
  starting transfers between devices: 9.17 us -> 11.3 us
    all_to_all x8, blocking collectives: 106 us -> 100 us  [exchange(): return lax.all_to_all(value, axes, split_axis=0, concat_axis=0, tiled=True)]
    ppermute x5, starting transfers between devices: 9.17 us -> 11.3 us  [swap(): return lax.ppermute(value, 'core', [(0, 1), (1, 0)])]
  transfers between devices with their start and end apart: 5 -> 5, of which waited for: 2 -> 1; matrix products, arithmetic and copies ran while one was open for 0% -> 0% of each run, Pallas kernels for 5% -> 3%
where the time goes in v5:
time: 126 us; the launch traced here: 125 us
  blocking collectives  100 us (79%)
  starting transfers between devices  11.3 us (9%)
  Pallas kernels  10.4 us (8%)
  waiting for transfers between devices  1.53 us (1%)
  between operations  1.41 us (1%)
    all_to_all x8, blocking collectives, exchange(): return lax.all_to_all(value, axes, split_axis=0, concat_axis=0, tiled=True)  100 us
    ppermute x5, starting transfers between devices, swap(): return lax.ppermute(value, 'core', [(0, 1), (1, 0)])  11.3 us
    pallas_call x2, Pallas kernels, apply_tiles(): call(apply_body, [shape((N_Z, OWN, RANK), IMAGE_SUM)], [VMEM] * 5)  2.91 us
  transfers between devices with their start and end apart: 5, of which 1 were waited for; matrix products, arithmetic and copies ran while one was open for 0% of the time, Pallas kernels for 3%

profile of v5, /device:TPU:1, one launch (start us, length us, event | category | flops | bytes accessed | tf_op | source)
XLA Modules:
  0.0 125.1 jit_solution(9114021233884022238)
XLA Ops:
  0.6 3.3 %collective-permute-start = (bf16[2048,256]{1,0:T(8,128)(2,1)}, bf16[2048,256]{1,0:T(8,128)(2,1)S(1)}, u32[]{:S(2)}, u32[]{:S(2)}) collective-permute-start(bf16[2048,256]{1,0:T(8,128)(2,1)} %factors_in.1), channel_id=1, source_target_pairs={{0,1},{1,0},{2,3},{3,2},{4,5},{5,4},{6,7},{7,6},{8,9},{9,8},{10,11... | collective-permute-start | bytes 3145736 | tf_op jit(solution)/shard_map/ppermute | solution.py:287
  4.6 1.9 %shard_map.77 = (bf16[256,2048]{1,0:T(8,128)(2,1)S(1)}, bf16[256,2048]{1,0:T(8,128)(2,1)S(1)}, bf16[2048,256]{1,0:T(8,128)(2,1)S(1)}) custom-call(s32[48]{0:T(128)} %bitcast.4, s32[48]{0:T(128)} %bitcast.5, s32[1,1]{1,0:T(1,128)S(6)} %copy.8.count_in, bf16[48,128,128]{2,1,0:T(8,128)(2,1)} %bitcast.3, bf16[2048,256]{1,0:T(8,128)(2,1)} %factors_in.1), custom_call_target="tpu_custom_call" | custom-call | tf_op jit(solution)/shard_map/pallas_call | solution.py:297
  6.5 0.1 collective-permute-start.1
  6.6 0.0 collective-permute-done.distant
  6.6 1.1 shard_map.78
  7.8 1.5 %collective-permute-done.1.far = bf16[256,2048]{1,0:T(8,128)(2,1)S(1)} collective-permute-done((bf16[256,2048]{1,0:T(8,128)(2,1)S(1)}, bf16[256,2048]{1,0:T(8,128)(2,1)S(1)}, u32[]{:S(2)}, u32[]{:S(2)}) %collective-permute-start.1) | collective-permute-done | bytes 1048608 | tf_op jit(solution)/shard_map/ppermute | solution.py:287
  9.3 0.4 shard_map.79
  9.8 14.6 %all_to_all.40 = f16[8,32,256]{2,1,0:T(8,128)(2,1)S(1)} all-to-all(f16[8,32,256]{2,1,0:T(8,128)(2,1)S(1)} %convert_element_type.6), channel_id=1, replica_groups=mesh['x'=4,'y'=4,'z'=8,'core'=2] {'z'}, dimensions={0} | all-to-all | bytes 262144 | tf_op jit(solution)/shard_map/all_to_all | solution.py:283
  24.4 10.3 %all_to_all.41.dirs.zero_own = bf16[8,32,256]{2,1,0:T(8,128)(2,1)S(1)} all-to-all(bf16[8,32,256]{2,1,0:T(8,128)(2,1)S(1)} %get-tuple-element.39), channel_id=1, replica_groups=mesh['x'=4,'y'=4,'z'=8,'core'=2] {'z'}, dimensions={0} | all-to-all | bytes 262144 | tf_op jit(solution)/shard_map/all_to_all | solution.py:283
  34.8 0.0 copy-start
  34.8 1.5 %shard_map.81 = bf16[8,32,256]{2,1,0:T(8,128)(2,1)S(1)} custom-call(bf16[8,32,256]{2,1,0:T(8,128)(2,1)S(1)} %all_to_all.41.dirs.zero_own, bf16[256,2048]{1,0:T(8,128)(2,1)S(1)} %get-tuple-element.32.near, bf16[256,2048]{1,0:T(8,128)(2,1)S(1)} %collective-permute-done.1.far, bf16[2048,256]{1,0:T(8,128)(2,1)S(1)} %get-tuple-element.34.factors, ...), custom_call_target="tpu_custom_call" | custom-call | tf_op jit(solution)/shard_map/pallas_call | solution.py:325
  36.2 10.3 %all_to_all.42.arrived = bf16[8,32,256]{2,1,0:T(8,128)(2,1)S(1)} all-to-all(bf16[8,32,256]{2,1,0:T(8,128)(2,1)S(1)} %shard_map.81), channel_id=1, replica_groups=mesh['x'=4,'y'=4,'z'=8,'core'=2] {'z'}, dimensions={0} | all-to-all | bytes 262144 | tf_op jit(solution)/shard_map/all_to_all | solution.py:283
  46.5 0.0 copy-done
  46.5 0.4 shard_map.82
  46.9 10.3 %all_to_all.43.dirs.one_own = bf16[8,32,256]{2,1,0:T(8,128)(2,1)S(1)} all-to-all(bf16[8,32,256]{2,1,0:T(8,128)(2,1)S(1)} %get-tuple-element.41), channel_id=1, replica_groups=mesh['x'=4,'y'=4,'z'=8,'core'=2] {'z'}, dimensions={0} | all-to-all | bytes 262144 | tf_op jit(solution)/shard_map/all_to_all | solution.py:283
  57.2 1.5 %shard_map.83 = bf16[8,32,256]{2,1,0:T(8,128)(2,1)S(1)} custom-call(bf16[8,32,256]{2,1,0:T(8,128)(2,1)S(1)} %all_to_all.43.dirs.one_own, bf16[256,2048]{1,0:T(8,128)(2,1)S(1)} %get-tuple-element.32.near, bf16[256,2048]{1,0:T(8,128)(2,1)S(1)} %collective-permute-done.1.far, bf16[2048,256]{1,0:T(8,128)(2,1)S(1)} %get-tuple-element.34.factors, ...), custom_call_target="tpu_custom_call" | custom-call | tf_op jit(solution)/shard_map/pallas_call | solution.py:325
  58.7 10.3 %all_to_all.44.arrived = bf16[8,32,256]{2,1,0:T(8,128)(2,1)S(1)} all-to-all(bf16[8,32,256]{2,1,0:T(8,128)(2,1)S(1)} %shard_map.83), channel_id=1, replica_groups=mesh['x'=4,'y'=4,'z'=8,'core'=2] {'z'}, dimensions={0} | all-to-all | bytes 262144 | tf_op jit(solution)/shard_map/all_to_all | solution.py:283
  69.0 0.4 shard_map.84
  69.5 11.7 %all_to_all.45.dirs.two_own = bf16[8,64,256]{2,1,0:T(8,128)(2,1)S(1)} all-to-all(bf16[8,64,256]{2,1,0:T(8,128)(2,1)S(1)} %get-tuple-element.45), channel_id=1, replica_groups=mesh['x'=4,'y'=4,'z'=8,'core'=2] {'z'}, dimensions={0} | all-to-all | bytes 524288 | tf_op jit(solution)/shard_map/all_to_all | solution.py:283
  81.2 7.4 %collective-permute-start.4 = (bf16[8,64,256]{2,1,0:T(8,128)(2,1)S(1)}, bf16[8,64,256]{2,1,0:T(8,128)(2,1)S(1)}, u32[]{:S(2)}, u32[]{:S(2)}) collective-permute-start(bf16[8,64,256]{2,1,0:T(8,128)(2,1)S(1)} %all_to_all.45.dirs.two_own), channel_id=1, source_target_pairs={{0,1},{1,0},{2,3},{3,2},{4,5},{5,4},{6,7},{7,6},{8,9},{9,8},{10,11... | collective-permute-start | bytes 786440 | tf_op jit(solution)/shard_map/ppermute | solution.py:287
  88.6 0.0 collective-permute-start.2
  88.6 0.5 collective-permute-start.3
  89.1 1.1 shard_map.85
  90.2 0.0 collective-permute-done.2.zero_other
  90.2 0.0 collective-permute-done.3.one_other
  90.3 0.0 collective-permute-done.4.two_other
  90.3 10.5 %all_to_all.46.arrived = f32[16,8,128]{2,1,0:T(8,128)S(1)} all-to-all(f32[16,8,128]{2,1,0:T(8,128)S(1)} %shard_map.85), channel_id=1, replica_groups=mesh['x'=4,'y'=4,'z'=8,'core'=2] {'z','core'}, dimensions={0} | all-to-all | bytes 131072 | tf_op jit(solution)/shard_map/all_to_all | solution.py:283
  100.7 1.1 shard_map.86
  101.9 22.4 %all_to_all.47.arrived = bf16[16,256,128]{2,1,0:T(8,128)(2,1)S(1)} all-to-all(bf16[16,256,128]{2,1,0:T(8,128)(2,1)S(1)} %get-tuple-element.57), channel_id=1, replica_groups=mesh['x'=4,'y'=4,'z'=8,'core'=2] {'x','y'}, dimensions={0} | all-to-all | bytes 2097152 | tf_op jit(solution)/shard_map/all_to_all | solution.py:283
  124.2 0.9 shard_map.87
  (3 shorter events, 0.1 us)
Async XLA Ops:
  0.6 6.0 %collective-permute-start = (bf16[2048,256]{1,0:T(8,128)(2,1)}, bf16[2048,256]{1,0:T(8,128)(2,1)S(1)}, u32[]{:S(2)}, u32[]{:S(2)}) collective-permute-start(bf16[2048,256]{1,0:T(8,128)(2,1)} %factors_in.1), channel_id=1, source_target_pairs={{0,1},{1,0},{2,3},{3,2},{4,5},{5,4},{6,7},{7,6},{8,9},{9,8},{10,11... | collective-permute-start | bytes 3145736 | tf_op jit(solution)/shard_map/ppermute | solution.py:287
  6.5 2.7 %collective-permute-start.1 = (bf16[256,2048]{1,0:T(8,128)(2,1)S(1)}, bf16[256,2048]{1,0:T(8,128)(2,1)S(1)}, u32[]{:S(2)}, u32[]{:S(2)}) collective-permute-start(bf16[256,2048]{1,0:T(8,128)(2,1)S(1)} %get-tuple-element.33.away), channel_id=1, source_target_pairs={{0,1},{1,0},{2,3},{3,2},{4,5},{5,4},{6,7},{7,6},{8,9},{9,8},{10,11... | collective-permute-start | bytes 3145736 | tf_op jit(solution)/shard_map/ppermute | solution.py:287
  34.8 11.8 %copy-start = (f32[256,256]{1,0:T(8,128)S(1)}, f32[256,256]{1,0:T(8,128)}, u32[]{:S(2)}) copy-start(f32[256,256]{1,0:T(8,128)} %gram.5) | copy-start | bytes 786436
  81.2 9.1 %collective-permute-start.4 = (bf16[8,64,256]{2,1,0:T(8,128)(2,1)S(1)}, bf16[8,64,256]{2,1,0:T(8,128)(2,1)S(1)}, u32[]{:S(2)}, u32[]{:S(2)}) collective-permute-start(bf16[8,64,256]{2,1,0:T(8,128)(2,1)S(1)} %all_to_all.45.dirs.two_own), channel_id=1, source_target_pairs={{0,1},{1,0},{2,3},{3,2},{4,5},{5,4},{6,7},{7,6},{8,9},{9,8},{10,11... | collective-permute-start | bytes 786440 | tf_op jit(solution)/shard_map/ppermute | solution.py:287
  88.6 1.6 %collective-permute-start.2 = (bf16[8,32,256]{2,1,0:T(8,128)(2,1)S(1)}, bf16[8,32,256]{2,1,0:T(8,128)(2,1)S(1)}, u32[]{:S(2)}, u32[]{:S(2)}) collective-permute-start(bf16[8,32,256]{2,1,0:T(8,128)(2,1)S(1)} %all_to_all.41.dirs.zero_own), channel_id=1, source_target_pairs={{0,1},{1,0},{2,3},{3,2},{4,5},{5,4},{6,7},{7,6},{8,9},{9,8},{10,11... | collective-permute-start | bytes 393224 | tf_op jit(solution)/shard_map/ppermute | solution.py:287
  88.6 1.6 %collective-permute-start.3 = (bf16[8,32,256]{2,1,0:T(8,128)(2,1)S(1)}, bf16[8,32,256]{2,1,0:T(8,128)(2,1)S(1)}, u32[]{:S(2)}, u32[]{:S(2)}) collective-permute-start(bf16[8,32,256]{2,1,0:T(8,128)(2,1)S(1)} %all_to_all.43.dirs.one_own), channel_id=1, source_target_pairs={{0,1},{1,0},{2,3},{3,2},{4,5},{5,4},{6,7},{7,6},{8,9},{9,8},{10,11... | collective-permute-start | bytes 393224 | tf_op jit(solution)/shard_map/ppermute | solution.py:287

commit v6 on v5

--- a/solution.py
+++ b/solution.py
@@ -127,7 +127,7 @@
 
 
 def apply_body(dirs, near, far, factors, distant, out):
-    rows = dirs[...].reshape(HALF, RANK)
+    rows = dirs[...].reshape(HALF, RANK).astype(BF16)
     total = jnp.zeros((HALF, RANK), F32)
     for dense, items in [(near, factors), (far, distant)]:
         for j in range(0, ITEMS, CHUNK):
@@ -150,9 +150,10 @@
 def first_body(arrived, direction, sent):
     rhs = arrived_sum(arrived) * (1.0 / RHS_SCALE)
     direction[...] = rhs
-    low = rhs.astype(BF16)
+    high = rhs.astype(BF16).astype(F32)
+    value = high + 0.85 * (rhs - high)
     for k in range(N_Z):
-        sent[k] = low
+        sent[k] = value
 
 
 def step_of(arrived, gram, direction, residual):
@@ -185,11 +186,8 @@
     norm_out[...] = norm
     step_out[...] = alpha
     low = new.astype(BF16)
-    rest = so_far - step_one[...] * first.astype(BF16).astype(F32) - alpha * second.astype(BF16).astype(F32)
-    rest = rest.astype(BF16)
     for k in range(N_Z):
-        sent[k, :OWN] = low
-        sent[k, OWN:] = rest
+        sent[k] = low
 
 
 def quad_body(
@@ -197,7 +195,7 @@
     sent, rows, column, first, second,
 ):
     for z in range(N_Z):
-        rows[z * OWN : (z + 1) * OWN, :] = dirs[z, :OWN]
+        rows[z * OWN : (z + 1) * OWN, :] = dirs[z]
     lanes = jnp.zeros((HALF, TILE), F32)
     for dense, items in [(near, factors), (far, distant)]:
         for j in range(0, ITEMS, CHUNK):
@@ -254,10 +252,9 @@
             for h in range(0, RANK, TILE):
                 lanes = slice(h, h + TILE)
                 rows[half * HALF + z * OWN : half * HALF + (z + 1) * OWN, lanes] = (
-                    alphas[0, at, :] * zero[z, :, lanes].astype(F32)
+                    alphas[0, at, :] * zero[z, :, lanes]
                     + alphas[1, at, :] * one[z, :, lanes].astype(F32)
-                    + two[z, OWN:, lanes].astype(F32)
-                    + alphas[2, at, :] * two[z, :OWN, lanes].astype(F32)
+                    + alphas[2, at, :] * two[z, :, lanes].astype(F32)
                 )
     mine = core * HALF + lax.axis_index("z") * OWN
     own_step[...] = alphas[2, pl.ds(pl.multiple_of(mine, OWN), OWN), :]
@@ -329,10 +326,11 @@
         )(dirs, near, far, factors, distant)
         return exchange(image, "z")
 
-    rhs, sent = call(first_body, [own, spread], [VMEM])(
+    rhs, sent = call(first_body, [own, shape((N_Z, OWN, RANK), F32)], [VMEM])(
         exchange(rhs_sums.astype(RHS_SUM), "z").astype(F32)
     )
-    zero_own = exchange(sent, "z")
+    zero_sent = exchange(sent.astype(jnp.float16), "z")
+    zero_own = zero_sent.astype(F32)
     arrived = apply_tiles(zero_own)
     dir_one, res_one, step_one, sent = call(second_body, [own, own, column, spread], [VMEM] * 3)(
         arrived, item_gram, rhs
@@ -341,7 +339,7 @@
     arrived = apply_tiles(one_own)
     dir_two, partial, norm, step_two, sent = call(
         third_body,
-        [own, own, column, column, shape((N_Z, 2 * OWN, RANK), BF16)],
+        [own, own, column, column, spread],
         [VMEM] * 6,
     )(arrived, item_gram, rhs, dir_one, res_one, step_one)
     two_own = exchange(sent, "z")
@@ -352,9 +350,9 @@
         [VMEM] * 10,
         [pltpu.VMEM((HALF, RANK), BF16), pltpu.VMEM((4, TILE, TILE), F32), message, message],
     )(two_own, near, far, factors, distant, item_gram, dir_two, norm, step_one, step_two)
-    zero_two, one_two = lax.optimization_barrier((zero_own, one_own, two_own))[:2]
+    zero_two, one_two = lax.optimization_barrier((zero_sent, one_own, two_own))[:2]
     sent, zero_other, one_other, two_other = lax.optimization_barrier(
-        (sent, swap(zero_two), swap(one_two), swap(two_own))
+        (sent, swap(zero_two).astype(F32), swap(one_two), swap(two_own))
     )
     own_step, sent = call(
         close_body,

time: 126 us -> 124 us (0.984)
    all_to_all x8, blocking collectives: 100 us -> 98.9 us  [exchange(): return lax.all_to_all(value, axes, split_axis=0, concat_axis=0, tiled=True)]
where the time goes in v6:
time: 124 us
  blocking collectives  98.9 us (80%)
  starting transfers between devices  11.3 us (9%)
  Pallas kernels  10.4 us (8%)
  waiting for transfers between devices  1.52 us (1%)
  between operations  1.44 us (1%)
    all_to_all x8, blocking collectives, exchange(): return lax.all_to_all(value, axes, split_axis=0, concat_axis=0, tiled=True)  98.9 us
    ppermute x5, starting transfers between devices, swap(): return lax.ppermute(value, 'core', [(0, 1), (1, 0)])  11.3 us
    pallas_call x2, Pallas kernels, apply_tiles(): call(apply_body, [shape((N_Z, OWN, RANK), IMAGE_SUM)], [VMEM] * 5)  2.91 us
  transfers between devices with their start and end apart: 5, of which 1 were waited for; matrix products, arithmetic and copies ran while one was open for 0% of the time, Pallas kernels for 3%

profile of v6, /device:TPU:1, one launch (start us, length us, event | category | flops | bytes accessed | tf_op | source)
XLA Modules:
  0.0 123.7 jit_solution(828615785881282377)
XLA Ops:
  0.6 3.3 %collective-permute-start = (bf16[2048,256]{1,0:T(8,128)(2,1)}, bf16[2048,256]{1,0:T(8,128)(2,1)S(1)}, u32[]{:S(2)}, u32[]{:S(2)}) collective-permute-start(bf16[2048,256]{1,0:T(8,128)(2,1)} %factors_in.1), channel_id=1, source_target_pairs={{0,1},{1,0},{2,3},{3,2},{4,5},{5,4},{6,7},{7,6},{8,9},{9,8},{10,11... | collective-permute-start | bytes 3145736 | tf_op jit(solution)/shard_map/ppermute | solution.py:284
  4.6 1.9 %shard_map.77 = (bf16[256,2048]{1,0:T(8,128)(2,1)S(1)}, bf16[256,2048]{1,0:T(8,128)(2,1)S(1)}, bf16[2048,256]{1,0:T(8,128)(2,1)S(1)}) custom-call(s32[48]{0:T(128)} %bitcast.4, s32[48]{0:T(128)} %bitcast.5, s32[1,1]{1,0:T(1,128)S(6)} %copy.8.count_in, bf16[48,128,128]{2,1,0:T(8,128)(2,1)} %bitcast.3, bf16[2048,256]{1,0:T(8,128)(2,1)} %factors_in.1), custom_call_target="tpu_custom_call" | custom-call | tf_op jit(solution)/shard_map/pallas_call | solution.py:294
  6.5 0.1 collective-permute-start.1
  6.6 0.0 collective-permute-done.distant
  6.6 1.1 shard_map.78
  7.8 1.5 %collective-permute-done.1.far = bf16[256,2048]{1,0:T(8,128)(2,1)S(1)} collective-permute-done((bf16[256,2048]{1,0:T(8,128)(2,1)S(1)}, bf16[256,2048]{1,0:T(8,128)(2,1)S(1)}, u32[]{:S(2)}, u32[]{:S(2)}) %collective-permute-start.1) | collective-permute-done | bytes 1048608 | tf_op jit(solution)/shard_map/ppermute | solution.py:284
  9.3 0.4 shard_map.79
  9.8 14.6 %all_to_all.40 = f16[8,32,256]{2,1,0:T(8,128)(2,1)S(1)} all-to-all(f16[8,32,256]{2,1,0:T(8,128)(2,1)S(1)} %convert_element_type.15), channel_id=1, replica_groups=mesh['x'=4,'y'=4,'z'=8,'core'=2] {'z'}, dimensions={0} | all-to-all | bytes 262144 | tf_op jit(solution)/shard_map/all_to_all | solution.py:280
  24.5 10.3 %all_to_all.41 = f16[8,32,256]{2,1,0:T(8,128)(2,1)S(1)} all-to-all(f16[8,32,256]{2,1,0:T(8,128)(2,1)S(1)} %convert_element_type.17), channel_id=1, replica_groups=mesh['x'=4,'y'=4,'z'=8,'core'=2] {'z'}, dimensions={0} | all-to-all | bytes 262144 | tf_op jit(solution)/shard_map/all_to_all | solution.py:280
  34.8 0.0 copy-start
  34.8 1.5 %shard_map.81 = bf16[8,32,256]{2,1,0:T(8,128)(2,1)S(1)} custom-call(f32[8,32,256]{2,1,0:T(8,128)S(1)} %convert_element_type.18.dirs.zero_own, bf16[256,2048]{1,0:T(8,128)(2,1)S(1)} %get-tuple-element.32.near, bf16[256,2048]{1,0:T(8,128)(2,1)S(1)} %collective-permute-done.1.far, bf16[2048,256]{1,0:T(8,128)(2,1)S(1)} %get-tuple-element.34.factors, ...), custom_call_target="tpu_custom_call" | custom-call | tf_op jit(solution)/shard_map/pallas_call | solution.py:322
  36.3 10.3 %all_to_all.42.arrived = bf16[8,32,256]{2,1,0:T(8,128)(2,1)S(1)} all-to-all(bf16[8,32,256]{2,1,0:T(8,128)(2,1)S(1)} %shard_map.81), channel_id=1, replica_groups=mesh['x'=4,'y'=4,'z'=8,'core'=2] {'z'}, dimensions={0} | all-to-all | bytes 262144 | tf_op jit(solution)/shard_map/all_to_all | solution.py:280
  46.6 0.0 copy-done
  46.6 0.4 shard_map.82
  47.0 10.3 %all_to_all.43.dirs.one_own = bf16[8,32,256]{2,1,0:T(8,128)(2,1)S(1)} all-to-all(bf16[8,32,256]{2,1,0:T(8,128)(2,1)S(1)} %get-tuple-element.41), channel_id=1, replica_groups=mesh['x'=4,'y'=4,'z'=8,'core'=2] {'z'}, dimensions={0} | all-to-all | bytes 262144 | tf_op jit(solution)/shard_map/all_to_all | solution.py:280
  57.3 1.5 %shard_map.83 = bf16[8,32,256]{2,1,0:T(8,128)(2,1)S(1)} custom-call(bf16[8,32,256]{2,1,0:T(8,128)(2,1)S(1)} %all_to_all.43.dirs.one_own, bf16[256,2048]{1,0:T(8,128)(2,1)S(1)} %get-tuple-element.32.near, bf16[256,2048]{1,0:T(8,128)(2,1)S(1)} %collective-permute-done.1.far, bf16[2048,256]{1,0:T(8,128)(2,1)S(1)} %get-tuple-element.34.factors, ...), custom_call_target="tpu_custom_call" | custom-call | tf_op jit(solution)/shard_map/pallas_call | solution.py:322
  58.8 10.3 %all_to_all.44.arrived = bf16[8,32,256]{2,1,0:T(8,128)(2,1)S(1)} all-to-all(bf16[8,32,256]{2,1,0:T(8,128)(2,1)S(1)} %shard_map.83), channel_id=1, replica_groups=mesh['x'=4,'y'=4,'z'=8,'core'=2] {'z'}, dimensions={0} | all-to-all | bytes 262144 | tf_op jit(solution)/shard_map/all_to_all | solution.py:280
  69.1 0.4 shard_map.84
  69.5 10.3 %all_to_all.45.dirs.two_own = bf16[8,32,256]{2,1,0:T(8,128)(2,1)S(1)} all-to-all(bf16[8,32,256]{2,1,0:T(8,128)(2,1)S(1)} %get-tuple-element.45), channel_id=1, replica_groups=mesh['x'=4,'y'=4,'z'=8,'core'=2] {'z'}, dimensions={0} | all-to-all | bytes 262144 | tf_op jit(solution)/shard_map/all_to_all | solution.py:280
  79.8 7.4 %collective-permute-start.2 = (f16[8,32,256]{2,1,0:T(8,128)(2,1)S(1)}, f16[8,32,256]{2,1,0:T(8,128)(2,1)S(1)}, u32[]{:S(2)}, u32[]{:S(2)}) collective-permute-start(f16[8,32,256]{2,1,0:T(8,128)(2,1)S(1)} %all_to_all.41), channel_id=1, source_target_pairs={{0,1},{1,0},{2,3},{3,2},{4,5},{5,4},{6,7},{7,6},{8,9},{9,8},{10,11... | collective-permute-start | bytes 393224 | tf_op jit(solution)/shard_map/ppermute | solution.py:284
  87.3 0.0 collective-permute-start.3
  87.3 0.5 collective-permute-start.4
  87.8 1.1 shard_map.85
  88.9 0.0 collective-permute-done.2
  88.9 0.0 collective-permute-done.3.one_other
  88.9 0.0 collective-permute-done.4.two_other
  88.9 10.4 %all_to_all.46.arrived = f32[16,8,128]{2,1,0:T(8,128)S(1)} all-to-all(f32[16,8,128]{2,1,0:T(8,128)S(1)} %shard_map.85), channel_id=1, replica_groups=mesh['x'=4,'y'=4,'z'=8,'core'=2] {'z','core'}, dimensions={0} | all-to-all | bytes 131072 | tf_op jit(solution)/shard_map/all_to_all | solution.py:280
  99.3 1.1 shard_map.86
  100.5 22.4 %all_to_all.47.arrived = bf16[16,256,128]{2,1,0:T(8,128)(2,1)S(1)} all-to-all(bf16[16,256,128]{2,1,0:T(8,128)(2,1)S(1)} %get-tuple-element.57), channel_id=1, replica_groups=mesh['x'=4,'y'=4,'z'=8,'core'=2] {'x','y'}, dimensions={0} | all-to-all | bytes 2097152 | tf_op jit(solution)/shard_map/all_to_all | solution.py:280
  122.8 0.9 shard_map.87
  (6 shorter events, 0.1 us)
Async XLA Ops:
  0.6 6.0 %collective-permute-start = (bf16[2048,256]{1,0:T(8,128)(2,1)}, bf16[2048,256]{1,0:T(8,128)(2,1)S(1)}, u32[]{:S(2)}, u32[]{:S(2)}) collective-permute-start(bf16[2048,256]{1,0:T(8,128)(2,1)} %factors_in.1), channel_id=1, source_target_pairs={{0,1},{1,0},{2,3},{3,2},{4,5},{5,4},{6,7},{7,6},{8,9},{9,8},{10,11... | collective-permute-start | bytes 3145736 | tf_op jit(solution)/shard_map/ppermute | solution.py:284
  6.5 2.7 %collective-permute-start.1 = (bf16[256,2048]{1,0:T(8,128)(2,1)S(1)}, bf16[256,2048]{1,0:T(8,128)(2,1)S(1)}, u32[]{:S(2)}, u32[]{:S(2)}) collective-permute-start(bf16[256,2048]{1,0:T(8,128)(2,1)S(1)} %get-tuple-element.33.away), channel_id=1, source_target_pairs={{0,1},{1,0},{2,3},{3,2},{4,5},{5,4},{6,7},{7,6},{8,9},{9,8},{10,11... | collective-permute-start | bytes 3145736 | tf_op jit(solution)/shard_map/ppermute | solution.py:284
  34.8 11.8 %copy-start = (f32[256,256]{1,0:T(8,128)S(1)}, f32[256,256]{1,0:T(8,128)}, u32[]{:S(2)}) copy-start(f32[256,256]{1,0:T(8,128)} %gram.5) | copy-start | bytes 786436
  79.8 9.0 %collective-permute-start.2 = (f16[8,32,256]{2,1,0:T(8,128)(2,1)S(1)}, f16[8,32,256]{2,1,0:T(8,128)(2,1)S(1)}, u32[]{:S(2)}, u32[]{:S(2)}) collective-permute-start(f16[8,32,256]{2,1,0:T(8,128)(2,1)S(1)} %all_to_all.41), channel_id=1, source_target_pairs={{0,1},{1,0},{2,3},{3,2},{4,5},{5,4},{6,7},{7,6},{8,9},{9,8},{10,11... | collective-permute-start | bytes 393224 | tf_op jit(solution)/shard_map/ppermute | solution.py:284
  87.3 1.7 %collective-permute-start.3 = (bf16[8,32,256]{2,1,0:T(8,128)(2,1)S(1)}, bf16[8,32,256]{2,1,0:T(8,128)(2,1)S(1)}, u32[]{:S(2)}, u32[]{:S(2)}) collective-permute-start(bf16[8,32,256]{2,1,0:T(8,128)(2,1)S(1)} %all_to_all.43.dirs.one_own), channel_id=1, source_target_pairs={{0,1},{1,0},{2,3},{3,2},{4,5},{5,4},{6,7},{7,6},{8,9},{9,8},{10,11... | collective-permute-start | bytes 393224 | tf_op jit(solution)/shard_map/ppermute | solution.py:284
  87.3 1.7 %collective-permute-start.4 = (bf16[8,32,256]{2,1,0:T(8,128)(2,1)S(1)}, bf16[8,32,256]{2,1,0:T(8,128)(2,1)S(1)}, u32[]{:S(2)}, u32[]{:S(2)}) collective-permute-start(bf16[8,32,256]{2,1,0:T(8,128)(2,1)S(1)} %all_to_all.45.dirs.two_own), channel_id=1, source_target_pairs={{0,1},{1,0},{2,3},{3,2},{4,5},{5,4},{6,7},{7,6},{8,9},{9,8},{10,11... | collective-permute-start | bytes 393224 | tf_op jit(solution)/shard_map/ppermute | solution.py:284

commit v7 on v6

--- a/solution.py
+++ b/solution.py
@@ -56,60 +56,71 @@
     return jnp.where(w > 0, 1.0 + w, 0.0).astype(BF16)
 
 
-def load_body(
-    users_in, items_in, count_in, vals_in, factors_in,
-    near, away, factors, users, items, count, vals, sems,
-):
-    batches = vals.shape[0] // BATCH
-    pairs = [(users_in, users), (items_in, items), (count_in, count)]
-    pairs += [(vals_in.at[pl.ds(k * BATCH, BATCH)], vals.at[pl.ds(k * BATCH, BATCH)]) for k in range(batches)]
-    pairs += [(factors_in, factors)]
+def place_rows(dense, vals, users, items, half, s):
+    user = users[s]
+    col = pl.ds(pl.multiple_of(items[s] * TILE, TILE), TILE)
+    for p in range(2):
+        row = pl.ds(pl.multiple_of((2 * user + p) * OWN, OWN), OWN)
+        dense[row, col] = vals[s, pl.ds(pl.multiple_of(half * OWN, OWN) + 2 * p * OWN, OWN), :]
+
+
+def place_batch(dense, vals, users, items, half, used, start, end):
+    @pl.when(used >= end)
+    def _():
+        for s in range(start, end):
+            place_rows(dense, vals, users, items, half, s)
+
+    @pl.when(used < end)
+    def _():
+        def put(s, carry):
+            place_rows(dense, vals, users, items, half, s)
+            return carry
+
+        lax.fori_loop(start, used, put, 0)
+
+
+def copies_of(pairs, sems):
     copies = [pltpu.make_async_copy(source, target, sems.at[k]) for k, (source, target) in enumerate(pairs)]
     for copy in copies:
         copy.start()
-    near[...] = jnp.zeros_like(near)
+    return copies
+
+
+def load_body(users_in, items_in, count_in, vals_in, away, vals, users, items, count, sems):
+    batches = vals.shape[0] // BATCH
+    copies = copies_of(
+        [(users_in, users), (items_in, items), (count_in, count)]
+        + [(vals_in.at[pl.ds(k * BATCH, BATCH)], vals.at[pl.ds(k * BATCH, BATCH)]) for k in range(batches)],
+        sems,
+    )
     away[...] = jnp.zeros_like(away)
     for copy in copies[:3]:
         copy.wait()
-    core = lax.axis_index("core")
-    mine = pl.multiple_of(core * OWN, OWN)
-    theirs = pl.multiple_of((1 - core) * OWN, OWN)
-    used = count[0, 0]
-
-    def put(s, carry):
-        user = users[s]
-        col = pl.ds(pl.multiple_of(items[s] * TILE, TILE), TILE)
-        for p in range(2):
-            row = pl.ds(pl.multiple_of((2 * user + p) * OWN, OWN), OWN)
-            near[row, col] = vals[s, pl.ds(mine + 2 * p * OWN, OWN), :]
-            away[row, col] = vals[s, pl.ds(theirs + 2 * p * OWN, OWN), :]
-        return carry
-
+    half = 1 - lax.axis_index("core")
     for k in range(batches):
         copies[3 + k].wait()
-        end = (k + 1) * BATCH
-
-        @pl.when(used >= end)
-        def _():
-            for s in range(k * BATCH, end):
-                put(s, 0)
-
-        @pl.when(used < end)
-        def _():
-            lax.fori_loop(k * BATCH, used, put, 0)
-
-    copies[-1].wait()
-
-
-def near_rhs_body(near, away, factors, conf_own, conf_other, sums):
+        place_batch(away, vals, users, items, half, count[0, 0], k * BATCH, (k + 1) * BATCH)
+
+
+def near_rhs_body(
+    users_in, items_in, count_in, factors, vals, away,
+    near, conf_own, conf_other, sums, users, items, count, sems,
+):
+    copies = copies_of([(users_in, users), (items_in, items), (count_in, count)], sems)
+    near[...] = jnp.zeros_like(near)
+    for j in range(0, ITEMS, CHUNK):
+        conf_other[:, j : j + CHUNK] = confidence_of(away[:, j : j + CHUNK])
+    for copy in copies:
+        copy.wait()
+    half = lax.axis_index("core")
+    for start in range(0, vals.shape[0], BATCH):
+        place_batch(near, vals, users, items, half, count[0, 0], start, start + BATCH)
     total = jnp.zeros((HALF, RANK), F32)
     for j in range(0, ITEMS, CHUNK):
         conf = confidence_of(near[:, j : j + CHUNK])
         conf_own[:, j : j + CHUNK] = conf
         total = total + jnp.dot(conf, factors[j : j + CHUNK, :], preferred_element_type=F32)
     sums[...] = total
-    for j in range(0, ITEMS, CHUNK):
-        conf_other[:, j : j + CHUNK] = confidence_of(away[:, j : j + CHUNK])
 
 
 def far_rhs_body(far, distant, sums, out):
@@ -288,27 +299,31 @@
 
 
 def local(item_factors, item_gram, tile_users, tile_items, tile_counts, tile_values):
-    half_tiles = shape((HALF, ITEMS), BF16)
     slots = tile_users.shape[2]
     distant = swap(item_factors)
-    near, away, factors = call(
+    ids = [pltpu.SMEM((slots,), jnp.int32), pltpu.SMEM((slots,), jnp.int32), pltpu.SMEM((1, 1), jnp.int32)]
+    tables = (tile_users[0, 0], tile_items[0, 0], tile_counts)
+    away, vals = call(
         load_body,
-        [pltpu.VMEM((HALF, ITEMS), BF16), pltpu.VMEM((HALF, ITEMS), BF16), pltpu.VMEM((ITEMS, RANK), BF16)],
-        [HBM] * 5,
+        [pltpu.VMEM((HALF, ITEMS), BF16), pltpu.VMEM((slots, TILE, TILE), BF16)],
+        [HBM] * 4,
+        ids + [pltpu.SemaphoreType.DMA((3 + slots // BATCH,))],
+        56,
+    )(*tables, tile_values[0, 0])
+    far = swap(away)
+    distant, vals = lax.optimization_barrier((distant, vals))
+    near, conf_own, conf_other, sums = call(
+        near_rhs_body,
         [
-            pltpu.SMEM((slots,), jnp.int32),
-            pltpu.SMEM((slots,), jnp.int32),
-            pltpu.SMEM((1, 1), jnp.int32),
-            pltpu.VMEM((slots, TILE, TILE), BF16),
-            pltpu.SemaphoreType.DMA((4 + slots // BATCH,)),
+            pltpu.VMEM((HALF, ITEMS), BF16),
+            pltpu.VMEM((HALF, ITEMS), BF16),
+            pltpu.VMEM((HALF, ITEMS), BF16),
+            pltpu.VMEM((HALF, RANK), F32),
         ],
-        54,
-    )(tile_users[0, 0], tile_items[0, 0], tile_counts, tile_values[0, 0], item_factors)
-    far = swap(away)
-    distant, near = lax.optimization_barrier((distant, near))
-    conf_own, conf_other, sums = call(
-        near_rhs_body, [half_tiles, half_tiles, shape((HALF, RANK), F32)], [VMEM] * 3
-    )(near, away, factors)
+        [HBM] * 3 + [VMEM] * 3,
+        ids + [pltpu.SemaphoreType.DMA((3,))],
+        16,
+    )(*tables, item_factors, vals, away)
     sums, far = lax.optimization_barrier((sums, far))
     (rhs_sums,) = call(
         far_rhs_body, [shape((N_Z, OWN, RANK), F32)], [VMEM] * 3
@@ -323,7 +338,7 @@
             apply_body,
             [shape((N_Z, OWN, RANK), IMAGE_SUM)],
             [VMEM] * 5,
-        )(dirs, near, far, factors, distant)
+        )(dirs, near, far, item_factors, distant)
         return exchange(image, "z")
 
     rhs, sent = call(first_body, [own, shape((N_Z, OWN, RANK), F32)], [VMEM])(
@@ -349,7 +364,7 @@
         [shape((N_ITEM, 8, TILE), F32)],
         [VMEM] * 10,
         [pltpu.VMEM((HALF, RANK), BF16), pltpu.VMEM((4, TILE, TILE), F32), message, message],
-    )(two_own, near, far, factors, distant, item_gram, dir_two, norm, step_one, step_two)
+    )(two_own, near, far, item_factors, distant, item_gram, dir_two, norm, step_one, step_two)
     zero_two, one_two = lax.optimization_barrier((zero_sent, one_own, two_own))[:2]
     sent, zero_other, one_other, two_other = lax.optimization_barrier(
         (sent, swap(zero_two).astype(F32), swap(one_two), swap(two_own))

time: 124 us -> 124 us (level)
  transfers between devices with their start and end apart: 5 -> 5, of which waited for: 1 -> 2; matrix products, arithmetic and copies ran while one was open for 0% -> 0% of each run, Pallas kernels for 3% -> 3%
where the time goes in v7:
time: 124 us; the launch traced here: 123 us
  blocking collectives  98.8 us (80%)
  starting transfers between devices  11.5 us (9%)
  Pallas kernels  10.3 us (8%)
  between operations  1.45 us (1%)
  waiting for transfers between devices  1.27 us (1%)
    all_to_all x8, blocking collectives, exchange(): return lax.all_to_all(value, axes, split_axis=0, concat_axis=0, tiled=True)  98.8 us
    ppermute x5, starting transfers between devices, swap(): return lax.ppermute(value, 'core', [(0, 1), (1, 0)])  11.5 us
    pallas_call x2, Pallas kernels, apply_tiles(): call(apply_body, [shape((N_Z, OWN, RANK), IMAGE_SUM)], [VMEM] * 5)  3.05 us
  transfers between devices with their start and end apart: 5, of which 2 were waited for; matrix products, arithmetic and copies ran while one was open for 0% of the time, Pallas kernels for 3%

profile of v7, /device:TPU:1, one launch (start us, length us, event | category | flops | bytes accessed | tf_op | source)
XLA Modules:
  0.0 123.4 jit_solution(17361549678961828857)
XLA Ops:
  0.6 0.0 copy-start
  0.6 0.0 copy-start.2
  0.7 0.0 copy-start.3
  0.7 3.3 %collective-permute-start = (bf16[2048,256]{1,0:T(8,128)(2,1)}, bf16[2048,256]{1,0:T(8,128)(2,1)S(1)}, u32[]{:S(2)}, u32[]{:S(2)}) collective-permute-start(bf16[2048,256]{1,0:T(8,128)(2,1)} %factors.7), channel_id=1, source_target_pairs={{0,1},{1,0},{2,3},{3,2},{4,5},{5,4},{6,7},{7,6},{8,9},{9,8},{10,11... | collective-permute-start | bytes 3145736 | tf_op jit(solution)/shard_map/ppermute | solution.py:295
  4.6 1.5 %shard_map.77 = (bf16[256,2048]{1,0:T(8,128)(2,1)S(1)}, bf16[48,128,128]{2,1,0:T(8,128)(2,1)S(1)}) custom-call(s32[48]{0:T(128)} %bitcast.3, s32[48]{0:T(128)} %bitcast.5, s32[1,1]{1,0:T(1,128)S(6)} %copy.8.count_in, bf16[48,128,128]{2,1,0:T(8,128)(2,1)} %bitcast.7), custom_call_target="tpu_custom_call" | custom-call | tf_op jit(solution)/shard_map/pallas_call | solution.py:306
  6.1 0.2 collective-permute-start.1
  6.3 0.1 collective-permute-done.distant
  6.5 1.3 %shard_map.78 = (bf16[256,2048]{1,0:T(8,128)(2,1)S(1)}, bf16[256,2048]{1,0:T(8,128)(2,1)S(1)}, bf16[256,2048]{1,0:T(8,128)(2,1)S(1)}, f32[256,256]{1,0:T(8,128)S(1)}) custom-call(s32[48]{0:T(128)S(1)} %bitcast.4, s32[48]{0:T(128)S(1)} %bitcast.6, s32[1,1]{1,0:T(1,128)S(6)} %copy.8.count_in, bf16[2048,256]{1,0:T(8,128)(2,1)S(1)} %copy-done, ...), custom_call_target="tpu_custom_call" | custom-call | tf_op jit(solution)/shard_map/pallas_call | solution.py:315
  7.8 1.1 collective-permute-done.1.far
  8.9 0.5 shard_map.79
  9.4 14.6 %all_to_all.40 = f16[8,32,256]{2,1,0:T(8,128)(2,1)S(1)} all-to-all(f16[8,32,256]{2,1,0:T(8,128)(2,1)S(1)} %convert_element_type.15), channel_id=1, replica_groups=mesh['x'=4,'y'=4,'z'=8,'core'=2] {'z'}, dimensions={0} | all-to-all | bytes 262144 | tf_op jit(solution)/shard_map/all_to_all | solution.py:291
  24.1 10.3 %all_to_all.41 = f16[8,32,256]{2,1,0:T(8,128)(2,1)S(1)} all-to-all(f16[8,32,256]{2,1,0:T(8,128)(2,1)S(1)} %convert_element_type.17), channel_id=1, replica_groups=mesh['x'=4,'y'=4,'z'=8,'core'=2] {'z'}, dimensions={0} | all-to-all | bytes 262144 | tf_op jit(solution)/shard_map/all_to_all | solution.py:291
  34.4 0.0 copy-start.1
  34.4 1.5 %shard_map.81 = bf16[8,32,256]{2,1,0:T(8,128)(2,1)S(1)} custom-call(f32[8,32,256]{2,1,0:T(8,128)S(1)} %convert_element_type.18.dirs.zero_own, bf16[256,2048]{1,0:T(8,128)(2,1)S(1)} %get-tuple-element.39.near, bf16[256,2048]{1,0:T(8,128)(2,1)S(1)} %collective-permute-done.1.far, bf16[2048,256]{1,0:T(8,128)(2,1)S(1)} %copy-done, ...), custom_call_target="tpu_custom_call" | custom-call | tf_op jit(solution)/shard_map/pallas_call | solution.py:337
  36.0 10.3 %all_to_all.42.arrived = bf16[8,32,256]{2,1,0:T(8,128)(2,1)S(1)} all-to-all(bf16[8,32,256]{2,1,0:T(8,128)(2,1)S(1)} %shard_map.81), channel_id=1, replica_groups=mesh['x'=4,'y'=4,'z'=8,'core'=2] {'z'}, dimensions={0} | all-to-all | bytes 262144 | tf_op jit(solution)/shard_map/all_to_all | solution.py:291
  46.3 0.4 shard_map.82
  46.7 10.3 %all_to_all.43.dirs.one_own = bf16[8,32,256]{2,1,0:T(8,128)(2,1)S(1)} all-to-all(bf16[8,32,256]{2,1,0:T(8,128)(2,1)S(1)} %get-tuple-element.41), channel_id=1, replica_groups=mesh['x'=4,'y'=4,'z'=8,'core'=2] {'z'}, dimensions={0} | all-to-all | bytes 262144 | tf_op jit(solution)/shard_map/all_to_all | solution.py:291
  57.0 1.5 %shard_map.83 = bf16[8,32,256]{2,1,0:T(8,128)(2,1)S(1)} custom-call(bf16[8,32,256]{2,1,0:T(8,128)(2,1)S(1)} %all_to_all.43.dirs.one_own, bf16[256,2048]{1,0:T(8,128)(2,1)S(1)} %get-tuple-element.39.near, bf16[256,2048]{1,0:T(8,128)(2,1)S(1)} %collective-permute-done.1.far, bf16[2048,256]{1,0:T(8,128)(2,1)S(1)} %copy-done, ...), custom_call_target="tpu_custom_call" | custom-call | tf_op jit(solution)/shard_map/pallas_call | solution.py:337
  58.5 10.3 %all_to_all.44.arrived = bf16[8,32,256]{2,1,0:T(8,128)(2,1)S(1)} all-to-all(bf16[8,32,256]{2,1,0:T(8,128)(2,1)S(1)} %shard_map.83), channel_id=1, replica_groups=mesh['x'=4,'y'=4,'z'=8,'core'=2] {'z'}, dimensions={0} | all-to-all | bytes 262144 | tf_op jit(solution)/shard_map/all_to_all | solution.py:291
  68.8 0.4 shard_map.84
  69.3 10.3 %all_to_all.45.dirs.two_own = bf16[8,32,256]{2,1,0:T(8,128)(2,1)S(1)} all-to-all(bf16[8,32,256]{2,1,0:T(8,128)(2,1)S(1)} %get-tuple-element.45), channel_id=1, replica_groups=mesh['x'=4,'y'=4,'z'=8,'core'=2] {'z'}, dimensions={0} | all-to-all | bytes 262144 | tf_op jit(solution)/shard_map/all_to_all | solution.py:291
  79.6 7.4 %collective-permute-start.2 = (f16[8,32,256]{2,1,0:T(8,128)(2,1)S(1)}, f16[8,32,256]{2,1,0:T(8,128)(2,1)S(1)}, u32[]{:S(2)}, u32[]{:S(2)}) collective-permute-start(f16[8,32,256]{2,1,0:T(8,128)(2,1)S(1)} %all_to_all.41), channel_id=1, source_target_pairs={{0,1},{1,0},{2,3},{3,2},{4,5},{5,4},{6,7},{7,6},{8,9},{9,8},{10,11... | collective-permute-start | bytes 393224 | tf_op jit(solution)/shard_map/ppermute | solution.py:295
  87.0 0.0 collective-permute-start.3
  87.0 0.5 collective-permute-start.4
  87.5 1.2 shard_map.85
  88.7 0.0 collective-permute-done.2
  88.8 0.0 collective-permute-done.3.one_other
  88.8 0.0 collective-permute-done.4.two_other
  88.8 10.3 %all_to_all.46.arrived = f32[16,8,128]{2,1,0:T(8,128)S(1)} all-to-all(f32[16,8,128]{2,1,0:T(8,128)S(1)} %shard_map.85), channel_id=1, replica_groups=mesh['x'=4,'y'=4,'z'=8,'core'=2] {'z','core'}, dimensions={0} | all-to-all | bytes 131072 | tf_op jit(solution)/shard_map/all_to_all | solution.py:291
  99.1 1.1 shard_map.86
  100.2 22.4 %all_to_all.47.arrived = bf16[16,256,128]{2,1,0:T(8,128)(2,1)S(1)} all-to-all(bf16[16,256,128]{2,1,0:T(8,128)(2,1)S(1)} %get-tuple-element.57), channel_id=1, replica_groups=mesh['x'=4,'y'=4,'z'=8,'core'=2] {'x','y'}, dimensions={0} | all-to-all | bytes 2097152 | tf_op jit(solution)/shard_map/all_to_all | solution.py:291
  122.6 0.9 shard_map.87
  (10 shorter events, 0.1 us)
Async XLA Ops:
  0.6 5.9 %copy-start = (bf16[2048,256]{1,0:T(8,128)(2,1)S(1)}, bf16[2048,256]{1,0:T(8,128)(2,1)}, u32[]{:S(2)}) copy-start(bf16[2048,256]{1,0:T(8,128)(2,1)} %factors.7) | copy-start | bytes 3145732
  0.6 5.9 %copy-start.2 = (s32[1,1,48]{2,1,0:T(1,128)S(1)}, s32[1,1,48]{2,1,0:T(1,128)}, u32[]{:S(2)}) copy-start(s32[1,1,48]{2,1,0:T(1,128)} %param.8) | copy-start | bytes 580
  0.7 5.8 %copy-start.3 = (s32[1,1,48]{2,1,0:T(1,128)S(1)}, s32[1,1,48]{2,1,0:T(1,128)}, u32[]{:S(2)}) copy-start(s32[1,1,48]{2,1,0:T(1,128)} %param.9) | copy-start | bytes 580
  0.7 5.8 %collective-permute-start = (bf16[2048,256]{1,0:T(8,128)(2,1)}, bf16[2048,256]{1,0:T(8,128)(2,1)S(1)}, u32[]{:S(2)}, u32[]{:S(2)}) collective-permute-start(bf16[2048,256]{1,0:T(8,128)(2,1)} %factors.7), channel_id=1, source_target_pairs={{0,1},{1,0},{2,3},{3,2},{4,5},{5,4},{6,7},{7,6},{8,9},{9,8},{10,11... | collective-permute-start | bytes 3145736 | tf_op jit(solution)/shard_map/ppermute | solution.py:295
  6.1 2.7 %collective-permute-start.1 = (bf16[256,2048]{1,0:T(8,128)(2,1)S(1)}, bf16[256,2048]{1,0:T(8,128)(2,1)S(1)}, u32[]{:S(2)}, u32[]{:S(2)}) collective-permute-start(bf16[256,2048]{1,0:T(8,128)(2,1)S(1)} %get-tuple-element.33.away), channel_id=1, source_target_pairs={{0,1},{1,0},{2,3},{3,2},{4,5},{5,4},{6,7},{7,6},{8,9},{9,8},{10,11... | collective-permute-start | bytes 3145736 | tf_op jit(solution)/shard_map/ppermute | solution.py:295
  34.4 11.9 %copy-start.1 = (f32[256,256]{1,0:T(8,128)S(1)}, f32[256,256]{1,0:T(8,128)}, u32[]{:S(2)}) copy-start(f32[256,256]{1,0:T(8,128)} %gram.5) | copy-start | bytes 786436
  79.6 9.1 %collective-permute-start.2 = (f16[8,32,256]{2,1,0:T(8,128)(2,1)S(1)}, f16[8,32,256]{2,1,0:T(8,128)(2,1)S(1)}, u32[]{:S(2)}, u32[]{:S(2)}) collective-permute-start(f16[8,32,256]{2,1,0:T(8,128)(2,1)S(1)} %all_to_all.41), channel_id=1, source_target_pairs={{0,1},{1,0},{2,3},{3,2},{4,5},{5,4},{6,7},{7,6},{8,9},{9,8},{10,11... | collective-permute-start | bytes 393224 | tf_op jit(solution)/shard_map/ppermute | solution.py:295
  87.0 1.8 %collective-permute-start.3 = (bf16[8,32,256]{2,1,0:T(8,128)(2,1)S(1)}, bf16[8,32,256]{2,1,0:T(8,128)(2,1)S(1)}, u32[]{:S(2)}, u32[]{:S(2)}) collective-permute-start(bf16[8,32,256]{2,1,0:T(8,128)(2,1)S(1)} %all_to_all.43.dirs.one_own), channel_id=1, source_target_pairs={{0,1},{1,0},{2,3},{3,2},{4,5},{5,4},{6,7},{7,6},{8,9},{9,8},{10,11... | collective-permute-start | bytes 393224 | tf_op jit(solution)/shard_map/ppermute | solution.py:295
  87.0 1.8 %collective-permute-start.4 = (bf16[8,32,256]{2,1,0:T(8,128)(2,1)S(1)}, bf16[8,32,256]{2,1,0:T(8,128)(2,1)S(1)}, u32[]{:S(2)}, u32[]{:S(2)}) collective-permute-start(bf16[8,32,256]{2,1,0:T(8,128)(2,1)S(1)} %all_to_all.45.dirs.two_own), channel_id=1, source_target_pairs={{0,1},{1,0},{2,3},{3,2},{4,5},{5,4},{6,7},{7,6},{8,9},{9,8},{10,11... | collective-permute-start | bytes 393224 | tf_op jit(solution)/shard_map/ppermute | solution.py:295

commit v8 on v7

--- a/solution.py
+++ b/solution.py
@@ -65,18 +65,19 @@
 
 
 def place_batch(dense, vals, users, items, half, used, start, end):
-    @pl.when(used >= end)
+    stop = jnp.minimum(used, end)
+    pairs = jnp.maximum(stop - start, 0) // 2
+
+    def put_pair(k, carry):
+        place_rows(dense, vals, users, items, half, start + 2 * k)
+        place_rows(dense, vals, users, items, half, start + 2 * k + 1)
+        return carry
+
+    lax.fori_loop(0, pairs, put_pair, 0)
+
+    @pl.when(start + 2 * pairs < stop)
     def _():
-        for s in range(start, end):
-            place_rows(dense, vals, users, items, half, s)
-
-    @pl.when(used < end)
-    def _():
-        def put(s, carry):
-            place_rows(dense, vals, users, items, half, s)
-            return carry
-
-        lax.fori_loop(start, used, put, 0)
+        place_rows(dense, vals, users, items, half, start + 2 * pairs)
 
 
 def copies_of(pairs, sems):

time: 124 us -> 124 us (level)
  transfers between devices with their start and end apart: 5 -> 5, of which waited for: 2 -> 2; matrix products, arithmetic and copies ran while one was open for 0% -> 0% of each run, Pallas kernels for 3% -> 4%
where the time goes in v8:
time: 124 us; the launch traced here: 123 us
  blocking collectives  98.7 us (80%)
  starting transfers between devices  11.3 us (9%)
  Pallas kernels  10.8 us (9%)
  between operations  1.46 us (1%)
    all_to_all x8, blocking collectives, exchange(): return lax.all_to_all(value, axes, split_axis=0, concat_axis=0, tiled=True)  98.7 us
    ppermute x5, starting transfers between devices, swap(): return lax.ppermute(value, 'core', [(0, 1), (1, 0)])  11.3 us
    pallas_call x2, Pallas kernels, apply_tiles(): call(apply_body, [shape((N_Z, OWN, RANK), IMAGE_SUM)], [VMEM] * 5)  3.05 us
  transfers between devices with their start and end apart: 5, of which 2 were waited for; matrix products, arithmetic and copies ran while one was open for 0% of the time, Pallas kernels for 4%

profile of v8, /device:TPU:1, one launch (start us, length us, event | category | flops | bytes accessed | tf_op | source)
XLA Modules:
  0.0 123.4 jit_solution(18265122428912026020)
XLA Ops:
  0.6 0.0 copy-start
  0.6 0.0 copy-start.2
  0.7 0.0 copy-start.3
  0.7 3.3 %collective-permute-start = (bf16[2048,256]{1,0:T(8,128)(2,1)}, bf16[2048,256]{1,0:T(8,128)(2,1)S(1)}, u32[]{:S(2)}, u32[]{:S(2)}) collective-permute-start(bf16[2048,256]{1,0:T(8,128)(2,1)} %factors.7), channel_id=1, source_target_pairs={{0,1},{1,0},{2,3},{3,2},{4,5},{5,4},{6,7},{7,6},{8,9},{9,8},{10,11... | collective-permute-start | bytes 3145736 | tf_op jit(solution)/shard_map/ppermute | solution.py:296
  4.6 1.6 %shard_map.77 = (bf16[256,2048]{1,0:T(8,128)(2,1)S(1)}, bf16[48,128,128]{2,1,0:T(8,128)(2,1)S(1)}) custom-call(s32[48]{0:T(128)} %bitcast.3, s32[48]{0:T(128)} %bitcast.5, s32[1,1]{1,0:T(1,128)S(6)} %copy.8.count_in, bf16[48,128,128]{2,1,0:T(8,128)(2,1)} %bitcast.7), custom_call_target="tpu_custom_call" | custom-call | tf_op jit(solution)/shard_map/pallas_call | solution.py:307
  6.2 0.1 collective-permute-start.1
  6.3 0.2 collective-permute-done.distant
  6.5 1.6 %shard_map.78 = (bf16[256,2048]{1,0:T(8,128)(2,1)S(1)}, bf16[256,2048]{1,0:T(8,128)(2,1)S(1)}, bf16[256,2048]{1,0:T(8,128)(2,1)S(1)}, f32[256,256]{1,0:T(8,128)S(1)}) custom-call(s32[48]{0:T(128)S(1)} %bitcast.4, s32[48]{0:T(128)S(1)} %bitcast.6, s32[1,1]{1,0:T(1,128)S(6)} %copy.8.count_in, bf16[2048,256]{1,0:T(8,128)(2,1)S(1)} %copy-done, ...), custom_call_target="tpu_custom_call" | custom-call | tf_op jit(solution)/shard_map/pallas_call | solution.py:316
  8.1 0.8 collective-permute-done.1.far
  9.0 0.5 shard_map.79
  9.5 14.6 %all_to_all.40 = f16[8,32,256]{2,1,0:T(8,128)(2,1)S(1)} all-to-all(f16[8,32,256]{2,1,0:T(8,128)(2,1)S(1)} %convert_element_type.15), channel_id=1, replica_groups=mesh['x'=4,'y'=4,'z'=8,'core'=2] {'z'}, dimensions={0} | all-to-all | bytes 262144 | tf_op jit(solution)/shard_map/all_to_all | solution.py:292
  24.2 10.3 %all_to_all.41 = f16[8,32,256]{2,1,0:T(8,128)(2,1)S(1)} all-to-all(f16[8,32,256]{2,1,0:T(8,128)(2,1)S(1)} %convert_element_type.17), channel_id=1, replica_groups=mesh['x'=4,'y'=4,'z'=8,'core'=2] {'z'}, dimensions={0} | all-to-all | bytes 262144 | tf_op jit(solution)/shard_map/all_to_all | solution.py:292
  34.5 0.0 copy-start.1
  34.5 1.5 %shard_map.81 = bf16[8,32,256]{2,1,0:T(8,128)(2,1)S(1)} custom-call(f32[8,32,256]{2,1,0:T(8,128)S(1)} %convert_element_type.18.dirs.zero_own, bf16[256,2048]{1,0:T(8,128)(2,1)S(1)} %get-tuple-element.39.near, bf16[256,2048]{1,0:T(8,128)(2,1)S(1)} %collective-permute-done.1.far, bf16[2048,256]{1,0:T(8,128)(2,1)S(1)} %copy-done, ...), custom_call_target="tpu_custom_call" | custom-call | tf_op jit(solution)/shard_map/pallas_call | solution.py:338
  36.1 10.3 %all_to_all.42.arrived = bf16[8,32,256]{2,1,0:T(8,128)(2,1)S(1)} all-to-all(bf16[8,32,256]{2,1,0:T(8,128)(2,1)S(1)} %shard_map.81), channel_id=1, replica_groups=mesh['x'=4,'y'=4,'z'=8,'core'=2] {'z'}, dimensions={0} | all-to-all | bytes 262144 | tf_op jit(solution)/shard_map/all_to_all | solution.py:292
  46.4 0.4 shard_map.82
  46.8 10.3 %all_to_all.43.dirs.one_own = bf16[8,32,256]{2,1,0:T(8,128)(2,1)S(1)} all-to-all(bf16[8,32,256]{2,1,0:T(8,128)(2,1)S(1)} %get-tuple-element.41), channel_id=1, replica_groups=mesh['x'=4,'y'=4,'z'=8,'core'=2] {'z'}, dimensions={0} | all-to-all | bytes 262144 | tf_op jit(solution)/shard_map/all_to_all | solution.py:292
  57.1 1.5 %shard_map.83 = bf16[8,32,256]{2,1,0:T(8,128)(2,1)S(1)} custom-call(bf16[8,32,256]{2,1,0:T(8,128)(2,1)S(1)} %all_to_all.43.dirs.one_own, bf16[256,2048]{1,0:T(8,128)(2,1)S(1)} %get-tuple-element.39.near, bf16[256,2048]{1,0:T(8,128)(2,1)S(1)} %collective-permute-done.1.far, bf16[2048,256]{1,0:T(8,128)(2,1)S(1)} %copy-done, ...), custom_call_target="tpu_custom_call" | custom-call | tf_op jit(solution)/shard_map/pallas_call | solution.py:338
  58.6 10.3 %all_to_all.44.arrived = bf16[8,32,256]{2,1,0:T(8,128)(2,1)S(1)} all-to-all(bf16[8,32,256]{2,1,0:T(8,128)(2,1)S(1)} %shard_map.83), channel_id=1, replica_groups=mesh['x'=4,'y'=4,'z'=8,'core'=2] {'z'}, dimensions={0} | all-to-all | bytes 262144 | tf_op jit(solution)/shard_map/all_to_all | solution.py:292
  68.9 0.4 shard_map.84
  69.4 10.3 %all_to_all.45.dirs.two_own = bf16[8,32,256]{2,1,0:T(8,128)(2,1)S(1)} all-to-all(bf16[8,32,256]{2,1,0:T(8,128)(2,1)S(1)} %get-tuple-element.45), channel_id=1, replica_groups=mesh['x'=4,'y'=4,'z'=8,'core'=2] {'z'}, dimensions={0} | all-to-all | bytes 262144 | tf_op jit(solution)/shard_map/all_to_all | solution.py:292
  79.7 7.4 %collective-permute-start.2 = (f16[8,32,256]{2,1,0:T(8,128)(2,1)S(1)}, f16[8,32,256]{2,1,0:T(8,128)(2,1)S(1)}, u32[]{:S(2)}, u32[]{:S(2)}) collective-permute-start(f16[8,32,256]{2,1,0:T(8,128)(2,1)S(1)} %all_to_all.41), channel_id=1, source_target_pairs={{0,1},{1,0},{2,3},{3,2},{4,5},{5,4},{6,7},{7,6},{8,9},{9,8},{10,11... | collective-permute-start | bytes 393224 | tf_op jit(solution)/shard_map/ppermute | solution.py:296
  87.1 0.0 collective-permute-start.3
  87.1 0.5 collective-permute-start.4
  87.6 1.2 shard_map.85
  88.8 0.0 collective-permute-done.2
  88.9 0.0 collective-permute-done.3.one_other
  88.9 0.0 collective-permute-done.4.two_other
  88.9 10.3 %all_to_all.46.arrived = f32[16,8,128]{2,1,0:T(8,128)S(1)} all-to-all(f32[16,8,128]{2,1,0:T(8,128)S(1)} %shard_map.85), channel_id=1, replica_groups=mesh['x'=4,'y'=4,'z'=8,'core'=2] {'z','core'}, dimensions={0} | all-to-all | bytes 131072 | tf_op jit(solution)/shard_map/all_to_all | solution.py:292
  99.2 1.1 shard_map.86
  100.3 22.3 %all_to_all.47.arrived = bf16[16,256,128]{2,1,0:T(8,128)(2,1)S(1)} all-to-all(bf16[16,256,128]{2,1,0:T(8,128)(2,1)S(1)} %get-tuple-element.57), channel_id=1, replica_groups=mesh['x'=4,'y'=4,'z'=8,'core'=2] {'x','y'}, dimensions={0} | all-to-all | bytes 2097152 | tf_op jit(solution)/shard_map/all_to_all | solution.py:292
  122.6 0.9 shard_map.87
  (10 shorter events, 0.1 us)
Async XLA Ops:
  0.6 5.9 %copy-start = (bf16[2048,256]{1,0:T(8,128)(2,1)S(1)}, bf16[2048,256]{1,0:T(8,128)(2,1)}, u32[]{:S(2)}) copy-start(bf16[2048,256]{1,0:T(8,128)(2,1)} %factors.7) | copy-start | bytes 3145732
  0.6 5.9 %copy-start.2 = (s32[1,1,48]{2,1,0:T(1,128)S(1)}, s32[1,1,48]{2,1,0:T(1,128)}, u32[]{:S(2)}) copy-start(s32[1,1,48]{2,1,0:T(1,128)} %param.8) | copy-start | bytes 580
  0.7 5.8 %copy-start.3 = (s32[1,1,48]{2,1,0:T(1,128)S(1)}, s32[1,1,48]{2,1,0:T(1,128)}, u32[]{:S(2)}) copy-start(s32[1,1,48]{2,1,0:T(1,128)} %param.9) | copy-start | bytes 580
  0.7 5.8 %collective-permute-start = (bf16[2048,256]{1,0:T(8,128)(2,1)}, bf16[2048,256]{1,0:T(8,128)(2,1)S(1)}, u32[]{:S(2)}, u32[]{:S(2)}) collective-permute-start(bf16[2048,256]{1,0:T(8,128)(2,1)} %factors.7), channel_id=1, source_target_pairs={{0,1},{1,0},{2,3},{3,2},{4,5},{5,4},{6,7},{7,6},{8,9},{9,8},{10,11... | collective-permute-start | bytes 3145736 | tf_op jit(solution)/shard_map/ppermute | solution.py:296
  6.2 2.7 %collective-permute-start.1 = (bf16[256,2048]{1,0:T(8,128)(2,1)S(1)}, bf16[256,2048]{1,0:T(8,128)(2,1)S(1)}, u32[]{:S(2)}, u32[]{:S(2)}) collective-permute-start(bf16[256,2048]{1,0:T(8,128)(2,1)S(1)} %get-tuple-element.33.away), channel_id=1, source_target_pairs={{0,1},{1,0},{2,3},{3,2},{4,5},{5,4},{6,7},{7,6},{8,9},{9,8},{10,11... | collective-permute-start | bytes 3145736 | tf_op jit(solution)/shard_map/ppermute | solution.py:296
  34.5 11.9 %copy-start.1 = (f32[256,256]{1,0:T(8,128)S(1)}, f32[256,256]{1,0:T(8,128)}, u32[]{:S(2)}) copy-start(f32[256,256]{1,0:T(8,128)} %gram.5) | copy-start | bytes 786436
  79.7 9.1 %collective-permute-start.2 = (f16[8,32,256]{2,1,0:T(8,128)(2,1)S(1)}, f16[8,32,256]{2,1,0:T(8,128)(2,1)S(1)}, u32[]{:S(2)}, u32[]{:S(2)}) collective-permute-start(f16[8,32,256]{2,1,0:T(8,128)(2,1)S(1)} %all_to_all.41), channel_id=1, source_target_pairs={{0,1},{1,0},{2,3},{3,2},{4,5},{5,4},{6,7},{7,6},{8,9},{9,8},{10,11... | collective-permute-start | bytes 393224 | tf_op jit(solution)/shard_map/ppermute | solution.py:296
  87.1 1.8 %collective-permute-start.3 = (bf16[8,32,256]{2,1,0:T(8,128)(2,1)S(1)}, bf16[8,32,256]{2,1,0:T(8,128)(2,1)S(1)}, u32[]{:S(2)}, u32[]{:S(2)}) collective-permute-start(bf16[8,32,256]{2,1,0:T(8,128)(2,1)S(1)} %all_to_all.43.dirs.one_own), channel_id=1, source_target_pairs={{0,1},{1,0},{2,3},{3,2},{4,5},{5,4},{6,7},{7,6},{8,9},{9,8},{10,11... | collective-permute-start | bytes 393224 | tf_op jit(solution)/shard_map/ppermute | solution.py:296
  87.1 1.8 %collective-permute-start.4 = (bf16[8,32,256]{2,1,0:T(8,128)(2,1)S(1)}, bf16[8,32,256]{2,1,0:T(8,128)(2,1)S(1)}, u32[]{:S(2)}, u32[]{:S(2)}) collective-permute-start(bf16[8,32,256]{2,1,0:T(8,128)(2,1)S(1)} %all_to_all.45.dirs.two_own), channel_id=1, source_target_pairs={{0,1},{1,0},{2,3},{3,2},{4,5},{5,4},{6,7},{7,6},{8,9},{9,8},{10,11... | collective-permute-start | bytes 393224 | tf_op jit(solution)/shard_map/ppermute | solution.py:296

commit v9 on v8

--- a/solution.py
+++ b/solution.py
@@ -270,7 +270,7 @@
                 )
     mine = core * HALF + lax.axis_index("z") * OWN
     own_step[...] = alphas[2, pl.ds(pl.multiple_of(mine, OWN), OWN), :]
-    turned = rows[...].T.astype(BF16)
+    turned = rows[...].astype(BF16).T
     for j in range(0, ITEMS, CHUNK):
         block = jnp.dot(
             turned[:, :HALF], conf_own[:, j : j + CHUNK], preferred_element_type=F32

time: 124 us -> 124 us (level)
  no operation moved by 1% of the time
where the time goes in v9:
time: 124 us; the launch traced here: 123 us
  blocking collectives  98.7 us (80%)
  starting transfers between devices  11.4 us (9%)
  Pallas kernels  10.8 us (9%)
  between operations  1.46 us (1%)
    all_to_all x8, blocking collectives, exchange(): return lax.all_to_all(value, axes, split_axis=0, concat_axis=0, tiled=True)  98.7 us
    ppermute x5, starting transfers between devices, swap(): return lax.ppermute(value, 'core', [(0, 1), (1, 0)])  11.4 us
    pallas_call x2, Pallas kernels, apply_tiles(): call(apply_body, [shape((N_Z, OWN, RANK), IMAGE_SUM)], [VMEM] * 5)  3.05 us
  transfers between devices with their start and end apart: 5, of which 2 were waited for; matrix products, arithmetic and copies ran while one was open for 0% of the time, Pallas kernels for 4%

profile of v9, /device:TPU:1, one launch (start us, length us, event | category | flops | bytes accessed | tf_op | source)
XLA Modules:
  0.0 123.4 jit_solution(11524471969923545488)
XLA Ops:
  0.6 0.0 copy-start
  0.6 0.0 copy-start.2
  0.7 0.0 copy-start.3
  0.7 3.3 %collective-permute-start = (bf16[2048,256]{1,0:T(8,128)(2,1)}, bf16[2048,256]{1,0:T(8,128)(2,1)S(1)}, u32[]{:S(2)}, u32[]{:S(2)}) collective-permute-start(bf16[2048,256]{1,0:T(8,128)(2,1)} %factors.7), channel_id=1, source_target_pairs={{0,1},{1,0},{2,3},{3,2},{4,5},{5,4},{6,7},{7,6},{8,9},{9,8},{10,11... | collective-permute-start | bytes 3145736 | tf_op jit(solution)/shard_map/ppermute | solution.py:296
  4.6 1.6 %shard_map.77 = (bf16[256,2048]{1,0:T(8,128)(2,1)S(1)}, bf16[48,128,128]{2,1,0:T(8,128)(2,1)S(1)}) custom-call(s32[48]{0:T(128)} %bitcast.3, s32[48]{0:T(128)} %bitcast.5, s32[1,1]{1,0:T(1,128)S(6)} %copy.8.count_in, bf16[48,128,128]{2,1,0:T(8,128)(2,1)} %bitcast.7), custom_call_target="tpu_custom_call" | custom-call | tf_op jit(solution)/shard_map/pallas_call | solution.py:307
  6.2 0.1 collective-permute-start.1
  6.3 0.2 collective-permute-done.distant
  6.5 1.6 %shard_map.78 = (bf16[256,2048]{1,0:T(8,128)(2,1)S(1)}, bf16[256,2048]{1,0:T(8,128)(2,1)S(1)}, bf16[256,2048]{1,0:T(8,128)(2,1)S(1)}, f32[256,256]{1,0:T(8,128)S(1)}) custom-call(s32[48]{0:T(128)S(1)} %bitcast.4, s32[48]{0:T(128)S(1)} %bitcast.6, s32[1,1]{1,0:T(1,128)S(6)} %copy.8.count_in, bf16[2048,256]{1,0:T(8,128)(2,1)S(1)} %copy-done, ...), custom_call_target="tpu_custom_call" | custom-call | tf_op jit(solution)/shard_map/pallas_call | solution.py:316
  8.1 0.8 collective-permute-done.1.far
  9.0 0.5 shard_map.79
  9.5 14.5 %all_to_all.40 = f16[8,32,256]{2,1,0:T(8,128)(2,1)S(1)} all-to-all(f16[8,32,256]{2,1,0:T(8,128)(2,1)S(1)} %convert_element_type.15), channel_id=1, replica_groups=mesh['x'=4,'y'=4,'z'=8,'core'=2] {'z'}, dimensions={0} | all-to-all | bytes 262144 | tf_op jit(solution)/shard_map/all_to_all | solution.py:292
  24.1 10.3 %all_to_all.41 = f16[8,32,256]{2,1,0:T(8,128)(2,1)S(1)} all-to-all(f16[8,32,256]{2,1,0:T(8,128)(2,1)S(1)} %convert_element_type.17), channel_id=1, replica_groups=mesh['x'=4,'y'=4,'z'=8,'core'=2] {'z'}, dimensions={0} | all-to-all | bytes 262144 | tf_op jit(solution)/shard_map/all_to_all | solution.py:292
  34.4 0.0 copy-start.1
  34.4 1.5 %shard_map.81 = bf16[8,32,256]{2,1,0:T(8,128)(2,1)S(1)} custom-call(f32[8,32,256]{2,1,0:T(8,128)S(1)} %convert_element_type.18.dirs.zero_own, bf16[256,2048]{1,0:T(8,128)(2,1)S(1)} %get-tuple-element.39.near, bf16[256,2048]{1,0:T(8,128)(2,1)S(1)} %collective-permute-done.1.far, bf16[2048,256]{1,0:T(8,128)(2,1)S(1)} %copy-done, ...), custom_call_target="tpu_custom_call" | custom-call | tf_op jit(solution)/shard_map/pallas_call | solution.py:338
  36.0 10.3 %all_to_all.42.arrived = bf16[8,32,256]{2,1,0:T(8,128)(2,1)S(1)} all-to-all(bf16[8,32,256]{2,1,0:T(8,128)(2,1)S(1)} %shard_map.81), channel_id=1, replica_groups=mesh['x'=4,'y'=4,'z'=8,'core'=2] {'z'}, dimensions={0} | all-to-all | bytes 262144 | tf_op jit(solution)/shard_map/all_to_all | solution.py:292
  46.3 0.4 shard_map.82
  46.7 10.3 %all_to_all.43.dirs.one_own = bf16[8,32,256]{2,1,0:T(8,128)(2,1)S(1)} all-to-all(bf16[8,32,256]{2,1,0:T(8,128)(2,1)S(1)} %get-tuple-element.41), channel_id=1, replica_groups=mesh['x'=4,'y'=4,'z'=8,'core'=2] {'z'}, dimensions={0} | all-to-all | bytes 262144 | tf_op jit(solution)/shard_map/all_to_all | solution.py:292
  57.0 1.5 %shard_map.83 = bf16[8,32,256]{2,1,0:T(8,128)(2,1)S(1)} custom-call(bf16[8,32,256]{2,1,0:T(8,128)(2,1)S(1)} %all_to_all.43.dirs.one_own, bf16[256,2048]{1,0:T(8,128)(2,1)S(1)} %get-tuple-element.39.near, bf16[256,2048]{1,0:T(8,128)(2,1)S(1)} %collective-permute-done.1.far, bf16[2048,256]{1,0:T(8,128)(2,1)S(1)} %copy-done, ...), custom_call_target="tpu_custom_call" | custom-call | tf_op jit(solution)/shard_map/pallas_call | solution.py:338
  58.5 10.3 %all_to_all.44.arrived = bf16[8,32,256]{2,1,0:T(8,128)(2,1)S(1)} all-to-all(bf16[8,32,256]{2,1,0:T(8,128)(2,1)S(1)} %shard_map.83), channel_id=1, replica_groups=mesh['x'=4,'y'=4,'z'=8,'core'=2] {'z'}, dimensions={0} | all-to-all | bytes 262144 | tf_op jit(solution)/shard_map/all_to_all | solution.py:292
  68.8 0.4 shard_map.84
  69.3 10.3 %all_to_all.45.dirs.two_own = bf16[8,32,256]{2,1,0:T(8,128)(2,1)S(1)} all-to-all(bf16[8,32,256]{2,1,0:T(8,128)(2,1)S(1)} %get-tuple-element.45), channel_id=1, replica_groups=mesh['x'=4,'y'=4,'z'=8,'core'=2] {'z'}, dimensions={0} | all-to-all | bytes 262144 | tf_op jit(solution)/shard_map/all_to_all | solution.py:292
  79.6 7.4 %collective-permute-start.2 = (f16[8,32,256]{2,1,0:T(8,128)(2,1)S(1)}, f16[8,32,256]{2,1,0:T(8,128)(2,1)S(1)}, u32[]{:S(2)}, u32[]{:S(2)}) collective-permute-start(f16[8,32,256]{2,1,0:T(8,128)(2,1)S(1)} %all_to_all.41), channel_id=1, source_target_pairs={{0,1},{1,0},{2,3},{3,2},{4,5},{5,4},{6,7},{7,6},{8,9},{9,8},{10,11... | collective-permute-start | bytes 393224 | tf_op jit(solution)/shard_map/ppermute | solution.py:296
  87.0 0.0 collective-permute-start.3
  87.0 0.5 collective-permute-start.4
  87.5 1.2 shard_map.85
  88.7 0.0 collective-permute-done.2
  88.8 0.0 collective-permute-done.3.one_other
  88.8 0.0 collective-permute-done.4.two_other
  88.8 10.3 %all_to_all.46.arrived = f32[16,8,128]{2,1,0:T(8,128)S(1)} all-to-all(f32[16,8,128]{2,1,0:T(8,128)S(1)} %shard_map.85), channel_id=1, replica_groups=mesh['x'=4,'y'=4,'z'=8,'core'=2] {'z','core'}, dimensions={0} | all-to-all | bytes 131072 | tf_op jit(solution)/shard_map/all_to_all | solution.py:292
  99.1 1.1 shard_map.86
  100.2 22.4 %all_to_all.47.arrived = bf16[16,256,128]{2,1,0:T(8,128)(2,1)S(1)} all-to-all(bf16[16,256,128]{2,1,0:T(8,128)(2,1)S(1)} %get-tuple-element.57), channel_id=1, replica_groups=mesh['x'=4,'y'=4,'z'=8,'core'=2] {'x','y'}, dimensions={0} | all-to-all | bytes 2097152 | tf_op jit(solution)/shard_map/all_to_all | solution.py:292
  122.5 0.9 shard_map.87
  (10 shorter events, 0.1 us)
Async XLA Ops:
  0.6 5.9 %copy-start = (bf16[2048,256]{1,0:T(8,128)(2,1)S(1)}, bf16[2048,256]{1,0:T(8,128)(2,1)}, u32[]{:S(2)}) copy-start(bf16[2048,256]{1,0:T(8,128)(2,1)} %factors.7) | copy-start | bytes 3145732
  0.6 5.9 %copy-start.2 = (s32[1,1,48]{2,1,0:T(1,128)S(1)}, s32[1,1,48]{2,1,0:T(1,128)}, u32[]{:S(2)}) copy-start(s32[1,1,48]{2,1,0:T(1,128)} %param.8) | copy-start | bytes 580
  0.7 5.8 %copy-start.3 = (s32[1,1,48]{2,1,0:T(1,128)S(1)}, s32[1,1,48]{2,1,0:T(1,128)}, u32[]{:S(2)}) copy-start(s32[1,1,48]{2,1,0:T(1,128)} %param.9) | copy-start | bytes 580
  0.7 5.8 %collective-permute-start = (bf16[2048,256]{1,0:T(8,128)(2,1)}, bf16[2048,256]{1,0:T(8,128)(2,1)S(1)}, u32[]{:S(2)}, u32[]{:S(2)}) collective-permute-start(bf16[2048,256]{1,0:T(8,128)(2,1)} %factors.7), channel_id=1, source_target_pairs={{0,1},{1,0},{2,3},{3,2},{4,5},{5,4},{6,7},{7,6},{8,9},{9,8},{10,11... | collective-permute-start | bytes 3145736 | tf_op jit(solution)/shard_map/ppermute | solution.py:296
  6.2 2.7 %collective-permute-start.1 = (bf16[256,2048]{1,0:T(8,128)(2,1)S(1)}, bf16[256,2048]{1,0:T(8,128)(2,1)S(1)}, u32[]{:S(2)}, u32[]{:S(2)}) collective-permute-start(bf16[256,2048]{1,0:T(8,128)(2,1)S(1)} %get-tuple-element.33.away), channel_id=1, source_target_pairs={{0,1},{1,0},{2,3},{3,2},{4,5},{5,4},{6,7},{7,6},{8,9},{9,8},{10,11... | collective-permute-start | bytes 3145736 | tf_op jit(solution)/shard_map/ppermute | solution.py:296
  34.4 11.9 %copy-start.1 = (f32[256,256]{1,0:T(8,128)S(1)}, f32[256,256]{1,0:T(8,128)}, u32[]{:S(2)}) copy-start(f32[256,256]{1,0:T(8,128)} %gram.5) | copy-start | bytes 786436
  79.6 9.2 %collective-permute-start.2 = (f16[8,32,256]{2,1,0:T(8,128)(2,1)S(1)}, f16[8,32,256]{2,1,0:T(8,128)(2,1)S(1)}, u32[]{:S(2)}, u32[]{:S(2)}) collective-permute-start(f16[8,32,256]{2,1,0:T(8,128)(2,1)S(1)} %all_to_all.41), channel_id=1, source_target_pairs={{0,1},{1,0},{2,3},{3,2},{4,5},{5,4},{6,7},{7,6},{8,9},{9,8},{10,11... | collective-permute-start | bytes 393224 | tf_op jit(solution)/shard_map/ppermute | solution.py:296
  87.0 1.8 %collective-permute-start.3 = (bf16[8,32,256]{2,1,0:T(8,128)(2,1)S(1)}, bf16[8,32,256]{2,1,0:T(8,128)(2,1)S(1)}, u32[]{:S(2)}, u32[]{:S(2)}) collective-permute-start(bf16[8,32,256]{2,1,0:T(8,128)(2,1)S(1)} %all_to_all.43.dirs.one_own), channel_id=1, source_target_pairs={{0,1},{1,0},{2,3},{3,2},{4,5},{5,4},{6,7},{7,6},{8,9},{9,8},{10,11... | collective-permute-start | bytes 393224 | tf_op jit(solution)/shard_map/ppermute | solution.py:296
  87.0 1.8 %collective-permute-start.4 = (bf16[8,32,256]{2,1,0:T(8,128)(2,1)S(1)}, bf16[8,32,256]{2,1,0:T(8,128)(2,1)S(1)}, u32[]{:S(2)}, u32[]{:S(2)}) collective-permute-start(bf16[8,32,256]{2,1,0:T(8,128)(2,1)S(1)} %all_to_all.45.dirs.two_own), channel_id=1, source_target_pairs={{0,1},{1,0},{2,3},{3,2},{4,5},{5,4},{6,7},{7,6},{8,9},{9,8},{10,11... | collective-permute-start | bytes 393224 | tf_op jit(solution)/shard_map/ppermute | solution.py:296

commit v10 on v8

--- a/solution.py
+++ b/solution.py
@@ -18,7 +18,7 @@
 HALF = 256
 ITEMS = 2048
 CHUNK = 256
-BATCH = 12
+BATCH = 24
 RHS_SCALE = 8.0
 
 HIGHEST = lax.Precision.HIGHEST

time: 124 us -> 124 us (level)
  transfers between devices with their start and end apart: 5 -> 5, of which waited for: 2 -> 2; matrix products, arithmetic and copies ran while one was open for 0% -> 0% of each run, Pallas kernels for 4% -> 3%
where the time goes in v10:
time: 124 us
  blocking collectives  99 us (80%)
  starting transfers between devices  11.4 us (9%)
  Pallas kernels  10.5 us (8%)
  between operations  1.45 us (1%)
    all_to_all x8, blocking collectives, exchange(): return lax.all_to_all(value, axes, split_axis=0, concat_axis=0, tiled=True)  99 us
    ppermute x5, starting transfers between devices, swap(): return lax.ppermute(value, 'core', [(0, 1), (1, 0)])  11.4 us
    pallas_call x2, Pallas kernels, apply_tiles(): call(apply_body, [shape((N_Z, OWN, RANK), IMAGE_SUM)], [VMEM] * 5)  3.05 us
  transfers between devices with their start and end apart: 5, of which 2 were waited for; matrix products, arithmetic and copies ran while one was open for 0% of the time, Pallas kernels for 3%

profile of v10, /device:TPU:1, one launch (start us, length us, event | category | flops | bytes accessed | tf_op | source)
XLA Modules:
  0.0 123.6 jit_solution(9661167353135155798)
XLA Ops:
  0.6 0.0 copy-start
  0.7 3.3 %collective-permute-start = (bf16[2048,256]{1,0:T(8,128)(2,1)}, bf16[2048,256]{1,0:T(8,128)(2,1)S(1)}, u32[]{:S(2)}, u32[]{:S(2)}) collective-permute-start(bf16[2048,256]{1,0:T(8,128)(2,1)} %factors.7), channel_id=1, source_target_pairs={{0,1},{1,0},{2,3},{3,2},{4,5},{5,4},{6,7},{7,6},{8,9},{9,8},{10,11... | collective-permute-start | bytes 3145736 | tf_op jit(solution)/shard_map/ppermute | solution.py:296
  4.6 1.5 %shard_map.77 = (bf16[256,2048]{1,0:T(8,128)(2,1)S(1)}, bf16[48,128,128]{2,1,0:T(8,128)(2,1)S(1)}) custom-call(s32[48]{0:T(128)} %bitcast.3, s32[48]{0:T(128)} %bitcast.5, s32[1,1]{1,0:T(1,128)S(6)} %copy.8.count_in, bf16[48,128,128]{2,1,0:T(8,128)(2,1)} %bitcast.7), custom_call_target="tpu_custom_call" | custom-call | tf_op jit(solution)/shard_map/pallas_call | solution.py:307
  6.1 0.2 collective-permute-start.1
  6.3 0.2 collective-permute-done.distant
  6.5 0.0 copy-done.3
  6.5 1.4 %shard_map.78 = (bf16[256,2048]{1,0:T(8,128)(2,1)S(1)}, bf16[256,2048]{1,0:T(8,128)(2,1)S(1)}, bf16[256,2048]{1,0:T(8,128)(2,1)S(1)}, f32[256,256]{1,0:T(8,128)S(1)}) custom-call(s32[48]{0:T(128)S(1)} %bitcast.4, s32[48]{0:T(128)S(1)} %bitcast.6, s32[1,1]{1,0:T(1,128)S(6)} %copy.8.count_in, bf16[2048,256]{1,0:T(8,128)(2,1)S(1)} %copy-done, ...), custom_call_target="tpu_custom_call" | custom-call | tf_op jit(solution)/shard_map/pallas_call | solution.py:316
  7.9 1.0 collective-permute-done.1.far
  8.9 0.5 shard_map.79
  9.4 14.6 %all_to_all.40 = f16[8,32,256]{2,1,0:T(8,128)(2,1)S(1)} all-to-all(f16[8,32,256]{2,1,0:T(8,128)(2,1)S(1)} %convert_element_type.15), channel_id=1, replica_groups=mesh['x'=4,'y'=4,'z'=8,'core'=2] {'z'}, dimensions={0} | all-to-all | bytes 262144 | tf_op jit(solution)/shard_map/all_to_all | solution.py:292
  24.1 10.3 %all_to_all.41 = f16[8,32,256]{2,1,0:T(8,128)(2,1)S(1)} all-to-all(f16[8,32,256]{2,1,0:T(8,128)(2,1)S(1)} %convert_element_type.17), channel_id=1, replica_groups=mesh['x'=4,'y'=4,'z'=8,'core'=2] {'z'}, dimensions={0} | all-to-all | bytes 262144 | tf_op jit(solution)/shard_map/all_to_all | solution.py:292
  34.4 0.0 copy-start.1
  34.4 1.5 %shard_map.81 = bf16[8,32,256]{2,1,0:T(8,128)(2,1)S(1)} custom-call(f32[8,32,256]{2,1,0:T(8,128)S(1)} %convert_element_type.18.dirs.zero_own, bf16[256,2048]{1,0:T(8,128)(2,1)S(1)} %get-tuple-element.39.near, bf16[256,2048]{1,0:T(8,128)(2,1)S(1)} %collective-permute-done.1.far, bf16[2048,256]{1,0:T(8,128)(2,1)S(1)} %copy-done, ...), custom_call_target="tpu_custom_call" | custom-call | tf_op jit(solution)/shard_map/pallas_call | solution.py:338
  36.0 10.3 %all_to_all.42.arrived = bf16[8,32,256]{2,1,0:T(8,128)(2,1)S(1)} all-to-all(bf16[8,32,256]{2,1,0:T(8,128)(2,1)S(1)} %shard_map.81), channel_id=1, replica_groups=mesh['x'=4,'y'=4,'z'=8,'core'=2] {'z'}, dimensions={0} | all-to-all | bytes 262144 | tf_op jit(solution)/shard_map/all_to_all | solution.py:292
  46.3 0.0 copy-done.1
  46.3 0.4 shard_map.82
  46.7 10.3 %all_to_all.43.dirs.one_own = bf16[8,32,256]{2,1,0:T(8,128)(2,1)S(1)} all-to-all(bf16[8,32,256]{2,1,0:T(8,128)(2,1)S(1)} %get-tuple-element.41), channel_id=1, replica_groups=mesh['x'=4,'y'=4,'z'=8,'core'=2] {'z'}, dimensions={0} | all-to-all | bytes 262144 | tf_op jit(solution)/shard_map/all_to_all | solution.py:292
  57.0 1.5 %shard_map.83 = bf16[8,32,256]{2,1,0:T(8,128)(2,1)S(1)} custom-call(bf16[8,32,256]{2,1,0:T(8,128)(2,1)S(1)} %all_to_all.43.dirs.one_own, bf16[256,2048]{1,0:T(8,128)(2,1)S(1)} %get-tuple-element.39.near, bf16[256,2048]{1,0:T(8,128)(2,1)S(1)} %collective-permute-done.1.far, bf16[2048,256]{1,0:T(8,128)(2,1)S(1)} %copy-done, ...), custom_call_target="tpu_custom_call" | custom-call | tf_op jit(solution)/shard_map/pallas_call | solution.py:338
  58.5 10.3 %all_to_all.44.arrived = bf16[8,32,256]{2,1,0:T(8,128)(2,1)S(1)} all-to-all(bf16[8,32,256]{2,1,0:T(8,128)(2,1)S(1)} %shard_map.83), channel_id=1, replica_groups=mesh['x'=4,'y'=4,'z'=8,'core'=2] {'z'}, dimensions={0} | all-to-all | bytes 262144 | tf_op jit(solution)/shard_map/all_to_all | solution.py:292
  68.8 0.4 shard_map.84
  69.3 10.3 %all_to_all.45.dirs.two_own = bf16[8,32,256]{2,1,0:T(8,128)(2,1)S(1)} all-to-all(bf16[8,32,256]{2,1,0:T(8,128)(2,1)S(1)} %get-tuple-element.45), channel_id=1, replica_groups=mesh['x'=4,'y'=4,'z'=8,'core'=2] {'z'}, dimensions={0} | all-to-all | bytes 262144 | tf_op jit(solution)/shard_map/all_to_all | solution.py:292
  79.6 7.4 %collective-permute-start.2 = (f16[8,32,256]{2,1,0:T(8,128)(2,1)S(1)}, f16[8,32,256]{2,1,0:T(8,128)(2,1)S(1)}, u32[]{:S(2)}, u32[]{:S(2)}) collective-permute-start(f16[8,32,256]{2,1,0:T(8,128)(2,1)S(1)} %all_to_all.41), channel_id=1, source_target_pairs={{0,1},{1,0},{2,3},{3,2},{4,5},{5,4},{6,7},{7,6},{8,9},{9,8},{10,11... | collective-permute-start | bytes 393224 | tf_op jit(solution)/shard_map/ppermute | solution.py:296
  87.0 0.0 collective-permute-start.3
  87.0 0.5 collective-permute-start.4
  87.5 1.2 shard_map.85
  88.7 0.0 collective-permute-done.2
  88.8 0.0 collective-permute-done.3.one_other
  88.8 0.0 collective-permute-done.4.two_other
  88.8 10.3 %all_to_all.46.arrived = f32[16,8,128]{2,1,0:T(8,128)S(1)} all-to-all(f32[16,8,128]{2,1,0:T(8,128)S(1)} %shard_map.85), channel_id=1, replica_groups=mesh['x'=4,'y'=4,'z'=8,'core'=2] {'z','core'}, dimensions={0} | all-to-all | bytes 131072 | tf_op jit(solution)/shard_map/all_to_all | solution.py:292
  99.1 1.1 shard_map.86
  100.2 22.5 %all_to_all.47.arrived = bf16[16,256,128]{2,1,0:T(8,128)(2,1)S(1)} all-to-all(bf16[16,256,128]{2,1,0:T(8,128)(2,1)S(1)} %get-tuple-element.57), channel_id=1, replica_groups=mesh['x'=4,'y'=4,'z'=8,'core'=2] {'x','y'}, dimensions={0} | all-to-all | bytes 2097152 | tf_op jit(solution)/shard_map/all_to_all | solution.py:292
  122.8 0.9 shard_map.87
  (10 shorter events, 0.1 us)
Async XLA Ops:
  0.6 5.9 %copy-start = (bf16[2048,256]{1,0:T(8,128)(2,1)S(1)}, bf16[2048,256]{1,0:T(8,128)(2,1)}, u32[]{:S(2)}) copy-start(bf16[2048,256]{1,0:T(8,128)(2,1)} %factors.7) | copy-start | bytes 3145732
  0.6 5.9 %copy-start.2 = (s32[1,1,48]{2,1,0:T(1,128)S(1)}, s32[1,1,48]{2,1,0:T(1,128)}, u32[]{:S(2)}) copy-start(s32[1,1,48]{2,1,0:T(1,128)} %param.8) | copy-start | bytes 580
  0.7 5.8 %copy-start.3 = (s32[1,1,48]{2,1,0:T(1,128)S(1)}, s32[1,1,48]{2,1,0:T(1,128)}, u32[]{:S(2)}) copy-start(s32[1,1,48]{2,1,0:T(1,128)} %param.9) | copy-start | bytes 580
  0.7 5.8 %collective-permute-start = (bf16[2048,256]{1,0:T(8,128)(2,1)}, bf16[2048,256]{1,0:T(8,128)(2,1)S(1)}, u32[]{:S(2)}, u32[]{:S(2)}) collective-permute-start(bf16[2048,256]{1,0:T(8,128)(2,1)} %factors.7), channel_id=1, source_target_pairs={{0,1},{1,0},{2,3},{3,2},{4,5},{5,4},{6,7},{7,6},{8,9},{9,8},{10,11... | collective-permute-start | bytes 3145736 | tf_op jit(solution)/shard_map/ppermute | solution.py:296
  6.1 2.7 %collective-permute-start.1 = (bf16[256,2048]{1,0:T(8,128)(2,1)S(1)}, bf16[256,2048]{1,0:T(8,128)(2,1)S(1)}, u32[]{:S(2)}, u32[]{:S(2)}) collective-permute-start(bf16[256,2048]{1,0:T(8,128)(2,1)S(1)} %get-tuple-element.33.away), channel_id=1, source_target_pairs={{0,1},{1,0},{2,3},{3,2},{4,5},{5,4},{6,7},{7,6},{8,9},{9,8},{10,11... | collective-permute-start | bytes 3145736 | tf_op jit(solution)/shard_map/ppermute | solution.py:296
  34.4 11.9 %copy-start.1 = (f32[256,256]{1,0:T(8,128)S(1)}, f32[256,256]{1,0:T(8,128)}, u32[]{:S(2)}) copy-start(f32[256,256]{1,0:T(8,128)} %gram.5) | copy-start | bytes 786436
  79.6 9.1 %collective-permute-start.2 = (f16[8,32,256]{2,1,0:T(8,128)(2,1)S(1)}, f16[8,32,256]{2,1,0:T(8,128)(2,1)S(1)}, u32[]{:S(2)}, u32[]{:S(2)}) collective-permute-start(f16[8,32,256]{2,1,0:T(8,128)(2,1)S(1)} %all_to_all.41), channel_id=1, source_target_pairs={{0,1},{1,0},{2,3},{3,2},{4,5},{5,4},{6,7},{7,6},{8,9},{9,8},{10,11... | collective-permute-start | bytes 393224 | tf_op jit(solution)/shard_map/ppermute | solution.py:296
  87.0 1.8 %collective-permute-start.3 = (bf16[8,32,256]{2,1,0:T(8,128)(2,1)S(1)}, bf16[8,32,256]{2,1,0:T(8,128)(2,1)S(1)}, u32[]{:S(2)}, u32[]{:S(2)}) collective-permute-start(bf16[8,32,256]{2,1,0:T(8,128)(2,1)S(1)} %all_to_all.43.dirs.one_own), channel_id=1, source_target_pairs={{0,1},{1,0},{2,3},{3,2},{4,5},{5,4},{6,7},{7,6},{8,9},{9,8},{10,11... | collective-permute-start | bytes 393224 | tf_op jit(solution)/shard_map/ppermute | solution.py:296
  87.0 1.8 %collective-permute-start.4 = (bf16[8,32,256]{2,1,0:T(8,128)(2,1)S(1)}, bf16[8,32,256]{2,1,0:T(8,128)(2,1)S(1)}, u32[]{:S(2)}, u32[]{:S(2)}) collective-permute-start(bf16[8,32,256]{2,1,0:T(8,128)(2,1)S(1)} %all_to_all.45.dirs.two_own), channel_id=1, source_target_pairs={{0,1},{1,0},{2,3},{3,2},{4,5},{5,4},{6,7},{7,6},{8,9},{9,8},{10,11... | collective-permute-start | bytes 393224 | tf_op jit(solution)/shard_map/ppermute | solution.py:296
